TPU v7x, 32 devices: a whole 2x2x4 slice. The times are simulated.
32 devices in a mesh: stream: 2 (over x), dp: 16 (over z, y, core).
Axes of the slice: x: 2, y: 2, z: 4, core: 2. Of those that a mesh axis runs over, the one named last changes fastest.
Arguments:
- tokens: bfloat16 [2, 16, 512, 768], P('stream', 'dp'), may hold values from -6 to 6
- boxes: int32 [2, 16, 2, 512], P('stream', 'dp'), may hold values from 0 to 1023
- rel_one: int32 [2, 16, 512, 512], P('stream', 'dp'), may hold values from 0 to 31
- rel_two: int32 [2, 16, 512, 512], P('stream', 'dp'), may hold values from 0 to 63
- vis_count: int32 [16], P('dp'), may hold values from 256 to 512, as said below
- spatial_tables: bfloat16 [2, 1024, 768], replicated, may hold values from -4.1875 to 4.1875
- proj_weights: bfloat16 [2, 2, 5, 768, 768], P('stream'), may hold values from -0.21875 to 0.21875
- out_weights: bfloat16 [2, 2, 768, 768], P('stream'), may hold values from -1.25 to 1.25
- ffn_in: bfloat16 [2, 2, 768, 3072], P('stream'), may hold values from -0.21875 to 0.21875
- ffn_out: bfloat16 [2, 2, 3072, 768], P('stream'), may hold values from -0.109375 to 0.109375
- norm_gains: float32 [2, 2, 2, 768], P('stream'), may hold values from 0.5 to 1.5
- norm_shifts: float32 [2, 2, 2, 768], P('stream'), may hold values from -1.8 to 1.8
- bias_tables: bfloat16 [2, 2, 12, 96], P('stream'), may hold values from -6 to 6
- cotangent: bfloat16 [2, 16, 512, 768], P('stream', 'dp'), may hold values from -6 to 6
Outputs:
- output: bfloat16 [2, 16, 512, 768], P('stream', 'dp')
- grad_tokens: float32 [2, 16, 512, 768], P('stream', 'dp')
- grad_spatial: float32 [2, 1024, 768], replicated
- grad_proj: float32 [2, 2, 5, 768, 768], P('stream', None, None, 'dp')
- grad_out: float32 [2, 2, 768, 768], P('stream', None, 'dp')
- grad_ffn_in: float32 [2, 2, 768, 3072], P('stream', None, 'dp')
- grad_ffn_out: float32 [2, 2, 3072, 768], P('stream', None, 'dp')
- grad_gains: float32 [2, 2, 2, 768], P('stream', None, None, 'dp')
- grad_shifts: float32 [2, 2, 2, 768], P('stream', None, None, 'dp')
- grad_tables: float32 [2, 2, 12, 96], P('stream')
Inputs may be any that keep to these rules, and one draw needn't show every extreme that they name: `vis_count`: each page has 256 or 512 visual tokens; the first page always has 512, the second 512 // 2.
All inputs are finite; a program needn't handle non-finite values.
Results may differ from a plain program's by a relative error of at most 0.035.
The roundings to bfloat16 on the way count: a program that leaves them out, or rounds other values in their place, can miss the bound.
Values sent between devices are 32-bit elements; how exact they have to be, the bound alone decides.
No kernel may reach another device: no remote copies, remote signals or barrier semaphores. Data moves between devices by JAX's collectives and lax.ppermute only.
A program may use at most 384 MiB of HBM per device.

v0:
```python
from functools import partial

import jax
import jax.numpy as jnp
from jax import lax
from jax.sharding import PartitionSpec as P

D = 768
HEADS = 12
HD = 64
NB1 = 32
NB2 = 64
LAYERS = 2


NEG_FILL = -1e30


def layer_norm(values, gain_vec, shift_vec):
    center = values - jnp.mean(values, axis=-1, keepdims=True)
    spread = jnp.mean(center * center, axis=-1, keepdims=True)
    return center * lax.rsqrt(spread + 1e-05) * gain_vec + shift_vec


def mixed_dot(formula, left, right):
    return jnp.einsum(formula, left, right, preferred_element_type=jnp.float32)


def bucket_lookup(rel_first, rel_second, bucket_table):
    first_hot = (rel_first[:, :, None] == jnp.arange(NB1, dtype=jnp.int32)[None, None, :]).astype(
        jnp.bfloat16
    )
    second_hot = (rel_second[:, :, None] == jnp.arange(NB2, dtype=jnp.int32)[None, None, :]).astype(
        jnp.bfloat16
    )
    bucket_bias = mixed_dot("qkb,hb->hqk", first_hot, bucket_table[:, :NB1]) + mixed_dot(
        "qkb,hb->hqk", second_hot, bucket_table[:, NB1:]
    )
    return (bucket_bias, first_hot, second_hot)


def page_scores(query_cat, key_cat, rel_first, rel_second, key_valid, bucket_table):
    bucket_bias, first_hot, second_hot = bucket_lookup(rel_first, rel_second, bucket_table)
    scores = mixed_dot("qhd,khd->hqk", query_cat, key_cat) * HD ** (-0.5) + bucket_bias
    scores = jnp.where(key_valid[None, None, :], scores, NEG_FILL)
    return (scores, first_hot, second_hot)


def page_forward(inputs, bucket_table):
    query_cat, key_cat, value_heads, rel_first, rel_second, key_valid = inputs
    scores, first_hot, second_hot = page_scores(
        query_cat, key_cat, rel_first, rel_second, key_valid, bucket_table
    )
    row_top = jnp.max(scores, axis=-1, keepdims=True)
    exp_scores = jnp.exp(scores - row_top)
    row_total = jnp.sum(exp_scores, axis=-1, keepdims=True)
    prob_low = (exp_scores / row_total).astype(jnp.bfloat16)
    context = mixed_dot("hqk,khd->qhd", prob_low, value_heads).astype(jnp.bfloat16)
    return (context, (row_top + jnp.log(row_total))[:, :, 0])


def page_backward(inputs, bucket_table):
    query_cat, key_cat, value_heads, rel_first, rel_second, key_valid, log_total, context_grad = (
        inputs
    )
    scores, first_hot, second_hot = page_scores(
        query_cat, key_cat, rel_first, rel_second, key_valid, bucket_table
    )
    prob_full = jnp.exp(scores - log_total[:, :, None])
    prob_low = prob_full.astype(jnp.bfloat16)
    prob_grad = mixed_dot("qhd,khd->hqk", context_grad, value_heads)
    score_grad = (
        prob_full * (prob_grad - jnp.sum(prob_full * prob_grad, axis=-1, keepdims=True))
    ).astype(jnp.bfloat16)
    score_scale = HD ** (-0.5)
    query_grad = (mixed_dot("hqk,khd->qhd", score_grad, key_cat) * score_scale).astype(jnp.bfloat16)
    key_grad = (mixed_dot("hqk,qhd->khd", score_grad, query_cat) * score_scale).astype(jnp.bfloat16)
    value_grad = mixed_dot("hqk,qhd->khd", prob_low, context_grad).astype(jnp.bfloat16)
    table_grad = jnp.concatenate(
        [
            mixed_dot("hqk,qkb->hb", score_grad, first_hot),
            mixed_dot("hqk,qkb->hb", score_grad, second_hot),
        ],
        axis=1,
    )
    return (query_grad, key_grad, value_grad, table_grad)


def head_layout(token_proj, spatial_proj, page_count):
    length = token_proj.shape[1] // page_count

    def to_heads(values):
        return values.reshape(page_count, length, HEADS, HD)

    query_cat = jnp.concatenate([to_heads(token_proj[0]), to_heads(spatial_proj[0])], axis=-1)
    key_cat = jnp.concatenate([to_heads(token_proj[1]), to_heads(spatial_proj[1])], axis=-1)
    return (query_cat, key_cat, to_heads(token_proj[2]))


def layer_forward(hidden_in, spatial, weights, layout):
    projections, out_proj, w_in, w_out, gains, shifts, bucket_table = weights
    rel_first, rel_second, key_valid, rowmask = layout
    page_count = rel_first.shape[0]
    row_count = hidden_in.shape[0]
    rounded = hidden_in.astype(jnp.bfloat16)
    token_proj = mixed_dot("rd,jde->jre", rounded, projections[:3]).astype(jnp.bfloat16)
    spatial_proj = mixed_dot("rd,jde->jre", spatial, projections[3:]).astype(jnp.bfloat16)
    query_cat, key_cat, value_heads = head_layout(token_proj, spatial_proj, page_count)
    context, log_total = lax.map(
        partial(page_forward, bucket_table=bucket_table),
        (query_cat, key_cat, value_heads, rel_first, rel_second, key_valid),
    )
    context = context.reshape(row_count, D)
    attn_out = jnp.dot(context, out_proj, preferred_element_type=jnp.float32) * rowmask
    mixed = lax.psum(attn_out, "stream")
    pre_attn = hidden_in + mixed
    normed = layer_norm(pre_attn, gains[0], shifts[0])
    normed_low = normed.astype(jnp.bfloat16)
    inner_pre = jnp.dot(normed_low, w_in, preferred_element_type=jnp.float32)
    activated = jax.nn.gelu(inner_pre, approximate=False).astype(jnp.bfloat16)
    branch = jnp.dot(activated, w_out, preferred_element_type=jnp.float32)
    result = layer_norm(normed + branch, gains[1], shifts[1])
    kept_state = (
        rounded,
        token_proj,
        spatial_proj,
        context,
        log_total,
        pre_attn,
        normed,
        normed_low,
        inner_pre,
        activated,
        branch,
    )
    return (result, kept_state)


def gelu_exact(values):
    return jax.nn.gelu(values, approximate=False)


def layer_backward(result_grad, spatial, weights, layout, kept_state):
    projections, out_proj, w_in, w_out, gains, shifts, bucket_table = weights
    rel_first, rel_second, key_valid, rowmask = layout
    (
        rounded,
        token_proj,
        spatial_proj,
        context,
        log_total,
        pre_attn,
        normed,
        normed_low,
        inner_pre,
        activated,
        branch,
    ) = kept_state
    page_count = rel_first.shape[0]
    row_count = rounded.shape[0]
    length = row_count // page_count
    unused, norm_pull = jax.vjp(layer_norm, normed + branch, gains[1], shifts[1])
    sum_grad, gain_two, shift_two = norm_pull(result_grad)
    branch_low = sum_grad.astype(jnp.bfloat16)
    w_out_grad = mixed_dot("rf,rd->fd", activated, branch_low)
    act_grad = mixed_dot("rd,fd->rf", branch_low, w_out)
    unused, gelu_pull = jax.vjp(gelu_exact, inner_pre)
    inner_low = gelu_pull(act_grad)[0].astype(jnp.bfloat16)
    w_in_grad = mixed_dot("rd,rf->df", normed_low, inner_low)
    normed_grad = sum_grad + mixed_dot("rf,df->rd", inner_low, w_in)
    unused, first_pull = jax.vjp(layer_norm, pre_attn, gains[0], shifts[0])
    pre_grad, gain_one, shift_one = first_pull(normed_grad)
    mixed_grad = lax.psum(pre_grad, "stream")
    attn_low = (mixed_grad * rowmask).astype(jnp.bfloat16)
    out_grad = mixed_dot("rd,re->de", context, attn_low)
    context_grad = mixed_dot("re,de->rd", attn_low, out_proj).astype(jnp.bfloat16)
    query_cat, key_cat, value_heads = head_layout(token_proj, spatial_proj, page_count)
    query_grad, key_grad, value_grad, table_grads = lax.map(
        partial(page_backward, bucket_table=bucket_table),
        (
            query_cat,
            key_cat,
            value_heads,
            rel_first,
            rel_second,
            key_valid,
            log_total,
            context_grad.reshape(page_count, length, HEADS, HD),
        ),
    )
    token_grads = jnp.stack(
        [
            query_grad[..., :HD].reshape(row_count, D),
            key_grad[..., :HD].reshape(row_count, D),
            value_grad.reshape(row_count, D),
        ]
    )
    spatial_grads = jnp.stack(
        [query_grad[..., HD:].reshape(row_count, D), key_grad[..., HD:].reshape(row_count, D)]
    )
    proj_grad = jnp.concatenate(
        [
            mixed_dot("rd,jre->jde", rounded, token_grads),
            mixed_dot("rd,jre->jde", spatial, spatial_grads),
        ],
        axis=0,
    )
    input_grad = pre_grad + mixed_dot("jre,jde->rd", token_grads, projections[:3])
    spatial_part = mixed_dot("jre,jde->rd", spatial_grads, projections[3:])
    weight_grads = (
        proj_grad,
        out_grad,
        w_in_grad,
        w_out_grad,
        jnp.stack([gain_one, gain_two]),
        jnp.stack([shift_one, shift_two]),
    )
    return (input_grad, spatial_part, weight_grads, jnp.sum(table_grads, axis=0))


def local(
    tokens,
    boxes,
    rel_one,
    rel_two,
    vis_count,
    spatial_tables,
    proj_weights,
    out_weights,
    ffn_in,
    ffn_out,
    norm_gains,
    norm_shifts,
    bias_tables,
    cotangent,
):
    page_count = tokens.shape[1]
    length = tokens.shape[2]
    row_count = page_count * length
    stream_at = lax.axis_index("stream")
    counts = jnp.where(stream_at == 0, length, vis_count)
    key_valid = jnp.arange(length, dtype=jnp.int32)[None, :] < counts[:, None]
    rowmask = key_valid.reshape(row_count, 1).astype(jnp.float32)
    layout = (rel_one[0], rel_two[0], key_valid, rowmask)
    bin_ids = jnp.arange(spatial_tables.shape[1], dtype=jnp.int32)
    hot_x = (boxes[0, :, 0].reshape(row_count, 1) == bin_ids[None, :]).astype(jnp.bfloat16)
    hot_y = (boxes[0, :, 1].reshape(row_count, 1) == bin_ids[None, :]).astype(jnp.bfloat16)
    spatial = (
        jnp.dot(hot_x, spatial_tables[0], preferred_element_type=jnp.float32)
        + jnp.dot(hot_y, spatial_tables[1], preferred_element_type=jnp.float32)
    ).astype(jnp.bfloat16)

    def layer_weights(layer_at):
        return (
            proj_weights[0, layer_at],
            out_weights[0, layer_at],
            ffn_in[0, layer_at],
            ffn_out[0, layer_at],
            norm_gains[0, layer_at],
            norm_shifts[0, layer_at],
            bias_tables[0, layer_at],
        )

    hidden = tokens[0].reshape(row_count, D).astype(jnp.float32)
    inputs_kept = []
    states_kept = []
    for layer_at in range(LAYERS):
        inputs_kept.append(hidden)
        hidden, kept_state = layer_forward(hidden, spatial, layer_weights(layer_at), layout)
        states_kept.append(kept_state)
    output = (hidden * rowmask).astype(jnp.bfloat16).reshape(1, page_count, length, D)
    result_grad = cotangent[0].reshape(row_count, D).astype(jnp.float32) * rowmask
    spatial_grad = jnp.zeros((row_count, D), jnp.float32)
    layer_grads = []
    table_grads = []
    for layer_at in reversed(range(LAYERS)):
        kept_state = states_kept[layer_at]
        result_grad, spatial_part, weight_grads, table_part = layer_backward(
            result_grad, spatial, layer_weights(layer_at), layout, kept_state
        )
        spatial_grad = spatial_grad + spatial_part
        layer_grads.insert(0, weight_grads)
        table_grads.insert(0, table_part)
    stacked = tuple((jnp.stack(members) for members in zip(*layer_grads)))
    stacked = (
        lax.psum_scatter(stacked[0], "dp", scatter_dimension=2, tiled=True),
        lax.psum_scatter(stacked[1], "dp", scatter_dimension=1, tiled=True),
        lax.psum_scatter(stacked[2], "dp", scatter_dimension=1, tiled=True),
        lax.psum_scatter(stacked[3], "dp", scatter_dimension=1, tiled=True),
        lax.psum_scatter(stacked[4], "dp", scatter_dimension=2, tiled=True),
        lax.psum_scatter(stacked[5], "dp", scatter_dimension=2, tiled=True),
    )
    spatial_low = spatial_grad.astype(jnp.bfloat16)
    table_x = mixed_dot("rb,rd->bd", hot_x, spatial_low)
    table_y = mixed_dot("rb,rd->bd", hot_y, spatial_low)
    own_slot = (jnp.arange(2, dtype=jnp.int32) == stream_at).astype(jnp.float32)
    bucket_all = own_slot[:, None, None, None] * jnp.stack(table_grads)[None]
    shared, buckets = lax.psum((jnp.stack([table_x, table_y]), bucket_all), ("stream", "dp"))
    bucket_own = lax.dynamic_slice_in_dim(buckets, stream_at, 1, 0)
    return (
        output,
        result_grad.reshape(1, page_count, length, D),
        shared,
        stacked[0][None],
        stacked[1][None],
        stacked[2][None],
        stacked[3][None],
        stacked[4][None],
        stacked[5][None],
        bucket_own,
    )


def solution(mesh):
    placed = (
        P("stream", "dp", None, None),
        P("stream", "dp", None, None),
        P("stream", "dp", None, None),
        P("stream", "dp", None, None),
        P("dp"),
        P(),
        P("stream", None, None, None, None),
        P("stream", None, None, None),
        P("stream", None, None, None),
        P("stream", None, None, None),
        P("stream", None, None, None),
        P("stream", None, None, None),
        P("stream", None, None, None),
        P("stream", "dp", None, None),
    )
    return jax.shard_map(
        local,
        mesh=mesh,
        in_specs=placed,
        out_specs=(
            P("stream", "dp", None, None),
            P("stream", "dp", None, None),
            P(),
            P("stream", None, None, "dp", None),
            P("stream", None, "dp", None),
            P("stream", None, "dp", None),
            P("stream", None, "dp", None),
            P("stream", None, None, "dp"),
            P("stream", None, None, "dp"),
            P("stream", None, None, None),
        ),
        check_vma=False,
    )
```

profile of v0, /device:TPU:0, one launch (start us, length us, event | category | flops | bytes accessed | tf_op | source)
XLA Modules:
  0.0 1694.2 jit_solution(16295816301324897043)
XLA Ops:
  15.2 14.7 fusion.3
  60.5 31.1 %fusion.242 = (f32[12,512]{1,0:T(8,128)S(1)}, f32[12,512,512]{1,2,0:T(8,128)}) fusion(f32[512,512,12]{0,2,1:T(8,128)} %fusion.3, f32[512,512,12]{0,2,1:T(8,128)} %fusion.11, bf16[1,512,12,64]{3,1,2,0:T(8,128)(2,1)} %copy.153, bf16[1,512,12,64]{3,1,2,0:T(8,128)(2,1)} %copy.152, bf16[1,512,12,64]{3,1,2,0:T(8,128)(2,1)} %copy.150, ...), kind=kOutput, calls=%fused_computation.338 | convolution fusion | flops 827320320 | bytes 40919552 | tf_op jit(solution)/shard_map/while/body/eval_jaxpr/qhd,khd->hqk/dot_general | solution.py:26
  127.0 14.4 fusion.2
  141.4 18.1 %all-reduce.8.cloned.1.call-done = f32[512,768]{1,0:T(8,128)} async-done(((f32[512,768]{1,0:T(8,128)}), f32[512,768]{1,0:T(8,128)}) %all-reduce.8.cloned.1.call-update) | async-done | bytes 1572880 | tf_op jit(solution)/shard_map/psum | solution.py:115
  162.5 20.5 %multiply_convert_fusion.3 = (bf16[512,3072]{1,0:T(8,128)(2,1)S(1)}, f32[512,3072]{1,0:T(8,128)}, f32[512,3072]{1,0:T(8,128)}) fusion(bf16[1,2,768,3072]{3,2,1,0:T(8,128)(2,1)} %param.22, f32[512,768]{1,0:T(8,128)S(1)} %get-tuple-element.219, f32[768]{0:T(1024)S(1)} %get-tuple-element.202, f32[768]{0:T(1024)S(1)} %get-tuple-element.265, ...), kind=kOutput, calls=%fused_computation.71 | convolution fusion | flops 2520121344 | bytes 22030336 | tf_op jit(solution)/shard_map/dot_general | solution.py:119
  201.7 30.1 %fusion.244 = (f32[12,512]{1,0:T(8,128)S(1)}, f32[12,512,512]{1,2,0:T(8,128)}) fusion(f32[512,512,12]{0,2,1:T(8,128)} %fusion.2, f32[512,512,12]{0,2,1:T(8,128)} %fusion.10, bf16[1,512,12,64]{3,1,2,0:T(8,128)(2,1)S(1)} %copy-done.12, bf16[1,512,12,64]{3,1,2,0:T(8,128)(2,1)} %copy.169, bf16[1,512,12,64]{3,1,2,0:T(8,128)(2,1)S(1)} %copy-done.13, ...), kind=kOutput, calls=%fused_computation.340 | convolution fusion | flops 827320320 | bytes 40919552 | tf_op jit(solution)/shard_map/while/body/eval_jaxpr/qhd,khd->hqk/dot_general | solution.py:26
  246.8 51.6 %all-reduce.10.cloned.1.call-done = f32[512,768]{1,0:T(8,128)} async-done(((f32[512,768]{1,0:T(8,128)}), f32[512,768]{1,0:T(8,128)}) %all-reduce.10.cloned.1.call-update) | async-done | bytes 1572880 | tf_op jit(solution)/shard_map/psum | solution.py:115
  301.3 20.1 %multiply_convert_fusion.2 = (bf16[512,3072]{1,0:T(8,128)(2,1)S(1)}, f32[512,3072]{1,0:T(8,128)}, f32[512,3072]{1,0:T(8,128)}) fusion(bf16[1,2,768,3072]{3,2,1,0:T(8,128)(2,1)} %param.22, f32[512,768]{1,0:T(8,128)S(1)} %get-tuple-element.215, f32[768]{0:T(1024)S(1)} %get-tuple-element.203, f32[768]{0:T(1024)S(1)} %get-tuple-element.264, ...), kind=kOutput, calls=%fused_computation.58 | convolution fusion | flops 2520121344 | bytes 22030336 | tf_op jit(solution)/shard_map/dot_general | solution.py:119
  344.8 51.5 %all-reduce.12.cloned.1.call-done = f32[512,768]{1,0:T(8,128)} async-done(((f32[512,768]{1,0:T(8,128)}), f32[512,768]{1,0:T(8,128)}) %all-reduce.12.cloned.1.call-update) | async-done | bytes 1572880 | tf_op jit(solution)/shard_map/psum | solution.py:173
  449.5 10.4 add_convert_fusion
  497.7 20.9 %all-reduce.14.cloned.1.call-done = f32[512,768]{1,0:T(8,128)} async-done(((f32[512,768]{1,0:T(8,128)}), f32[512,768]{1,0:T(8,128)}) %all-reduce.14.cloned.1.call-update) | async-done | bytes 1572880 | tf_op jit(solution)/shard_map/psum | solution.py:173
  576.4 10.1 maximum_bitcast_fusion
  586.5 16.6 pad_maximum_fusion
  603.1 35.0 %copy.204 = f32[2,5,768,768]{3,0,1,2:T(2,128)} copy(f32[2,5,768,768]{2,3,1,0:T(8,128)} %pad_maximum_fusion) | data formatting | bytes 47185920 | tf_op jit(solution)/shard_map/stack | solution.py:284
  693.0 10.1 fusion.177
  703.2 13.9 fusion.183
  720.2 10.6 fusion.174
  730.8 14.1 fusion.180
  745.0 41.0 %psum.47 = f32[2,2,12,96]{3,1,2,0:T(2,128)S(1)} all-reduce(f32[2,2,12,96]{3,1,2,0:T(2,128)S(1)} %broadcast_multiply_fusion), channel_id=1, replica_groups=mesh['stream'=2,'dp'=16] {'stream','dp'}, use_global_device_ids=true, to_apply=%region_41.42 | all-reduce | flops 4608 | bytes 36864 | tf_op jit(solution)/shard_map/psum | solution.py:298
  792.6 249.2 %all-reduce.18.cloned.1.call-done = f32[2,5,768,768]{3,0,1,2:T(2,128)} async-done(((f32[2,5,768,768]{3,0,1,2:T(2,128)}), f32[2,5,768,768]{3,0,1,2:T(2,128)}) %all-reduce.18.cloned.1.call-update) | async-done | bytes 23592976
  1044.9 159.0 %all-reduce.16.cloned.1.call-done = f32[2,1024,768]{2,1,0:T(8,128)} async-done(((f32[2,1024,768]{2,1,0:T(8,128)}), f32[2,1024,768]{2,1,0:T(8,128)}) %all-reduce.16.cloned.1.call-update) | async-done | bytes 6291472 | tf_op jit(solution)/shard_map/psum | solution.py:298
  1203.9 80.3 %reduce-scatter.10.cloned.1.call-done = f32[2,48,768]{2,1,0:T(8,128)} async-done(((f32[2,768,768]{2,1,0:T(8,128)}), f32[2,48,768]{2,1,0:T(8,128)}) %reduce-scatter.10.cloned.1.call-update) | async-done | bytes 294928 | tf_op jit(solution)/shard_map/reduce_scatter | solution.py:287
  1284.2 198.6 %reduce-scatter.12.cloned.1.call-done = f32[2,48,3072]{2,1,0:T(8,128)} async-done(((f32[2,768,3072]{2,1,0:T(8,128)}), f32[2,48,3072]{2,1,0:T(8,128)}) %reduce-scatter.12.cloned.1.call-update) | async-done | bytes 1179664 | tf_op jit(solution)/shard_map/reduce_scatter | solution.py:288
  1482.8 198.8 %reduce-scatter.14.cloned.1.call-done = f32[2,192,768]{2,1,0:T(8,128)} async-done(((f32[2,3072,768]{2,1,0:T(8,128)}), f32[2,192,768]{2,1,0:T(8,128)}) %reduce-scatter.14.cloned.1.call-update) | async-done | bytes 1179664 | tf_op jit(solution)/shard_map/reduce_scatter | solution.py:289
  (421 shorter events, 356.6 us)
Async XLA Ops:
  7.2 152.4 %all-reduce.8.cloned.1.call-start = ((), (), s32[]{:S(2)}) async-start(), calls=%async_computation.5 | async-start | bytes 3145728 | tf_op jit(solution)/shard_map/psum | solution.py:115
  12.8 85.4 %copy-start.25 = (bf16[1,512,768]{1,2,0:T(8,128)(2,1)}, bf16[1,512,768]{1,2,0:T(8,128)(2,1)S(1)}, u32[]{:S(2)}) copy-start(bf16[1,512,768]{1,2,0:T(8,128)(2,1)S(1)} %get-tuple-element.225) | copy-start | bytes 2359300
  13.3 113.8 %copy-start.6 = (s32[512,512]{0,1:T(8,128)}, s32[512,512]{0,1:T(8,128)S(1)}, u32[]{:S(2)}) copy-start(s32[512,512]{0,1:T(8,128)S(1)} %copy.157) | copy-start | bytes 3145732
  15.2 103.2 %copy-start.4 = (s32[512,512]{0,1:T(8,128)}, s32[512,512]{0,1:T(8,128)S(1)}, u32[]{:S(2)}) copy-start(s32[512,512]{0,1:T(8,128)S(1)} %copy.154) | copy-start | bytes 3145732
  105.2 193.2 %all-reduce.10.cloned.1.call-start = ((), (), s32[]{:S(2)}) async-start(), calls=%async_computation.6 | async-start | bytes 3145728 | tf_op jit(solution)/shard_map/psum | solution.py:115
  118.4 64.6 %copy-start.71 = (f32[768]{0:T(1024)}, f32[768]{0:T(1024)S(1)}, u32[]{:S(2)}) copy-start(f32[768]{0:T(1024)S(1)} %get-tuple-element.265) | copy-start | bytes 9220
  118.4 64.6 %copy-start.82 = (f32[768]{0:T(1024)}, f32[768]{0:T(1024)S(1)}, u32[]{:S(2)}) copy-start(f32[768]{0:T(1024)S(1)} %get-tuple-element.202) | copy-start | bytes 9220
  118.4 203.0 %copy-start.84 = (f32[768]{0:T(1024)}, f32[768]{0:T(1024)S(1)}, u32[]{:S(2)}) copy-start(f32[768]{0:T(1024)S(1)} %get-tuple-element.203) | copy-start | bytes 9220
  118.4 224.1 %copy-start.73 = (f32[768]{0:T(1024)}, f32[768]{0:T(1024)S(1)}, u32[]{:S(2)}) copy-start(f32[768]{0:T(1024)S(1)} %get-tuple-element.264) | copy-start | bytes 9220
  127.0 32.5 %copy-start.44 = (bf16[1,1,512,768]{3,2,1,0:T(8,128)(2,1)S(1)}, bf16[1,1,512,768]{3,2,1,0:T(8,128)(2,1)}, u32[]{:S(2)}) copy-start(bf16[1,1,512,768]{3,2,1,0:T(8,128)(2,1)} %param.14) | copy-start | bytes 2359300
  246.7 149.6 %all-reduce.12.cloned.1.call-start = ((), (), s32[]{:S(2)}) async-start(), calls=%async_computation.7 | async-start | bytes 3145728 | tf_op jit(solution)/shard_map/psum | solution.py:173
  300.9 41.7 %copy-start.18 = (f32[512,768]{1,0:T(8,128)}, f32[512,768]{1,0:T(8,128)S(1)}, u32[]{:S(2)}) copy-start(f32[512,768]{1,0:T(8,128)S(1)} %get-tuple-element.215) | copy-start | bytes 4718596
  300.9 41.7 %copy-start.65 = (f32[512]{0:T(512)}, f32[512]{0:T(512)S(1)}, u32[]{:S(2)}) copy-start(f32[512]{0:T(512)S(1)} %broadcast_multiply_fusion.2) | copy-start | bytes 6148
  301.2 41.3 %copy-start.80 = (f32[512]{0:T(512)}, f32[512]{0:T(512)S(1)}, u32[]{:S(2)}) copy-start(f32[512]{0:T(512)S(1)} %fusion.200) | copy-start | bytes 6148
  344.6 174.0 %all-reduce.14.cloned.1.call-start = ((), (), s32[]{:S(2)}) async-start(), calls=%async_computation.8 | async-start | bytes 3145728 | tf_op jit(solution)/shard_map/psum | solution.py:173
  467.0 250.2 %reduce-scatter.16.cloned.1.call-start = ((), (), s32[]{:S(2)}) async-start(), calls=%async_computation.13 | async-start | bytes 417792
  495.9 222.8 %reduce-scatter.18.cloned.1.call-start = ((), (), s32[]{:S(2)}) async-start(), calls=%async_computation.14 | async-start | bytes 417792
  497.6 544.1 %all-reduce.18.cloned.1.call-start = ((), (), s32[]{:S(2)}) async-start(), calls=%async_computation.15 | async-start | bytes 47185920
  638.1 565.8 %all-reduce.16.cloned.1.call-start = ((), (), s32[]{:S(2)}) async-start(), calls=%async_computation.9 | async-start | bytes 12582912 | tf_op jit(solution)/shard_map/psum | solution.py:298
  651.4 632.8 %reduce-scatter.10.cloned.1.call-start = ((), (), s32[]{:S(2)}) async-start(), calls=%async_computation.10 | async-start | bytes 5013504 | tf_op jit(solution)/shard_map/reduce_scatter | solution.py:287
  658.5 824.3 %reduce-scatter.12.cloned.1.call-start = ((), (), s32[]{:S(2)}) async-start(), calls=%async_computation.11 | async-start | bytes 20054016 | tf_op jit(solution)/shard_map/reduce_scatter | solution.py:288
  674.9 1006.7 %reduce-scatter.14.cloned.1.call-start = ((), (), s32[]{:S(2)}) async-start(), calls=%async_computation.12 | async-start | bytes 20054016 | tf_op jit(solution)/shard_map/reduce_scatter | solution.py:289
  730.7 55.9 %copy-start.47 = (bf16[1,512,768]{2,1,0:T(8,128)(2,1)S(1)}, bf16[1,512,768]{2,1,0:T(8,128)(2,1)}, u32[]{:S(2)}) copy-start(bf16[1,512,768]{2,1,0:T(8,128)(2,1)} %copy.194) | copy-start | bytes 2359300
  730.8 55.9 %copy-start.49 = (bf16[1,512,768]{2,1,0:T(8,128)(2,1)S(1)}, bf16[1,512,768]{2,1,0:T(8,128)(2,1)}, u32[]{:S(2)}) copy-start(bf16[1,512,768]{2,1,0:T(8,128)(2,1)} %copy.193) | copy-start | bytes 2359300
  (104 other events, 723.5 us)
Sparse Core Ops, SparseCore 0:
  105.3 54.1 all-reduce.7
  246.8 51.4 all-reduce.9
  344.7 51.4 all-reduce.11
  467.1 51.4 all-reduce.13
  522.0 55.6 reduce-scatter.15
  581.4 54.5 reduce-scatter.17
  639.8 401.9 all-reduce.17
  1048.0 155.8 all-reduce.15
  1208.8 75.2 reduce-scatter.9
  1288.7 194.0 reduce-scatter.11
  1487.4 194.0 reduce-scatter.13
where the time goes:
time: 1700 us; the launch traced here: 1690 us
  waiting for transfers between devices  1030 us (61%)
  matrix products  370 us (22%)
  local copies, waits for them, and re-layouts  140 us (8%)
  other arithmetic  97 us (6%)
  blocking collectives  41 us (2%)
  between operations  17 us (1%)
    dot_general x46, matrix products, mixed_dot(): return jnp.einsum(formula, left, right, preferred_element_type=jnp.float32)  318 us
    unnamed x14, waiting for transfers between devices  249 us
    reduce_scatter x1, waiting for transfers between devices, local(): lax.psum_scatter(stacked[3], 'dp', scatter_dimension=1, tiled=True)  199 us
    reduce_scatter x1, waiting for transfers between devices, local(): lax.psum_scatter(stacked[2], 'dp', scatter_dimension=1, tiled=True)  199 us
    psum x1, waiting for transfers between devices, local(): lax.psum((jnp.stack([table_x, table_y]), bucket_all), ('stream', 'dp'))  159 us
    reduce_scatter x1, waiting for transfers between devices, local(): lax.psum_scatter(stacked[1], 'dp', scatter_dimension=1, tiled=True)  80.3 us
    psum x2, waiting for transfers between devices, layer_backward(): mixed_grad = lax.psum(pre_grad, 'stream')  72.4 us
    psum x2, waiting for transfers between devices, layer_forward(): mixed = lax.psum(attn_out, 'stream')  69.7 us
  transfers between devices with their start and end apart: 11, of which 9 were waited for; matrix products, arithmetic and copies ran while one was open for 17% of the time, Pallas kernels for 0%

commit v1 on v0

v1 whole, which is shorter than its diff:
```python
from functools import partial

import jax
import jax.numpy as jnp
from jax import lax
from jax.experimental import pallas as pl
from jax.experimental.pallas import tpu as pltpu
from jax.sharding import PartitionSpec as P

D = 768
HEADS = 12
HD = 64
NB1 = 32
NB2 = 64
LAYERS = 2
LANES = 128
NEG_FILL = -1e30
EPS = 1e-05
SCALE = HD ** (-0.5)
SQRT_HALF = 0.5**0.5
DENSITY = 0.3989422804014327
SWAP = [(0, 1), (1, 0)]
VMEM_LIMIT = 48 << 20
COST = pl.CostEstimate(flops=10**13, bytes_accessed=10**9, transcendentals=0)


def dot(left, right, left_dim=1, right_dim=0):
    return lax.dot_general(
        left, right, (((left_dim,), (right_dim,)), ((), ())), preferred_element_type=jnp.float32
    )


def low(values):
    return values.astype(jnp.bfloat16)


def gate(values, *deps):
    return lax.optimization_barrier((values,) + deps)[0]


class Order:
    def __init__(self):
        self.last = ()

    def call(self, kernel, shapes, operands, in_specs, out_specs, grid, name, scratch=(), scalars=()):
        after = tuple(self.last)
        taken = len(scalars) + len(operands)

        def body(*refs):
            kernel(*refs[:taken], *refs[taken + len(after) :])

        single = not isinstance(shapes, list)
        results = pl.pallas_call(
            body,
            grid_spec=pltpu.PrefetchScalarGridSpec(
                num_scalar_prefetch=len(scalars),
                grid=grid,
                in_specs=list(in_specs) + [pl.BlockSpec(memory_space=pl.ANY)] * len(after),
                out_specs=out_specs,
                scratch_shapes=list(scratch),
            ),
            out_shape=shapes,
            compiler_params=pltpu.CompilerParams(vmem_limit_bytes=VMEM_LIMIT),
            cost_estimate=COST,
            name=name,
        )(*scalars, *operands, *after)
        self.last = (results if single else results[0],)
        return results


def whole_spec(shape):
    return pl.BlockSpec(shape, lambda *ids: (0,) * len(shape))


def bias_kernel(one_ref, two_ref, table_ref, bias_ref):
    rows, length = one_ref.shape

    def group(step, carry):
        span = pl.ds(pl.multiple_of(step * 8, 8), 8)
        for col in range(0, length, LANES):
            cols = slice(col, col + LANES)
            first = one_ref[span, cols]
            second = two_ref[span, cols]
            for head in range(HEADS):
                first_row = jnp.broadcast_to(table_ref[0, head : head + 1, :], (8, LANES))
                second_row = jnp.broadcast_to(table_ref[1, head : head + 1, :], (8, LANES))
                bias_ref[head, span, cols] = jnp.take_along_axis(
                    first_row, first, axis=1
                ) + jnp.take_along_axis(second_row, second, axis=1)
        return carry

    lax.fori_loop(0, rows // 8, group, 0)


def score_bias(rel_one, rel_two, table, at, rows):
    length = rel_one.shape[1]
    step = 64
    first = at * rows // step
    rel = pl.BlockSpec((step, length), lambda i: (first + i, 0))
    return pl.pallas_call(
        bias_kernel,
        grid=(rows // step,),
        in_specs=[rel, rel, whole_spec(table.shape)],
        out_specs=pl.BlockSpec((HEADS, step, length), lambda i: (0, i, 0)),
        out_shape=jax.ShapeDtypeStruct((HEADS, rows, length), jnp.float32),
        cost_estimate=COST,
        name="score_bias",
    )(rel_one, rel_two, table)


def attend_kernel(
    at,
    tile,
    count_ref,
    query_ref,
    key_ref,
    value_ref,
    squery_ref,
    skey_ref,
    bias_ref,
    out_w_ref,
    context_ref,
    attn_ref,
    prob_ref,
    score_ref,
    low_ref,
):
    pair = pl.program_id(0)
    rows = query_ref.shape[0]
    length = value_ref.shape[0]
    lanes = lax.broadcasted_iota(jnp.int32, (1, 2 * HD), 1)
    valid = lax.broadcasted_iota(jnp.int32, (1, length), 1) < count_ref[0]
    keys = jnp.concatenate([key_ref[...], skey_ref[...]], axis=0)
    for half in range(2):
        keep = low(((lanes >= HD) == (half == 1)).astype(jnp.float32) * SCALE)
        queries = jnp.concatenate([query_ref[...] * keep, squery_ref[...] * keep], axis=1)
        score_ref[half] = dot(queries, keys)

    def group(step, carry):
        span = pl.ds(pl.multiple_of(step * tile, tile), tile)
        for half in range(2):
            scores = score_ref[half, span, :] + bias_ref[half, span, :]
            scores = jnp.where(valid, scores, NEG_FILL)
            weights = jnp.exp(scores - jnp.max(scores, axis=1, keepdims=True))
            prob = weights * (1.0 / jnp.sum(weights, axis=1, keepdims=True))
            prob_ref[half, span, :] = prob
            low_ref[half, span, :] = low(prob)
        return carry

    lax.fori_loop(0, rows // tile, group, 0)
    first = dot(low_ref[0], value_ref[...])
    second = dot(low_ref[1], value_ref[...])
    cols = pl.ds(pl.multiple_of(pair * 2 * HD, 2 * HD), 2 * HD)
    context_ref[:, cols] = low(jnp.where(lanes >= HD, second, first))

    @pl.when(pair == pl.num_programs(0) - 1)
    def finish():
        index = lax.broadcasted_iota(jnp.int32, (rows, 1), 0) + at * rows
        mask = (index < count_ref[0]).astype(jnp.float32)
        attn_ref[...] = dot(context_ref[...], out_w_ref[...]) * mask


def attend(count, projected, bias, out_w, layer_at, at, rows):
    query, key_t, value, squery, skey_t = projected
    length = value.shape[0]
    row_pair = pl.BlockSpec((rows, 2 * HD), lambda p, c: (at, p))
    key_pair = pl.BlockSpec((2 * HD, length), lambda p, c: (p, 0))
    value_pair = pl.BlockSpec((length, 2 * HD), lambda p, c: (0, p))
    score_pair = pl.BlockSpec((2, rows, length), lambda p, c: (p, 0, 0))
    return pl.pallas_call(
        partial(attend_kernel, at, 128),
        grid_spec=pltpu.PrefetchScalarGridSpec(
            num_scalar_prefetch=1,
            grid=(HEADS // 2,),
            in_specs=[
                row_pair,
                key_pair,
                value_pair,
                row_pair,
                key_pair,
                score_pair,
                pl.BlockSpec((None, None, D, D), lambda p, c: (0, layer_at, 0, 0)),
            ],
            out_specs=[whole_spec((rows, D)), whole_spec((rows, D)), score_pair],
            scratch_shapes=[
                pltpu.VMEM((2, rows, length), jnp.float32),
                pltpu.VMEM((2, rows, length), jnp.bfloat16),
            ],
        ),
        out_shape=[
            jax.ShapeDtypeStruct((rows, D), jnp.bfloat16),
            jax.ShapeDtypeStruct((rows, D), jnp.float32),
            jax.ShapeDtypeStruct((HEADS, rows, length), jnp.float32),
        ],
        compiler_params=pltpu.CompilerParams(vmem_limit_bytes=VMEM_LIMIT),
        cost_estimate=COST,
        name="attend",
    )(count, query, key_t, value, squery, skey_t, bias, out_w)


def attend_back_kernel(
    tile,
    *refs,
):
    (query_ref, key_ref, value_ref, squery_ref, skey_ref, grad_ref), refs = refs[:6], refs[6:]
    attn_ref, refs = refs[0], refs[1:]
    prob_refs, (out_ref, score_out_ref, dprob_ref, prob_low_ref) = refs[:-4], refs[-4:]
    rows = prob_refs[0].shape[1]
    lanes = lax.broadcasted_iota(jnp.int32, (1, 2 * HD), 1)
    queries = jnp.concatenate([query_ref[...], squery_ref[...]], axis=1)
    keys = jnp.concatenate([key_ref[...], skey_ref[...]], axis=1)
    grads = grad_ref[...]
    results = []
    for half in range(2):
        own = low(((lanes >= HD) == (half == 1)).astype(jnp.float32))
        dprob_ref[...] = dot(grads * own, value_ref[...])
        for chunk, prob_ref in enumerate(prob_refs):

            def group(step, carry, chunk=chunk, prob_ref=prob_ref):
                span = pl.ds(pl.multiple_of(step * tile, tile), tile)
                there = pl.ds(pl.multiple_of(chunk * rows + step * tile, tile), tile)
                prob = prob_ref[half, span, :]
                dprob = dprob_ref[there, :]
                total = jnp.sum(prob * dprob, axis=1, keepdims=True)
                score_out_ref[half, there, :] = low(prob * (dprob - total))
                prob_low_ref[there, :] = low(prob)
                return carry

            lax.fori_loop(0, rows // tile, group, 0)
        scores = score_out_ref[half]
        results.append(
            (
                dot(scores, keys) * SCALE,
                dot(scores, queries, 0, 0) * SCALE,
                dot(prob_low_ref[...], grads, 0, 0),
            )
        )
    (dq0, dk0, dv0), (dq1, dk1, dv1) = results
    upper = lanes >= HD
    wide = 2 * HD
    out_ref[0] = low(jnp.where(upper, dq1[:, :wide], dq0[:, :wide]))
    out_ref[1] = low(jnp.where(upper, dk1[:, :wide], dk0[:, :wide]))
    out_ref[2] = low(jnp.where(upper, dv1, dv0))
    out_ref[3] = low(jnp.where(upper, dq1[:, wide:], dq0[:, wide:]))
    out_ref[4] = low(jnp.where(upper, dk1[:, wide:], dk0[:, wide:]))
    out_ref[5] = attn_ref[...]


def attend_back(clock, projected, probs, context_grad, attn_low):
    query, key, value_t, squery, skey = projected
    length = query.shape[0]
    pair = pl.BlockSpec((length, 2 * HD), lambda p: (0, p))
    value_pair = pl.BlockSpec((2 * HD, length), lambda p: (p, 0))
    prob_specs = [pl.BlockSpec((2,) + prob.shape[1:], lambda p: (p, 0, 0)) for prob in probs]
    return clock.call(
        partial(attend_back_kernel, 128),
        [
            jax.ShapeDtypeStruct((6, length, D), jnp.bfloat16),
            jax.ShapeDtypeStruct((HEADS, length, length), jnp.bfloat16),
        ],
        [query, key, value_t, squery, skey, context_grad, attn_low, *probs],
        [pair, pair, value_pair, pair, pair, pair, pair] + prob_specs,
        [
            pl.BlockSpec((6, length, 2 * HD), lambda p: (0, 0, p)),
            pl.BlockSpec((2, length, length), lambda p: (p, 0, 0)),
        ],
        (HEADS // 2,),
        "attend_back",
        [
            pltpu.VMEM((length, length), jnp.float32),
            pltpu.VMEM((length, length), jnp.bfloat16),
        ],
    )


def bucket_kernel(one_ref, two_ref, grad_ref, out_ref, sum_ref):
    step = pl.program_id(0)
    group, length = one_ref.shape
    buckets = NB1 + NB2

    @pl.when(step == 0)
    def clear():
        sum_ref[...] = jnp.zeros_like(sum_ref)

    first_ids = lax.broadcasted_iota(jnp.int32, (NB1, 1), 0)
    second_ids = lax.broadcasted_iota(jnp.int32, (NB2, 1), 0)
    hot = []
    for row in range(group):
        hot.append(low((one_ref[row : row + 1, :] == first_ids).astype(jnp.float32)))
        hot.append(low((two_ref[row : row + 1, :] == second_ids).astype(jnp.float32)))
    hot = jnp.concatenate(hot, axis=0)
    grads = grad_ref[...].reshape(HEADS * group, length)
    sum_ref[...] += dot(hot, grads, 1, 1)

    @pl.when(step == pl.num_programs(0) - 1)
    def finish():
        member = lax.broadcasted_iota(jnp.int32, (1, HEADS * group), 1) % group
        total = jnp.zeros((buckets, HEADS * group), jnp.float32)
        for row in range(group):
            block = sum_ref[row * buckets : (row + 1) * buckets, :]
            total = total + jnp.where(member == row, block, 0.0)
        out_ref[...] = total


def bucket_sums(clock, rel_one, rel_two, score_grad):
    length = rel_one.shape[0]
    group = 16
    buckets = NB1 + NB2
    rel = pl.BlockSpec((group, length), lambda i: (i, 0))
    sums = clock.call(
        bucket_kernel,
        jax.ShapeDtypeStruct((buckets, HEADS * group), jnp.float32),
        [rel_one, rel_two, score_grad],
        [rel, rel, pl.BlockSpec((HEADS, group, length), lambda i: (0, i, 0))],
        whole_spec((buckets, HEADS * group)),
        (length // group,),
        "bucket_sums",
        [pltpu.VMEM((group * buckets, HEADS * group), jnp.float32)],
    )
    return jnp.sum(sums.reshape(buckets, HEADS, group), axis=2).T


def dp_strides(size):
    return tuple(1 << place for place in range(size.bit_length() - 1))


def orders(size):
    rest = dp_strides(size)[1:]
    if len(rest) < 2:
        return rest, rest
    return rest, (rest[1], rest[0]) + rest[2:]


def place(relative, order):
    spot = relative * 0
    for stride in order:
        spot = spot * 2 + (relative // (stride // 2)) % 2
    return spot


def rows_kernel(parts, order, ends, me_ref, *refs):
    left_refs, (right_ref, send_ref, keep_ref, sum_ref) = refs[:-4], refs[-4:]
    width = sum_ref.shape[0] // parts
    step = pl.program_id(0)
    right = right_ref[...].reshape(right_ref.shape[-2:])
    for index, left_ref in enumerate(left_refs):
        start = ends[index - 1] if index else 0

        @pl.when((step >= start) & (step < ends[index]))
        def product(left_ref=left_ref):
            sum_ref[...] = dot(left_ref[...], right, 0, 0)

    me = me_ref[0]
    core = me % 2
    for block in range(parts // 2):
        spot = place(jnp.bitwise_xor(block, me // 2), order)
        own = pl.ds(pl.multiple_of((2 * block + core) * width, 8), width)
        other = pl.ds(pl.multiple_of((2 * block + 1 - core) * width, 8), width)
        shape = (1,) * (len(keep_ref.shape) - 2) + (width, sum_ref.shape[1])
        keep_ref[pl.ds(spot, 1)] = sum_ref[own, :].reshape(shape)
        send_ref[pl.ds(spot, 1)] = sum_ref[other, :].reshape(shape)


def pair_kernel(me_ref, left_ref, right_ref, send_ref, keep_ref, sum_ref):
    width = sum_ref.shape[0] // 2
    sum_ref[...] = dot(left_ref[...], right_ref[...], 0, 0)
    core = me_ref[0] % 2
    own = pl.ds(pl.multiple_of(core * width, 8), width)
    other = pl.ds(pl.multiple_of((1 - core) * width, 8), width)
    keep_ref[0] = sum_ref[own, :]
    send_ref[0] = sum_ref[other, :]


def natural_blocks(values, me, size, order):
    blocks = values.reshape((size // 2, 2) + (values.shape[0] // size,) + values.shape[1:])
    spots = jnp.arange(size // 2, dtype=jnp.int32)
    relative = spots * 0
    for rank, stride in enumerate(reversed(order)):
        relative = relative + (spots >> rank) % 2 * (stride // 2)
    blocks = jnp.take(blocks, jnp.bitwise_xor(relative, me // 2), axis=0)
    core = me % 2
    own = lax.dynamic_index_in_dim(blocks, core, 1, keepdims=False)
    other = lax.dynamic_index_in_dim(blocks, 1 - core, 1, keepdims=False)
    return other, own


def wide_grad(clock, left, right, me, size, order):
    length, rows = left.shape
    wide = right.shape[1]
    width = rows // size
    if width % 8:
        return natural_blocks(dot(left, right, 0, 0), me[0], size, order)
    step = D
    half = size // 2
    block = pl.BlockSpec((half, width, step), lambda j, m: (0, 0, j))
    shape = jax.ShapeDtypeStruct((half, width, wide), jnp.float32)
    return clock.call(
        partial(rows_kernel, size, order, (wide // step,)),
        [shape, shape],
        [left, right],
        [whole_spec(left.shape), pl.BlockSpec((length, step), lambda j, m: (0, j))],
        [block, block],
        (wide // step,),
        "wide_grad",
        [pltpu.VMEM((rows, step), jnp.float32)],
        [me],
    )


def proj_grad(clock, lefts, right, first, me, size, order):
    length, rows = lefts[0][0].shape
    ends = []
    for left, count in lefts:
        ends.append(count + (ends[-1] if ends else 0))
    width = rows // size
    if width % 8:
        used = [left for left, count in lefts for at in range(count)]
        parts = jnp.stack([dot(left, right[first + j], 0, 0) for j, left in enumerate(used)])
        blocks = natural_blocks(jnp.swapaxes(parts, 0, 1), me[0], size, order)
        return [jnp.swapaxes(part, 1, 2) for part in blocks]
    half = size // 2
    block = pl.BlockSpec((half, 1, width, D), lambda j, m: (0, j, 0, 0))
    shape = jax.ShapeDtypeStruct((half, ends[-1], width, D), jnp.float32)
    return clock.call(
        partial(rows_kernel, size, order, tuple(ends)),
        [shape, shape],
        [left for left, count in lefts] + [right],
        [whole_spec((length, rows)) for left in lefts]
        + [pl.BlockSpec((1, length, D), lambda j, m: (first + j, 0, 0))],
        [block, block],
        (ends[-1],),
        "proj_grad",
        [pltpu.VMEM((rows, D), jnp.float32)],
        [me],
    )


def tall_grad(clock, left, right, me, size, order):
    length, rows = left.shape
    wide = right.shape[1]
    width = rows // size
    if width % 8 or 2 * width % LANES:
        return natural_blocks(dot(left, right, 0, 0), me[0], size, order)
    half = size // 2
    block = pl.BlockSpec(
        (1, width, wide), lambda i, m: (place(jnp.bitwise_xor(i, m[0] // 2), order), 0, 0)
    )
    shape = jax.ShapeDtypeStruct((half, width, wide), jnp.float32)
    return clock.call(
        pair_kernel,
        [shape, shape],
        [left, right],
        [pl.BlockSpec((length, 2 * width), lambda i, m: (0, i)), whole_spec(right.shape)],
        [block, block],
        (half,),
        "tall_grad",
        [pltpu.VMEM((2 * width, wide), jnp.float32)],
        [me],
    )


def swap_dp(values, stride, size):
    return lax.ppermute(values, "dp", [(index, index ^ stride) for index in range(size)])


def add_kernel(*refs):
    total = refs[0][...]
    for ref in refs[1:-1]:
        total = total + ref[...]
    refs[-1][...] = total


def add_blocks(clock, parts, first, count):
    shape = parts[0].shape[1:]
    tail = (0,) * len(shape)
    return clock.call(
        add_kernel,
        jax.ShapeDtypeStruct((count,) + shape, jnp.float32),
        parts,
        [pl.BlockSpec((1,) + shape, lambda i: (first + i,) + tail)] * len(parts),
        pl.BlockSpec((1,) + shape, lambda i: (i,) + tail),
        (count,),
        "add_blocks",
    )


class Reduction:
    def __init__(self, clock, blocks, order, size):
        self.clock = clock
        self.size = size
        self.order = list(order)
        send, keep = blocks
        self.parts = [keep, swap_dp(send, 1, size)]
        self.left = keep.shape[0]
        self.total = None

    def advance(self):
        if not self.order:
            self.total = add_blocks(self.clock, self.parts, 0, 1)[0]
            return
        self.left //= 2
        sent = add_blocks(self.clock, self.parts, self.left, self.left)
        self.parts.append(swap_dp(sent, self.order.pop(0), self.size))

    def finish(self):
        while self.total is None:
            self.advance()
        return self.total


def bins_kernel(half, at_ref, boxes_ref, grad_ref, send_ref, keep_ref):
    step = pl.program_id(0)
    width = keep_ref.shape[1]
    for ref, spot in ((keep_ref, step), (send_ref, step + half)):
        block = jnp.bitwise_xor(spot, at_ref[0])
        table = block // half
        ids = lax.broadcasted_iota(jnp.int32, (width, 1), 0) + (block - table * half) * width
        hot = low((boxes_ref[pl.ds(table, 1), :] == ids).astype(jnp.float32))
        ref[0] = dot(hot, grad_ref[...])


def table_grad(clock, boxes, grad, bins, at, parts):
    half = parts // 2
    width = 2 * bins // parts
    block = pl.BlockSpec((1, width, D), lambda i, m: (i, 0, 0))
    shape = jax.ShapeDtypeStruct((half, width, D), jnp.float32)
    return clock.call(
        partial(bins_kernel, half),
        [shape, shape],
        [boxes, grad],
        [whole_spec(boxes.shape), whole_spec(grad.shape)],
        [block, block],
        (half,),
        "table_grad",
        (),
        [at],
    )


def join_kernel(starts, *refs):
    step = pl.program_id(0)
    for part, ref in enumerate(refs[:-1]):

        @pl.when((step >= starts[part]) & (step < starts[part + 1]))
        def copy(ref=ref):
            refs[-1][...] = ref[...]


def join(clock, parts, at=None):
    starts = [0]
    for part in parts:
        starts.append(starts[-1] + part.shape[0])
    shape = parts[0].shape[1:]
    mask = starts[-1] - 1

    def spec(index):
        start, count = starts[index], parts[index].shape[0]
        return pl.BlockSpec((1,) + shape, lambda i, *m: (jnp.clip(i - start, 0, count - 1), 0, 0))

    def kernel(*refs):
        join_kernel(starts, *(refs if at is None else refs[1:]))

    def spot(i, *m):
        return (i if at is None else jnp.bitwise_xor(i, m[0][0] & mask), 0, 0)

    return clock.call(
        kernel,
        jax.ShapeDtypeStruct((starts[-1],) + shape, jnp.float32),
        parts,
        [spec(index) for index in range(len(parts))],
        pl.BlockSpec((1,) + shape, spot),
        (starts[-1],),
        "join",
        (),
        () if at is None else [at],
    )


def halves_kernel(core_ref, own_ref, other_ref, out_ref):
    here = pl.program_id(0) == core_ref[0]

    @pl.when(here)
    def own():
        out_ref[0] = own_ref[...]

    @pl.when(jnp.logical_not(here))
    def other():
        out_ref[0] = other_ref[...]


def halves(clock, own, other, core):
    step = 4
    count = own.shape[0] // step
    block = (step,) + own.shape[1:]

    def spec(mine):
        def spot(half, i, c):
            here = (half == c[0]) if mine else (half != c[0])
            return (jnp.where(here, i, jnp.where(half == 0, 0, count - 1)), 0, 0)

        return pl.BlockSpec(block, spot)

    return clock.call(
        halves_kernel,
        jax.ShapeDtypeStruct((2,) + own.shape, jnp.float32),
        [own, other],
        [spec(True), spec(False)],
        pl.BlockSpec((1,) + block, lambda half, i, c: (half, i, 0, 0)),
        (2, count),
        "halves",
        (),
        [core],
    )


class EverySum:
    def __init__(self, clock, boxes, grad, bins, size):
        self.clock = clock
        self.size = size
        strides = dp_strides(size)
        self.steps = [strides[0], None] + list(strides[1:])
        dp_at = lax.axis_index("dp")
        at = dp_at * 0
        for stride in self.steps:
            bit = lax.axis_index("stream") if stride is None else dp_at // stride % 2
            at = at * 2 + bit
        self.at = at.astype(jnp.int32).reshape(1)
        send, keep = table_grad(clock, boxes, grad, bins, self.at, 2 * size)
        self.parts = [keep, self.swap(send, self.steps[0])]
        self.left = size
        self.down = self.steps[1:]
        self.up = list(reversed(self.steps))

    def swap(self, values, stride):
        if stride is None:
            return lax.ppermute(values, "stream", SWAP)
        return swap_dp(values, stride, self.size)

    def advance(self):
        if self.down:
            self.left //= 2
            sent = add_blocks(self.clock, self.parts, self.left, self.left)
            self.parts.append(self.swap(sent, self.down.pop(0)))
        elif self.up:
            if self.left:
                self.parts = [add_blocks(self.clock, self.parts, 0, 1)]
                self.left = 0
                sent = self.parts[0]
            else:
                at = self.at if len(self.up) == 1 else None
                sent = join(self.clock, self.parts, at)
                self.parts = [sent]
            self.parts.append(self.swap(sent, self.up.pop(0)))

    def finish(self):
        while self.down or self.up:
            self.advance()
        return halves(self.clock, *self.parts, self.at // self.size)


class SmallSum:
    def __init__(self, clock, values, size):
        self.clock = clock
        self.size = size
        self.parts = [values[None]]
        self.strides = list(dp_strides(size))

    def advance(self):
        if len(self.parts) > 1:
            self.parts = [add_blocks(self.clock, self.parts, 0, 1)]
        if self.strides:
            self.parts.append(swap_dp(self.parts[0], self.strides.pop(0), self.size))

    def finish(self):
        while len(self.parts) > 1:
            self.advance()
        return self.parts[0][0]


def norm_back(grad, normal, root, gain):
    scaled = grad * gain
    inner = jnp.mean(scaled * normal, axis=-1, keepdims=True)
    outer = jnp.mean(scaled, axis=-1, keepdims=True)
    return (scaled - outer - normal * inner) * root


def norm_sums(grad, normal):
    return jnp.concatenate(
        [
            jnp.sum(grad * normal, axis=0, keepdims=True),
            jnp.sum(grad, axis=0, keepdims=True),
            jnp.zeros((6, grad.shape[1]), jnp.float32),
        ],
        axis=0,
    )


def second_kernel(grad_ref, normal_ref, root_ref, gain_ref, back_ref, low_ref, sums_ref):
    @pl.when(pl.program_id(0) == 0)
    def clear():
        sums_ref[...] = jnp.zeros_like(sums_ref)

    grad = grad_ref[...]
    back = norm_back(grad, normal_ref[...], root_ref[...], gain_ref[...])
    back_ref[...] = back
    low_ref[...] = low(back)
    sums_ref[...] += norm_sums(grad, normal_ref[...])


def second_back(clock, grad, normal, root, gain):
    length = grad.shape[0]
    step = 128
    rows = pl.BlockSpec((step, D), lambda i: (i, 0))
    return clock.call(
        second_kernel,
        [
            jax.ShapeDtypeStruct((length, D), jnp.float32),
            jax.ShapeDtypeStruct((length, D), jnp.bfloat16),
            jax.ShapeDtypeStruct((8, D), jnp.float32),
        ],
        [grad, normal, root, gain[None]],
        [rows, rows, pl.BlockSpec((step, 1), lambda i: (i, 0)), whole_spec((1, D))],
        [rows, rows, whole_spec((8, D))],
        (length // step,),
        "second_back",
    )


def inner_kernel(branch_ref, w_ref, inner_ref, out_ref):
    act_grad = dot(branch_ref[...], w_ref[...], 1, 1)
    inner = inner_ref[...]
    slope = 0.5 * (1.0 + lax.erf(inner * SQRT_HALF)) + inner * (
        DENSITY * jnp.exp(-0.5 * inner * inner)
    )
    out_ref[...] = low(act_grad * slope)


def inner_back(clock, branch_low, w_out, at, inner):
    length, wide = inner.shape
    step = 512
    cols = pl.BlockSpec((length, step), lambda j: (0, j))
    return clock.call(
        inner_kernel,
        jax.ShapeDtypeStruct((length, wide), jnp.bfloat16),
        [branch_low, w_out, inner],
        [
            whole_spec(branch_low.shape),
            pl.BlockSpec((None, None, step, D), lambda j: (0, at, j, 0)),
            cols,
        ],
        cols,
        (wide // step,),
        "inner_back",
    )


def first_kernel(
    inner_ref, w_ref, back_ref, normal_ref, root_ref, gain_ref, out_ref, sums_ref, sum_ref
):
    step = pl.program_id(0)
    part = dot(inner_ref[...], w_ref[...], 1, 1)

    @pl.when(step == 0)
    def start():
        sum_ref[...] = back_ref[...] + part

    @pl.when(step > 0)
    def more():
        sum_ref[...] += part

    @pl.when(step == pl.num_programs(0) - 1)
    def finish():
        tile = 128
        sums = jnp.zeros((8, D), jnp.float32)
        for at in range(0, sum_ref.shape[0], tile):
            span = slice(at, at + tile)
            grad = sum_ref[span, :]
            out_ref[span, :] = norm_back(
                grad, normal_ref[span, :], root_ref[span, :], gain_ref[...]
            )
            sums = sums + norm_sums(grad, normal_ref[span, :])
        sums_ref[...] = sums


def first_back(clock, inner_low, w_in, at, sum_grad, normal, root, gain):
    length, wide = inner_low.shape
    step = 768
    return clock.call(
        first_kernel,
        [
            jax.ShapeDtypeStruct((length, D), jnp.float32),
            jax.ShapeDtypeStruct((8, D), jnp.float32),
        ],
        [inner_low, w_in, sum_grad, normal, root, gain[None]],
        [
            pl.BlockSpec((length, step), lambda j: (0, j)),
            pl.BlockSpec((None, None, D, step), lambda j: (0, at, 0, j)),
            whole_spec((length, D)),
            whole_spec((length, D)),
            whole_spec((length, 1)),
            whole_spec((1, D)),
        ],
        [whole_spec((length, D)), whole_spec((8, D))],
        (wide // step,),
        "first_back",
        [pltpu.VMEM((length, D), jnp.float32)],
    )


def context_kernel(count_ref, own_ref, other_ref, w_ref, out_ref, attn_ref):
    rows = own_ref.shape[0]
    mask = (lax.broadcasted_iota(jnp.int32, (rows, 1), 0) < count_ref[0]).astype(jnp.float32)
    attn = low((own_ref[...] + other_ref[...]) * mask)
    attn_ref[...] = attn
    out_ref[...] = low(dot(attn, w_ref[...], 1, 1))


def context_back(clock, count, own, other, out_w, at):
    shape = jax.ShapeDtypeStruct(own.shape, jnp.bfloat16)
    return clock.call(
        context_kernel,
        [shape, shape],
        [own, other, out_w],
        [
            whole_spec(own.shape),
            whole_spec(own.shape),
            pl.BlockSpec((None, None, D, D), lambda i, c: (0, at, 0, 0)),
        ],
        [whole_spec(own.shape), whole_spec(own.shape)],
        (1,),
        "context_back",
        (),
        [count],
    )


def input_kernel(grad_ref, w_ref, start_ref, out_ref):
    step = pl.program_id(0)
    part = dot(grad_ref[0], w_ref[0], 1, 1)

    @pl.when(step == 0)
    def start():
        out_ref[...] = start_ref[...] + part

    @pl.when(step > 0)
    def more():
        out_ref[...] += part


def input_back(clock, grads, weights, at, start, first, count):
    length = grads.shape[1]
    return clock.call(
        input_kernel,
        jax.ShapeDtypeStruct(start.shape, jnp.float32),
        [grads, weights, start],
        [
            pl.BlockSpec((1, length, D), lambda j: (first + j, 0, 0)),
            pl.BlockSpec((None, None, 1, D, D), lambda j: (0, at, first + j, 0, 0)),
            whole_spec(start.shape),
        ],
        whole_spec(start.shape),
        (count,),
        "input_back",
    )


def normalize(values):
    center = values - jnp.mean(values, axis=-1, keepdims=True)
    root = lax.rsqrt(jnp.mean(center * center, axis=-1, keepdims=True) + EPS)
    return center * root, root


def swap_stream(values):
    return lax.ppermute(values, "stream", SWAP)


def layer_forward(hidden, spatial, weights, out_w, layer_at, biases, count, pause):
    projections, w_in, w_out, gains, shifts = weights
    length = hidden.shape[0]
    chunks = len(biases)
    rows = length // chunks
    rounded = low(hidden)
    projected = (
        low(dot(rounded, projections[0])),
        low(dot(projections[1], rounded, 0, 1)),
        low(dot(rounded, projections[2])),
        low(dot(spatial, projections[3])),
        low(dot(projections[4], spatial, 0, 1)),
    )
    contexts, mixed, probs = [], [], []
    last = None
    for at in range(chunks):
        bias = biases[at]
        bias = bias(last) if callable(bias) else bias
        context, attn, prob = attend(count, projected, bias, out_w, layer_at, at, rows)
        contexts.append(context)
        mixed.append(attn + swap_stream(attn))
        probs.append(prob)
        last = attn
    extra = pause(last)
    mixed = jnp.concatenate(mixed, axis=0)
    if extra is not None:
        mixed = gate(mixed, *extra)
    first_normal, first_root = normalize(hidden + mixed)
    normed = first_normal * gains[0] + shifts[0]
    normed_low = low(normed)
    inner = dot(normed_low, w_in)
    activated = low(0.5 * inner * (1.0 + lax.erf(inner * SQRT_HALF)))
    second_normal, second_root = normalize(normed + dot(activated, w_out))
    result = second_normal * gains[1] + shifts[1]
    kept = (
        rounded,
        projected,
        jnp.concatenate(contexts, axis=0),
        probs,
        (first_normal, first_root),
        normed_low,
        inner,
        activated,
        (second_normal, second_root),
    )
    return result, kept, extra


def local(
    dp_size,
    tokens,
    boxes,
    rel_one,
    rel_two,
    vis_count,
    spatial_tables,
    proj_weights,
    out_weights,
    ffn_in,
    ffn_out,
    norm_gains,
    norm_shifts,
    bias_tables,
    cotangent,
):
    length = tokens.shape[2]
    stream_at = lax.axis_index("stream")
    me = lax.axis_index("dp").astype(jnp.int32).reshape(1)
    count = jnp.where(stream_at == 0, length, vis_count).astype(jnp.int32)
    rowmask = (jnp.arange(length, dtype=jnp.int32)[:, None] < count[0]).astype(jnp.float32)
    rel = (rel_one[0, 0], rel_two[0, 0])
    bin_ids = jnp.arange(spatial_tables.shape[1], dtype=jnp.int32)
    hot_x = low(boxes[0, 0, 0][:, None] == bin_ids[None, :])
    hot_y = low(boxes[0, 0, 1][:, None] == bin_ids[None, :])
    spatial = low(dot(hot_x, spatial_tables[0]) + dot(hot_y, spatial_tables[1]))
    tables = bias_tables[0].astype(jnp.float32)
    tables = jnp.stack(
        [
            jnp.pad(tables[:, :, :NB1], ((0, 0), (0, 0), (0, LANES - NB1))),
            jnp.pad(tables[:, :, NB1:], ((0, 0), (0, 0), (0, LANES - NB2))),
        ],
        axis=1,
    )

    def layer_weights(layer_at):
        return (
            proj_weights[0, layer_at],
            ffn_in[0, layer_at],
            ffn_out[0, layer_at],
            norm_gains[0, layer_at],
            norm_shifts[0, layer_at],
        )

    chunks = 2
    rows = length // chunks

    def bias_of(layer_at, at):
        def make(last):
            ones = rel[0] if last is None else gate(rel[0], last)
            return score_bias(ones, rel[1], tables[layer_at], at, rows)

        return make

    hidden = tokens[0, 0].astype(jnp.float32)
    kept = []
    biases = [bias_of(0, at) for at in range(chunks)]
    for layer_at in range(LAYERS):

        def pause(last, layer_at=layer_at):
            if layer_at + 1 == LAYERS:
                return None
            return [bias_of(layer_at + 1, at)(last) for at in range(chunks)]

        hidden, state, biases = layer_forward(
            hidden, spatial, layer_weights(layer_at), out_weights, layer_at, biases, count, pause
        )
        kept.append(state)
    output = low(hidden * rowmask)[None, None]

    grad = cotangent[0, 0].astype(jnp.float32) * rowmask
    clock = Order()
    both_orders = orders(dp_size)
    step_order = {
        name + layer: both_orders[name + layer in NEAR]
        for name in ("tall", "wide", "token", "place")
        for layer in "01"
    }
    moves = {}
    state = {"grad1": grad}

    def move(name, blocks):
        moves[name] = Reduction(clock, blocks, step_order[name], dp_size)

    def second(layer):
        gains = norm_gains[0, int(layer)]
        normal, root = kept[int(layer)][8]
        results = second_back(clock, state["grad" + layer], normal, root, gains[1])
        state["sum" + layer], state["branch" + layer], state["second_sums" + layer] = results

    def tall(layer):
        activated = kept[int(layer)][7]
        name = "tall" + layer
        move(name, tall_grad(clock, activated, state["branch" + layer], me, dp_size, step_order[name]))

    def inner(layer):
        state["inner" + layer] = inner_back(
            clock, state["branch" + layer], ffn_out, int(layer), kept[int(layer)][6]
        )

    def wide(layer):
        normed_low = kept[int(layer)][5]
        name = "wide" + layer
        move(name, wide_grad(clock, normed_low, state["inner" + layer], me, dp_size, step_order[name]))

    def first(layer):
        normal, root = kept[int(layer)][4]
        gains = norm_gains[0, int(layer)]
        state["first" + layer], state["first_sums" + layer] = first_back(
            clock,
            state["inner" + layer],
            ffn_in,
            int(layer),
            state["sum" + layer],
            normal,
            root,
            gains[0],
        )
        state["other" + layer] = swap_stream(state["first" + layer])

    def context(layer):
        state["context" + layer], state["attn" + layer] = context_back(
            clock, count, state["first" + layer], state["other" + layer], out_weights, int(layer)
        )

    def attention(layer):
        query, key_t, value, squery, skey_t = kept[int(layer)][1]
        state["proj" + layer], state["scores" + layer] = attend_back(
            clock,
            (query, key_t.T, value.T, squery, skey_t.T),
            kept[int(layer)][3],
            state["context" + layer],
            state["attn" + layer],
        )

    def token(layer):
        lefts = [(kept[int(layer)][0], 3)]
        name = "token" + layer
        move(name, proj_grad(clock, lefts, state["proj" + layer], 0, me, dp_size, step_order[name]))

    def place_step(layer):
        lefts = [(spatial, 2), (kept[int(layer)][2], 1)]
        name = "place" + layer
        move(name, proj_grad(clock, lefts, state["proj" + layer], 3, me, dp_size, step_order[name]))

    def dx(layer):
        grad = input_back(
            clock, state["proj" + layer], proj_weights, int(layer), state["first" + layer], 0, 3
        )
        state["grad" + str(int(layer) - 1)] = grad

    def space(layer):
        last = int(layer) + 1 == LAYERS
        start = jnp.zeros((length, D), jnp.float32) if last else state["space" + str(int(layer) + 1)]
        state["space" + layer] = input_back(
            clock, state["proj" + layer], proj_weights, int(layer), start, 3, 2
        )

    bins = spatial_tables.shape[1]

    def table(layer):
        moves["all0"] = EverySum(clock, boxes[0, 0], low(state["space0"]), bins, dp_size)

    def bucket(layer):
        state["buckets" + layer] = bucket_sums(clock, rel[0], rel[1], state["scores" + layer])

    def tiny(layer):
        norms = []
        for at in "01":
            sums = (state["first_sums" + at], state["second_sums" + at])
            norms += [sums[0][0], sums[1][0], sums[0][1], sums[1][1]]
        buckets = [state["buckets" + at] for at in "01"]
        flat = jnp.concatenate(
            [part.reshape(-1, LANES) for part in (jnp.stack(norms), jnp.stack(buckets))], axis=0
        )
        moves["norms0"] = SmallSum(clock, flat, dp_size)

    kernels = (
        second,
        tall,
        inner,
        wide,
        first,
        context,
        attention,
        token,
        place_step,
        dx,
        space,
        table,
        bucket,
        tiny,
    )
    for step in PLAN:
        name, layer = step // 2, str(step % 2)
        if name < len(kernels):
            kernels[name](layer)
        else:
            moves[NAMES[name - len(kernels)] + layer].advance()
    owns = {name: moves[name].finish() for name in step_order}
    layers = "01"
    scattered = (
        jnp.stack([jnp.concatenate([owns["token" + at], owns["place" + at][:2]]) for at in layers]),
        jnp.stack([owns["place" + at][2] for at in layers]),
        jnp.stack([owns["wide" + at] for at in layers]),
        jnp.stack([owns["tall" + at] for at in layers]),
    )
    shared = moves["all0"].finish().reshape(2, bins, D)
    flat = moves["norms0"].finish()
    normed = flat[: 4 * LAYERS * D // LANES].reshape(LAYERS, 4, D)
    width = D // dp_size
    normed = lax.dynamic_slice_in_dim(normed, me[0] * width, width, 2)
    bucket_own = flat[4 * LAYERS * D // LANES :].reshape(1, LAYERS, HEADS, NB1 + NB2)
    return (
        output,
        state["grad-1"][None, None],
        shared,
        *(part[None] for part in scattered),
        normed[None, :, :2],
        normed[None, :, 2:],
        bucket_own,
    )


NAMES = ("tall", "wide", "token", "place", "all", "norms")
(SECOND0, SECOND1, TALL0, TALL1, INNER0, INNER1, WIDE0, WIDE1, FIRST0, FIRST1) = range(10)
(CONTEXT0, CONTEXT1, ATTEND0, ATTEND1, TOKEN0, TOKEN1, PLACE0, PLACE1, DX0, DX1) = range(10, 20)
(SPACE0, SPACE1, TABLE0, TABLE1, BUCKET0, BUCKET1, TINY0, TINY1) = range(20, 28)
(T0, T1, W0, W1, K0, K1, P0, P1, A0, A1, N0, N1) = range(28, 40)
NEAR = ("wide1", "place1",)
PLAN = (
    SECOND1, TALL1, INNER1, WIDE1, FIRST1, T1, W1, CONTEXT1, ATTEND1, T1, TOKEN1, W1, DX1, SECOND0,
    K1, T1, TALL0, INNER0, W1, T1, WIDE0, T0, SPACE1, FIRST0, W1, K1, PLACE1, BUCKET1, CONTEXT0, P1,
    W0, K1, ATTEND0, SPACE0, K1, TABLE0, DX0, P1, A0, W0, P1, A0, W0, P1, TOKEN0, A0, K0, T0, A0,
    W0, PLACE0, A0, P0, A0, T0, BUCKET0, A0, K0, T0, TINY0, P0, A0, N0, N0, K0, P0, A0, N0, K0, N0,
    A0, P0,
)


def solution(mesh):
    placed = (
        P("stream", "dp", None, None),
        P("stream", "dp", None, None),
        P("stream", "dp", None, None),
        P("stream", "dp", None, None),
        P("dp"),
        P(),
        P("stream", None, None, None, None),
        P("stream", None, None, None),
        P("stream", None, None, None),
        P("stream", None, None, None),
        P("stream", None, None, None),
        P("stream", None, None, None),
        P("stream", None, None, None),
        P("stream", "dp", None, None),
    )
    return jax.shard_map(
        partial(local, mesh.shape["dp"]),
        mesh=mesh,
        in_specs=placed,
        out_specs=(
            P("stream", "dp", None, None),
            P("stream", "dp", None, None),
            P(),
            P("stream", None, None, "dp", None),
            P("stream", None, "dp", None),
            P("stream", None, "dp", None),
            P("stream", None, "dp", None),
            P("stream", None, None, "dp"),
            P("stream", None, None, "dp"),
            P("stream", None, None, None),
        ),
        check_vma=False,
    )
```

time: 1700 us -> 813 us (0.48)
  waiting for transfers between devices: 1030 us -> 162 us
  Pallas kernels: 0 us -> 440 us
  matrix products: 370 us -> 44.1 us
  local copies, waits for them, and re-layouts: 140 us -> 59.4 us
  other arithmetic: 97 us -> 23.8 us
  starting transfers between devices: 0.92 us -> 70.5 us
  blocking collectives: 41 us -> 0 us
    reduce_scatter x3 -> x0, waiting for transfers between devices: 478 us -> none  [the longest x1 199 us: local(): lax.psum_scatter(stacked[3], 'dp', scatter_dimension=1, tiled=True)]
    pallas_call x0 -> x79, Pallas kernels: none -> 440 us  [the longest x71 354 us: call(): pl.pallas_call(body, grid_spec=pltpu.PrefetchScalarGridSpec(num_scalar_pr...]
    dot_general x54 -> x16, matrix products: 370 us -> 44.1 us  [dot(): lax.dot_general(left, right, (((left_dim,), (right_dim,)), ((), ())), pre...]
    psum x5 -> x0, waiting for transfers between devices: 301 us -> none  [the longest x1 159 us: local(): lax.psum((jnp.stack([table_x, table_y]), bucket_all), ('stream', 'dp'))]
    unnamed x14 -> x0, waiting for transfers between devices: 249 us -> none
    ppermute x0 -> x52, waiting for transfers between devices: none -> 162 us  [the longest x44 91.9 us: swap_dp(): lax.ppermute(values, 'dp', [(index, index ^ stride) for index in range(si...]
    another operation x20 -> x2, local copies, waits for them, and re-layouts: 77.6 us -> 0.06 us  [the longest x1 0.05 us: tiny(): jnp.stack(norms)]
    ppermute x0 -> x52, starting transfers between devices: none -> 70.5 us  [the longest x44 59.7 us: swap_dp(): lax.ppermute(values, 'dp', [(index, index ^ stride) for index in range(si...]
  transfers between devices with their start and end apart: 11 -> 52, of which waited for: 9 -> 19; matrix products, arithmetic and copies ran while one was open for 17% -> 3% of each run, Pallas kernels for 0% -> 48%
where the time goes in v1:
time: 813 us; the launch traced here: 803 us
  Pallas kernels  440 us (54%)
  waiting for transfers between devices  162 us (20%)
  starting transfers between devices  70.5 us (9%)
  local copies, waits for them, and re-layouts  59.4 us (7%)
  matrix products  44.1 us (5%)
  other arithmetic  23.8 us (3%)
    pallas_call x71, Pallas kernels, call(): pl.pallas_call(body, grid_spec=pltpu.PrefetchScalarGridSpec(num_scalar_pr...  354 us
    ppermute x44, waiting for transfers between devices, swap_dp(): lax.ppermute(values, 'dp', [(index, index ^ stride) for index in range(si...  91.9 us
    ppermute x44, starting transfers between devices, swap_dp(): lax.ppermute(values, 'dp', [(index, index ^ stride) for index in range(si...  59.7 us
    ppermute x6, waiting for transfers between devices, swap_stream(): return lax.ppermute(values, 'stream', SWAP)  48.5 us
    pallas_call x4, Pallas kernels, attend(): pl.pallas_call(partial(attend_kernel, at, 128), grid_spec=pltpu.PrefetchS...  44.9 us
    dot_general x16, matrix products, dot(): lax.dot_general(left, right, (((left_dim,), (right_dim,)), ((), ())), pre...  44.1 us
    unnamed x241, local copies, waits for them, and re-layouts  42.2 us
    pallas_call x4, Pallas kernels, score_bias(): pl.pallas_call(bias_kernel, grid=(rows // step,), in_specs=[rel, rel, who...  41.5 us
  transfers between devices with their start and end apart: 52, of which 19 were waited for; matrix products, arithmetic and copies ran while one was open for 3% of the time, Pallas kernels for 48%

profile of v1, /device:TPU:0, one launch (start us, length us, event | category | flops | bytes accessed | tf_op | source)
XLA Modules:
  0.0 802.5 jit_solution(2069913151248592154)
XLA Ops:
  19.7 10.5 %score_bias.4.bias_ref = f32[12,256,512]{2,1,0:T(8,128)} custom-call(s32[512,512]{1,0:T(8,128)} %bitcast.178, s32[512,512]{1,0:T(8,128)} %bitcast.184, f32[2,12,128]{2,1,0:T(8,128)} %get-tuple-element.151.table_ref), custom_call_target="tpu_custom_call" | custom-call | flops 9999999827968 | bytes 1000000000 | tf_op jit(solution)/shard_map/score_bias/pallas_call | solution.py:100
  34.8 11.2 %attend.4 = (bf16[256,768]{1,0:T(8,128)(2,1)S(1)}, f32[256,768]{1,0:T(8,128)}, f32[12,256,512]{2,1,0:T(8,128)}) custom-call(s32[1]{0:T(128)} %select_n.47.count_ref.refs_0_, bf16[512,768]{1,0:T(8,128)(2,1)S(1)} %copy-done.54, bf16[768,512]{1,0:T(8,128)(2,1)S(1)} %copy.46.key_ref, bf16[512,768]{1,0:T(8,128)(2,1)S(1)} %copy-done.16, ...), custom_call_target="tpu_custom_call" | custom-call | flops 9999999827968 | bytes 1000000000 | tf_op jit(solution)/shard_map/attend/pallas_call | solution.py:170
  48.9 10.3 %score_bias.5.bias_ref = f32[12,256,512]{2,1,0:T(8,128)} custom-call(s32[512,512]{1,0:T(8,128)} %bitcast.179, s32[512,512]{1,0:T(8,128)} %bitcast.185, f32[2,12,128]{2,1,0:T(8,128)} %get-tuple-element.151.table_ref), custom_call_target="tpu_custom_call" | custom-call | flops 9999999827968 | bytes 1000000000 | tf_op jit(solution)/shard_map/score_bias/pallas_call | solution.py:100
  63.8 11.1 %attend.5 = (bf16[256,768]{1,0:T(8,128)(2,1)S(1)}, f32[256,768]{1,0:T(8,128)}, f32[12,256,512]{2,1,0:T(8,128)}) custom-call(s32[1]{0:T(128)} %select_n.47.count_ref.refs_0_, bf16[512,768]{1,0:T(8,128)(2,1)S(1)} %copy-done.55, bf16[768,512]{1,0:T(8,128)(2,1)S(1)} %copy.46.key_ref, bf16[512,768]{1,0:T(8,128)(2,1)S(1)} %copy-done.17, ...), custom_call_target="tpu_custom_call" | custom-call | flops 9999999827968 | bytes 1000000000 | tf_op jit(solution)/shard_map/attend/pallas_call | solution.py:170
  75.6 10.3 %score_bias.6.bias_ref = f32[12,256,512]{2,1,0:T(8,128)} custom-call(s32[512,512]{1,0:T(8,128)} %bitcast.180, s32[512,512]{1,0:T(8,128)} %bitcast.186, f32[2,12,128]{2,1,0:T(8,128)} %get-tuple-element.150.table_ref), custom_call_target="tpu_custom_call" | custom-call | flops 9999999827968 | bytes 1000000000 | tf_op jit(solution)/shard_map/score_bias/pallas_call | solution.py:100
  85.9 10.3 %score_bias.7.bias_ref = f32[12,256,512]{2,1,0:T(8,128)} custom-call(s32[512,512]{1,0:T(8,128)} %bitcast.181, s32[512,512]{1,0:T(8,128)} %bitcast.187, f32[2,12,128]{2,1,0:T(8,128)} %get-tuple-element.150.table_ref), custom_call_target="tpu_custom_call" | custom-call | flops 9999999827968 | bytes 1000000000 | tf_op jit(solution)/shard_map/score_bias/pallas_call | solution.py:100
  139.0 11.5 %attend.7 = (bf16[256,768]{1,0:T(8,128)(2,1)S(1)}, f32[256,768]{1,0:T(8,128)}, f32[12,256,512]{2,1,0:T(8,128)}) custom-call(s32[1]{0:T(128)} %select_n.47.count_ref.refs_0_, bf16[512,768]{1,0:T(8,128)(2,1)S(1)} %copy-done.62, bf16[768,512]{1,0:T(8,128)(2,1)S(1)} %copy-done.20, bf16[512,768]{1,0:T(8,128)(2,1)S(1)} %copy-done.21, ...), custom_call_target="tpu_custom_call" | custom-call | flops 9999999827968 | bytes 1000000000 | tf_op jit(solution)/shard_map/attend/pallas_call | solution.py:170
  151.3 11.1 %attend.6 = (bf16[256,768]{1,0:T(8,128)(2,1)S(1)}, f32[256,768]{1,0:T(8,128)}, f32[12,256,512]{2,1,0:T(8,128)}) custom-call(s32[1]{0:T(128)} %select_n.47.count_ref.refs_0_, bf16[512,768]{1,0:T(8,128)(2,1)S(1)} %copy-done.62, bf16[768,512]{1,0:T(8,128)(2,1)S(1)} %copy-done.20, bf16[512,768]{1,0:T(8,128)(2,1)S(1)} %copy-done.21, ...), custom_call_target="tpu_custom_call" | custom-call | flops 9999999827968 | bytes 1000000000 | tf_op jit(solution)/shard_map/attend/pallas_call | solution.py:170
  171.3 12.7 %collective-permute-done.3 = f32[256,768]{1,0:T(8,128)} collective-permute-done((f32[256,768]{1,0:T(8,128)}, f32[256,768]{1,0:T(8,128)}, u32[]{:S(2)}, u32[]{:S(2)}) %collective-permute-start.3) | collective-permute-done | bytes 786464 | tf_op jit(solution)/shard_map/ppermute | solution.py:874
  185.4 13.9 %collective-permute-done.2 = f32[256,768]{1,0:T(8,128)} collective-permute-done((f32[256,768]{1,0:T(8,128)}, f32[256,768]{1,0:T(8,128)}, u32[]{:S(2)}, u32[]{:S(2)}) %collective-permute-start.2) | collective-permute-done | bytes 786464 | tf_op jit(solution)/shard_map/ppermute | solution.py:874
  272.0 21.9 %collective-permute-done.4.refs_2_ = f32[512,768]{1,0:T(8,128)} collective-permute-done((f32[512,768]{1,0:T(8,128)}, f32[512,768]{1,0:T(8,128)}, u32[]{:S(2)}, u32[]{:S(2)}) %collective-permute-start.4) | collective-permute-done | bytes 1572896 | tf_op jit(solution)/shard_map/ppermute | solution.py:874
  297.3 19.9 %attend_back.2 = (bf16[6,512,768]{2,1,0:T(8,128)(2,1)}, bf16[12,512,512]{2,1,0:T(8,128)(2,1)}) custom-call(bf16[512,768]{1,0:T(8,128)(2,1)S(1)} %copy-done.63, bf16[512,768]{1,0:T(8,128)(2,1)S(1)} %copy-done.12, bf16[768,512]{1,0:T(8,128)(2,1)S(1)} %bitcast.174, bf16[512,768]{1,0:T(8,128)(2,1)S(1)} %copy-done.61, bf16[512,768]{1,0:T(8,128)(2,1)S(1)} %copy-done.10, ...), custom_call_target="tpu_custom_call" | custom-call | flops 9999999827968 | bytes 1000000000 | tf_op jit(solution)/shard_map/attend_back/pallas_call | solution.py:53
  345.2 9.1 %collective-permute-done.9.refs_3_ = f32[2,192,768]{2,1,0:T(8,128)} collective-permute-done((f32[2,192,768]{2,1,0:T(8,128)}, f32[2,192,768]{2,1,0:T(8,128)}, u32[]{:S(2)}, u32[]{:S(2)}) %collective-permute-start.9) | collective-permute-done | bytes 1179680 | tf_op jit(solution)/shard_map/ppermute | solution.py:463
  419.5 13.0 %collective-permute-start.17 = (f32[2,3,48,768]{3,2,1,0:T(8,128)}, f32[2,3,48,768]{3,2,1,0:T(8,128)}, u32[]{:S(2)}, u32[]{:S(2)}) collective-permute-start(f32[2,3,48,768]{3,2,1,0:T(8,128)} %add_blocks.51.refs_4_), channel_id=1, source_target_pairs={{0,4},{1,5},{2,6},{3,7},{4,0},{5,1},{6,2},{7,3},{8,12},{9,13},{10,... | collective-permute-start | bytes 2654216 | tf_op jit(solution)/shard_map/ppermute | solution.py:463
  439.3 25.8 %bucket_sums.2.refs_4_ = f32[96,192]{1,0:T(8,128)S(1)} custom-call(s32[512,512]{1,0:T(8,128)S(1)} %bitcast.182, s32[512,512]{1,0:T(8,128)S(1)} %bitcast.188, bf16[12,512,512]{2,1,0:T(8,128)(2,1)} %get-tuple-element.88.refs_2_, f32[8,3,48,768]{3,2,1,0:T(8,128)} %get-tuple-element.91.refs_3_), custom_call_target="tpu_custom_call" | custom-call | flops 9999999827968 | bytes 1000000000 | tf_op jit(solution)/shard_map/bucket_sums/pallas_call | solution.py:53
  484.5 19.9 %attend_back.3 = (bf16[6,512,768]{2,1,0:T(8,128)(2,1)}, bf16[12,512,512]{2,1,0:T(8,128)(2,1)}) custom-call(bf16[512,768]{1,0:T(8,128)(2,1)S(1)} %copy-done.56, bf16[512,768]{1,0:T(8,128)(2,1)S(1)} %bitcast.169, bf16[768,512]{1,0:T(8,128)(2,1)S(1)} %bitcast.170, bf16[512,768]{1,0:T(8,128)(2,1)S(1)} %copy-done.59, ...), custom_call_target="tpu_custom_call" | custom-call | flops 9999999827968 | bytes 1000000000 | tf_op jit(solution)/shard_map/attend_back/pallas_call | solution.py:53
  508.0 14.3 %collective-permute-done.20.refs_4_ = f32[1,3,48,768]{3,2,1,0:T(8,128)} collective-permute-done((f32[1,3,48,768]{3,2,1,0:T(8,128)}, f32[1,3,48,768]{3,2,1,0:T(8,128)}, u32[]{:S(2)}, u32[]{:S(2)}) %collective-permute-start.20) | collective-permute-done | bytes 442400 | tf_op jit(solution)/shard_map/ppermute | solution.py:463
  524.0 9.0 %table_grad.1 = (f32[16,64,768]{2,1,0:T(8,128)}, f32[16,64,768]{2,1,0:T(8,128)}) custom-call(s32[1]{0:T(128)} %bitcast.47.refs_0_, s32[2,512]{1,0:T(2,128)S(1)} %bitcast.177, bf16[512,768]{1,0:T(8,128)(2,1)S(1)} %convert_element_type.125.refs_2_, f32[1,3,48,768]{3,2,1,0:T(8,128)S(1)} %add_blocks.55.refs_3_), custom_call_target="tpu_custom_call" | custom-call | flops 9999999827968 | bytes 1000000000 | tf_op jit(solution)/shard_map/table_grad/pallas_call | solution.py:53
  571.8 16.0 %collective-permute-done.23.refs_2_ = f32[8,64,768]{2,1,0:T(8,128)} collective-permute-done((f32[8,64,768]{2,1,0:T(8,128)}, f32[8,64,768]{2,1,0:T(8,128)}, u32[]{:S(2)}, u32[]{:S(2)}) %collective-permute-start.23) | collective-permute-done | bytes 1572896 | tf_op jit(solution)/shard_map/ppermute | solution.py:636
  647.1 9.7 %collective-permute-done.32.refs_5_ = f32[1,64,768]{2,1,0:T(8,128)} collective-permute-done((f32[1,64,768]{2,1,0:T(8,128)}, f32[1,64,768]{2,1,0:T(8,128)}, u32[]{:S(2)}, u32[]{:S(2)}) %collective-permute-start.32) | collective-permute-done | bytes 196640 | tf_op jit(solution)/shard_map/ppermute | solution.py:463
  673.8 25.7 %bucket_sums.3.refs_2_ = f32[96,192]{1,0:T(8,128)S(1)} custom-call(s32[512,512]{1,0:T(8,128)S(1)} %bitcast.183, s32[512,512]{1,0:T(8,128)S(1)} %bitcast.189, bf16[12,512,512]{2,1,0:T(8,128)(2,1)} %get-tuple-element.107.refs_2_, f32[1,192,768]{2,1,0:T(8,128)} %add_blocks.70.refs_3_), custom_call_target="tpu_custom_call" | custom-call | flops 9999999827968 | bytes 1000000000 | tf_op jit(solution)/shard_map/bucket_sums/pallas_call | solution.py:53
  716.4 8.4 %collective-permute-done.38.refs_1_ = f32[4,64,768]{2,1,0:T(8,128)} collective-permute-done((f32[4,64,768]{2,1,0:T(8,128)}, f32[4,64,768]{2,1,0:T(8,128)}, u32[]{:S(2)}, u32[]{:S(2)}) %collective-permute-start.38) | collective-permute-done | bytes 786464 | tf_op jit(solution)/shard_map/ppermute | solution.py:463
  737.7 21.6 %collective-permute-done.43.refs_3_ = f32[2,3,48,768]{3,2,1,0:T(8,128)} collective-permute-done((f32[2,3,48,768]{3,2,1,0:T(8,128)}, f32[2,3,48,768]{3,2,1,0:T(8,128)}, u32[]{:S(2)}, u32[]{:S(2)}) %collective-permute-start.43) | collective-permute-done | bytes 884768 | tf_op jit(solution)/shard_map/ppermute | solution.py:463
  766.9 10.0 %join.7.refs_2_.refs_1_ = f32[16,64,768]{2,1,0:T(8,128)} custom-call(s32[1]{0:T(128)} %bitcast.47.refs_0_, f32[8,64,768]{2,1,0:T(8,128)} %join.6.refs_2_.refs_1_, f32[8,64,768]{2,1,0:T(8,128)} %collective-permute-done.42.refs_2_, f32[1,3,48,768]{3,2,1,0:T(8,128)} %add_blocks.76.refs_3_), custom_call_target="tpu_custom_call" | custom-call | flops 9999999827968 | bytes 1000000000 | tf_op jit(solution)/shard_map/join/pallas_call | solution.py:53
  (490 shorter events, 462.3 us)
Async XLA Ops:
  46.0 59.9 %collective-permute-start = (f32[256,768]{1,0:T(8,128)}, f32[256,768]{1,0:T(8,128)}, u32[]{:S(2)}, u32[]{:S(2)}) collective-permute-start(f32[256,768]{1,0:T(8,128)} %get-tuple-element.61), channel_id=1, source_target_pairs={{0,16},{16,0},{1,17},{17,1},{2,18},{18,2},{3,19},{19,3},{4,20},{20... | collective-permute-start | bytes 2359304 | tf_op jit(solution)/shard_map/ppermute | solution.py:874
  257.3 36.6 %collective-permute-start.4 = (f32[512,768]{1,0:T(8,128)}, f32[512,768]{1,0:T(8,128)}, u32[]{:S(2)}, u32[]{:S(2)}) collective-permute-start(f32[512,768]{1,0:T(8,128)} %get-tuple-element.72.refs_2_.refs_1_), channel_id=1, source_target_pairs={{0,16},{16,0},{1,17},{17,1},{2,18},{18,2},{3,19},{19,3},{4,20},{20... | collective-permute-start | bytes 4718600 | tf_op jit(solution)/shard_map/ppermute | solution.py:874
  264.5 53.2 %collective-permute-start.8 = (f32[4,192,768]{2,1,0:T(8,128)}, f32[4,192,768]{2,1,0:T(8,128)}, u32[]{:S(2)}, u32[]{:S(2)}) collective-permute-start(f32[4,192,768]{2,1,0:T(8,128)} %add_blocks.41.refs_2_), channel_id=1, source_target_pairs={{0,2},{1,3},{2,0},{3,1},{4,6},{5,7},{6,4},{7,5},{8,10},{9,11},{10,... | collective-permute-start | bytes 7077896 | tf_op jit(solution)/shard_map/ppermute | solution.py:463
  270.4 58.4 %collective-permute-start.7 = (f32[4,48,3072]{2,1,0:T(8,128)}, f32[4,48,3072]{2,1,0:T(8,128)}, u32[]{:S(2)}, u32[]{:S(2)}) collective-permute-start(f32[4,48,3072]{2,1,0:T(8,128)} %add_blocks.42.refs_4_), channel_id=1, source_target_pairs={{0,4},{1,5},{2,6},{3,7},{4,0},{5,1},{6,2},{7,3},{8,12},{9,13},{10,... | collective-permute-start | bytes 7077896 | tf_op jit(solution)/shard_map/ppermute | solution.py:463
  337.3 40.0 %collective-permute-start.13 = (f32[2,48,3072]{2,1,0:T(8,128)}, f32[2,48,3072]{2,1,0:T(8,128)}, u32[]{:S(2)}, u32[]{:S(2)}) collective-permute-start(f32[2,48,3072]{2,1,0:T(8,128)} %add_blocks.44.refs_3_), channel_id=1, source_target_pairs={{0,2},{1,3},{2,0},{3,1},{4,6},{5,7},{6,4},{7,5},{8,10},{9,11},{10,... | collective-permute-start | bytes 3538952 | tf_op jit(solution)/shard_map/ppermute | solution.py:463
  344.8 71.9 %collective-permute-start.15 = (f32[4,3,48,768]{3,2,1,0:T(8,128)}, f32[4,3,48,768]{3,2,1,0:T(8,128)}, u32[]{:S(2)}, u32[]{:S(2)}) collective-permute-start(f32[4,3,48,768]{3,2,1,0:T(8,128)} %add_blocks.45.refs_4_), channel_id=1, source_target_pairs={{0,2},{1,3},{2,0},{3,1},{4,6},{5,7},{6,4},{7,5},{8,10},{9,11},{10,... | collective-permute-start | bytes 5308424 | tf_op jit(solution)/shard_map/ppermute | solution.py:463
  393.6 80.2 %collective-permute-start.18 = (f32[8,48,3072]{2,1,0:T(8,128)}, f32[8,48,3072]{2,1,0:T(8,128)}, u32[]{:S(2)}, u32[]{:S(2)}) collective-permute-start(f32[8,48,3072]{2,1,0:T(8,128)} %get-tuple-element.86.refs_2_), channel_id=1, source_target_pairs={{0,1},{1,0},{2,3},{3,2},{4,5},{5,4},{6,7},{7,6},{8,9},{9,8},{10,11... | collective-permute-start | bytes 14155784 | tf_op jit(solution)/shard_map/ppermute | solution.py:463
  397.9 226.4 %collective-permute-start.30 = (f32[4,192,768]{2,1,0:T(8,128)}, f32[4,192,768]{2,1,0:T(8,128)}, u32[]{:S(2)}, u32[]{:S(2)}) collective-permute-start(f32[4,192,768]{2,1,0:T(8,128)} %add_blocks.49.refs_3_), channel_id=1, source_target_pairs={{0,2},{1,3},{2,0},{3,1},{4,6},{5,7},{6,4},{7,5},{8,10},{9,11},{10,... | collective-permute-start | bytes 7077896 | tf_op jit(solution)/shard_map/ppermute | solution.py:463
  412.7 53.9 %collective-permute-start.14 = (f32[512,768]{1,0:T(8,128)}, f32[512,768]{1,0:T(8,128)}, u32[]{:S(2)}, u32[]{:S(2)}) collective-permute-start(f32[512,768]{1,0:T(8,128)} %get-tuple-element.87.refs_5_.refs_1_.refs_2_), channel_id=1, source_target_pairs={{0,16},{16,0},{1,17},{17,1},{2,18},{18,2},{3,19},{19,3},{4,20},{20... | collective-permute-start | bytes 4718600 | tf_op jit(solution)/shard_map/ppermute | solution.py:874
  419.5 59.3 %collective-permute-start.17 = (f32[2,3,48,768]{3,2,1,0:T(8,128)}, f32[2,3,48,768]{3,2,1,0:T(8,128)}, u32[]{:S(2)}, u32[]{:S(2)}) collective-permute-start(f32[2,3,48,768]{3,2,1,0:T(8,128)} %add_blocks.51.refs_4_), channel_id=1, source_target_pairs={{0,4},{1,5},{2,6},{3,7},{4,0},{5,1},{6,2},{7,3},{8,12},{9,13},{10,... | collective-permute-start | bytes 2654216 | tf_op jit(solution)/shard_map/ppermute | solution.py:463
  473.7 65.8 %collective-permute-start.22 = (f32[4,3,48,768]{3,2,1,0:T(8,128)}, f32[4,3,48,768]{3,2,1,0:T(8,128)}, u32[]{:S(2)}, u32[]{:S(2)}) collective-permute-start(f32[4,3,48,768]{3,2,1,0:T(8,128)} %add_blocks.52.refs_2_), channel_id=1, source_target_pairs={{0,4},{1,5},{2,6},{3,7},{4,0},{5,1},{6,2},{7,3},{8,12},{9,13},{10,... | collective-permute-start | bytes 5308424 | tf_op jit(solution)/shard_map/ppermute | solution.py:463
  478.1 73.2 %collective-permute-start.25 = (f32[4,48,3072]{2,1,0:T(8,128)}, f32[4,48,3072]{2,1,0:T(8,128)}, u32[]{:S(2)}, u32[]{:S(2)}) collective-permute-start(f32[4,48,3072]{2,1,0:T(8,128)} %add_blocks.53.refs_4_), channel_id=1, source_target_pairs={{0,2},{1,3},{2,0},{3,1},{4,6},{5,7},{6,4},{7,5},{8,10},{9,11},{10,... | collective-permute-start | bytes 7077896 | tf_op jit(solution)/shard_map/ppermute | solution.py:463
  481.1 41.2 %collective-permute-start.20 = (f32[1,3,48,768]{3,2,1,0:T(8,128)}, f32[1,3,48,768]{3,2,1,0:T(8,128)}, u32[]{:S(2)}, u32[]{:S(2)}) collective-permute-start(f32[1,3,48,768]{3,2,1,0:T(8,128)} %add_blocks.54.refs_9_), channel_id=1, source_target_pairs={{0,8},{1,9},{2,10},{3,11},{4,12},{5,13},{6,14},{7,15},{8,0},{9,1},... | collective-permute-start | bytes 1327112 | tf_op jit(solution)/shard_map/ppermute | solution.py:463
  551.0 36.8 %collective-permute-start.23 = (f32[8,64,768]{2,1,0:T(8,128)}, f32[8,64,768]{2,1,0:T(8,128)}, u32[]{:S(2)}, u32[]{:S(2)}) collective-permute-start(f32[8,64,768]{2,1,0:T(8,128)} %add_blocks.57.refs_3_), channel_id=1, source_target_pairs={{0,16},{16,0},{1,17},{17,1},{2,18},{18,2},{3,19},{19,3},{4,20},{20... | collective-permute-start | bytes 4718600 | tf_op jit(solution)/shard_map/ppermute | solution.py:636
  554.4 41.5 %collective-permute-start.28 = (f32[2,48,3072]{2,1,0:T(8,128)}, f32[2,48,3072]{2,1,0:T(8,128)}, u32[]{:S(2)}, u32[]{:S(2)}) collective-permute-start(f32[2,48,3072]{2,1,0:T(8,128)} %add_blocks.58.refs_4_), channel_id=1, source_target_pairs={{0,4},{1,5},{2,6},{3,7},{4,0},{5,1},{6,2},{7,3},{8,12},{9,13},{10,... | collective-permute-start | bytes 3538952 | tf_op jit(solution)/shard_map/ppermute | solution.py:463
  598.4 38.9 %collective-permute-start.33 = (f32[1,48,3072]{2,1,0:T(8,128)}, f32[1,48,3072]{2,1,0:T(8,128)}, u32[]{:S(2)}, u32[]{:S(2)}) collective-permute-start(f32[1,48,3072]{2,1,0:T(8,128)} %add_blocks.61.refs_5_), channel_id=1, source_target_pairs={{0,8},{1,9},{2,10},{3,11},{4,12},{5,13},{6,14},{7,15},{8,0},{9,1},... | collective-permute-start | bytes 1769480 | tf_op jit(solution)/shard_map/ppermute | solution.py:463
  623.7 82.6 %collective-permute-start.41 = (f32[4,3,48,768]{3,2,1,0:T(8,128)}, f32[4,3,48,768]{3,2,1,0:T(8,128)}, u32[]{:S(2)}, u32[]{:S(2)}) collective-permute-start(f32[4,3,48,768]{3,2,1,0:T(8,128)} %add_blocks.64.refs_3_), channel_id=1, source_target_pairs={{0,2},{1,3},{2,0},{3,1},{4,6},{5,7},{6,4},{7,5},{8,10},{9,11},{10,... | collective-permute-start | bytes 5308424 | tf_op jit(solution)/shard_map/ppermute | solution.py:463
  627.2 43.1 %collective-permute-start.37 = (f32[2,192,768]{2,1,0:T(8,128)}, f32[2,192,768]{2,1,0:T(8,128)}, u32[]{:S(2)}, u32[]{:S(2)}) collective-permute-start(f32[2,192,768]{2,1,0:T(8,128)} %add_blocks.65.refs_5_), channel_id=1, source_target_pairs={{0,4},{1,5},{2,6},{3,7},{4,0},{5,1},{6,2},{7,3},{8,12},{9,13},{10,... | collective-permute-start | bytes 3538952 | tf_op jit(solution)/shard_map/ppermute | solution.py:463
  666.1 46.0 %collective-permute-start.39 = (f32[4,3,48,768]{3,2,1,0:T(8,128)}, f32[4,3,48,768]{3,2,1,0:T(8,128)}, u32[]{:S(2)}, u32[]{:S(2)}) collective-permute-start(f32[4,3,48,768]{3,2,1,0:T(8,128)} %add_blocks.69.refs_2_), channel_id=1, source_target_pairs={{0,2},{1,3},{2,0},{3,1},{4,6},{5,7},{6,4},{7,5},{8,10},{9,11},{10,... | collective-permute-start | bytes 5308424 | tf_op jit(solution)/shard_map/ppermute | solution.py:463
  673.0 36.0 %collective-permute-start.40 = (f32[1,192,768]{2,1,0:T(8,128)}, f32[1,192,768]{2,1,0:T(8,128)}, u32[]{:S(2)}, u32[]{:S(2)}) collective-permute-start(f32[1,192,768]{2,1,0:T(8,128)} %add_blocks.70.refs_3_), channel_id=1, source_target_pairs={{0,8},{1,9},{2,10},{3,11},{4,12},{5,13},{6,14},{7,15},{8,0},{9,1},... | collective-permute-start | bytes 1769480 | tf_op jit(solution)/shard_map/ppermute | solution.py:463
  714.6 44.7 %collective-permute-start.43 = (f32[2,3,48,768]{3,2,1,0:T(8,128)}, f32[2,3,48,768]{3,2,1,0:T(8,128)}, u32[]{:S(2)}, u32[]{:S(2)}) collective-permute-start(f32[2,3,48,768]{3,2,1,0:T(8,128)} %add_blocks.73.refs_2_), channel_id=1, source_target_pairs={{0,4},{1,5},{2,6},{3,7},{4,0},{5,1},{6,2},{7,3},{8,12},{9,13},{10,... | collective-permute-start | bytes 2654216 | tf_op jit(solution)/shard_map/ppermute | solution.py:463
  730.4 36.5 %collective-permute-start.42 = (f32[8,64,768]{2,1,0:T(8,128)}, f32[8,64,768]{2,1,0:T(8,128)}, u32[]{:S(2)}, u32[]{:S(2)}) collective-permute-start(f32[8,64,768]{2,1,0:T(8,128)} %join.6.refs_2_.refs_1_), channel_id=1, source_target_pairs={{0,16},{16,0},{1,17},{17,1},{2,18},{18,2},{3,19},{19,3},{4,20},{20... | collective-permute-start | bytes 4718600 | tf_op jit(solution)/shard_map/ppermute | solution.py:636
  733.5 43.4 %collective-permute-start.48 = (f32[1,66,128]{2,1,0:T(8,128)}, f32[1,66,128]{2,1,0:T(8,128)}, u32[]{:S(2)}, u32[]{:S(2)}) collective-permute-start(f32[1,66,128]{2,1,0:T(8,128)} %add_blocks.74.refs_4_.refs_0_), channel_id=1, source_target_pairs={{0,2},{1,3},{2,0},{3,1},{4,6},{5,7},{6,4},{7,5},{8,10},{9,11},{10,... | collective-permute-start | bytes 101384 | tf_op jit(solution)/shard_map/ppermute | solution.py:463
  736.1 45.1 %collective-permute-start.50 = (f32[1,3,48,768]{3,2,1,0:T(8,128)}, f32[1,3,48,768]{3,2,1,0:T(8,128)}, u32[]{:S(2)}, u32[]{:S(2)}) collective-permute-start(f32[1,3,48,768]{3,2,1,0:T(8,128)} %add_blocks.75.refs_4_), channel_id=1, source_target_pairs={{0,8},{1,9},{2,10},{3,11},{4,12},{5,13},{6,14},{7,15},{8,0},{9,1},... | collective-permute-start | bytes 1327112 | tf_op jit(solution)/shard_map/ppermute | solution.py:463
  (148 other events, 1370.0 us)

commit v2 on v1

--- a/solution.py
+++ b/solution.py
@@ -42,12 +42,28 @@
     def __init__(self):
         self.last = ()
 
-    def call(self, kernel, shapes, operands, in_specs, out_specs, grid, name, scratch=(), scalars=()):
+    def call(
+        self,
+        kernel,
+        shapes,
+        operands,
+        in_specs,
+        out_specs,
+        grid,
+        name,
+        scratch=(),
+        scalars=(),
+        carried=(),
+        mark=0,
+    ):
         after = tuple(self.last)
+        if any(one is other for one in after for other in carried):
+            after = ()
         taken = len(scalars) + len(operands)
+        unread = len(carried) + len(after)
 
         def body(*refs):
-            kernel(*refs[:taken], *refs[taken + len(after) :])
+            kernel(*refs[:taken], *refs[taken + unread :])
 
         single = not isinstance(shapes, list)
         results = pl.pallas_call(
@@ -55,16 +71,17 @@
             grid_spec=pltpu.PrefetchScalarGridSpec(
                 num_scalar_prefetch=len(scalars),
                 grid=grid,
-                in_specs=list(in_specs) + [pl.BlockSpec(memory_space=pl.ANY)] * len(after),
+                in_specs=list(in_specs) + [pl.BlockSpec(memory_space=pl.ANY)] * unread,
                 out_specs=out_specs,
                 scratch_shapes=list(scratch),
             ),
             out_shape=shapes,
+            input_output_aliases={taken + at: at for at in range(len(carried))},
             compiler_params=pltpu.CompilerParams(vmem_limit_bytes=VMEM_LIMIT),
             cost_estimate=COST,
             name=name,
-        )(*scalars, *operands, *after)
-        self.last = (results if single else results[0],)
+        )(*scalars, *operands, *carried, *after)
+        self.last = (results if single else results[mark],)
         return results
 
 
@@ -92,20 +109,20 @@
     lax.fori_loop(0, rows // 8, group, 0)
 
 
-def score_bias(rel_one, rel_two, table, at, rows):
+def score_bias(clock, rel_one, rel_two, table, at, rows):
     length = rel_one.shape[1]
     step = 64
     first = at * rows // step
     rel = pl.BlockSpec((step, length), lambda i: (first + i, 0))
-    return pl.pallas_call(
+    return clock.call(
         bias_kernel,
-        grid=(rows // step,),
-        in_specs=[rel, rel, whole_spec(table.shape)],
-        out_specs=pl.BlockSpec((HEADS, step, length), lambda i: (0, i, 0)),
-        out_shape=jax.ShapeDtypeStruct((HEADS, rows, length), jnp.float32),
-        cost_estimate=COST,
-        name="score_bias",
-    )(rel_one, rel_two, table)
+        jax.ShapeDtypeStruct((HEADS, rows, length), jnp.float32),
+        [rel_one, rel_two, table],
+        [rel, rel, whole_spec(table.shape)],
+        pl.BlockSpec((HEADS, step, length), lambda i: (0, i, 0)),
+        (rows // step,),
+        "score_bias",
+    )
 
 
 def attend_kernel(
@@ -160,42 +177,165 @@
         attn_ref[...] = dot(context_ref[...], out_w_ref[...]) * mask
 
 
-def attend(count, projected, bias, out_w, layer_at, at, rows):
-    query, key_t, value, squery, skey_t = projected
-    length = value.shape[0]
-    row_pair = pl.BlockSpec((rows, 2 * HD), lambda p, c: (at, p))
-    key_pair = pl.BlockSpec((2 * HD, length), lambda p, c: (p, 0))
-    value_pair = pl.BlockSpec((length, 2 * HD), lambda p, c: (0, p))
+def project_kernel(flipped, left_ref, w_ref, out_ref, flip_ref):
+    step = pl.program_id(0)
+    result = low(dot(left_ref[...], w_ref[...]))
+    out_ref[...] = result
+
+    @pl.when(step >= flipped)
+    def flip():
+        flip_ref[...] = result.T
+
+
+def project(clock, left, weights, layer_at, first, count, flipped):
+    length = left.shape[0]
+    return clock.call(
+        partial(project_kernel, flipped),
+        [
+            jax.ShapeDtypeStruct((count, length, D), jnp.bfloat16),
+            jax.ShapeDtypeStruct((count - flipped, D, length), jnp.bfloat16),
+        ],
+        [left, weights],
+        [
+            whole_spec((length, D)),
+            pl.BlockSpec((None, None, None, D, D), lambda j: (0, layer_at, first + j, 0, 0)),
+        ],
+        [
+            pl.BlockSpec((None, length, D), lambda j: (j, 0, 0)),
+            pl.BlockSpec((None, D, length), lambda j: (jnp.maximum(j - flipped, 0), 0, 0)),
+        ],
+        (count,),
+        "project",
+    )
+
+
+def attend(clock, count, projected, bias, out_w, layer_at, at, rows, carried):
+    tokens, tokens_t, places, places_t = projected
+    length = tokens.shape[1]
+    row_pair = pl.BlockSpec((None, rows, 2 * HD), lambda p, c: (0, at, p))
+    key_pair = pl.BlockSpec((None, 2 * HD, length), lambda p, c: (0, p, 0))
+    value_pair = pl.BlockSpec((None, length, 2 * HD), lambda p, c: (2, 0, p))
     score_pair = pl.BlockSpec((2, rows, length), lambda p, c: (p, 0, 0))
-    return pl.pallas_call(
+    return clock.call(
         partial(attend_kernel, at, 128),
-        grid_spec=pltpu.PrefetchScalarGridSpec(
-            num_scalar_prefetch=1,
-            grid=(HEADS // 2,),
-            in_specs=[
-                row_pair,
-                key_pair,
-                value_pair,
-                row_pair,
-                key_pair,
-                score_pair,
-                pl.BlockSpec((None, None, D, D), lambda p, c: (0, layer_at, 0, 0)),
-            ],
-            out_specs=[whole_spec((rows, D)), whole_spec((rows, D)), score_pair],
-            scratch_shapes=[
-                pltpu.VMEM((2, rows, length), jnp.float32),
-                pltpu.VMEM((2, rows, length), jnp.bfloat16),
-            ],
-        ),
-        out_shape=[
-            jax.ShapeDtypeStruct((rows, D), jnp.bfloat16),
+        [
+            jax.ShapeDtypeStruct((length, D), jnp.bfloat16),
             jax.ShapeDtypeStruct((rows, D), jnp.float32),
             jax.ShapeDtypeStruct((HEADS, rows, length), jnp.float32),
         ],
-        compiler_params=pltpu.CompilerParams(vmem_limit_bytes=VMEM_LIMIT),
-        cost_estimate=COST,
-        name="attend",
-    )(count, query, key_t, value, squery, skey_t, bias, out_w)
+        [tokens, tokens_t, tokens, places, places_t, bias, out_w],
+        [
+            row_pair,
+            key_pair,
+            value_pair,
+            row_pair,
+            key_pair,
+            score_pair,
+            pl.BlockSpec((None, None, D, D), lambda p, c: (0, layer_at, 0, 0)),
+        ],
+        [pl.BlockSpec((rows, D), lambda p, c: (at, 0)), whole_spec((rows, D)), score_pair],
+        (HEADS // 2,),
+        "attend",
+        [
+            pltpu.VMEM((2, rows, length), jnp.float32),
+            pltpu.VMEM((2, rows, length), jnp.bfloat16),
+        ],
+        [count],
+        carried,
+        1,
+    )
+
+
+def ffn_kernel(
+    x_ref,
+    own_ref,
+    other_ref,
+    gain_ref,
+    shift_ref,
+    w_in_ref,
+    w_out_ref,
+    result_ref,
+    rounded_ref,
+    first_ref,
+    first_root_ref,
+    low_ref,
+    inner_ref,
+    act_ref,
+    second_ref,
+    second_root_ref,
+    sum_ref,
+):
+    step = pl.program_id(0)
+
+    @pl.when(step == 0)
+    def start():
+        normal, root = normalize(
+            x_ref[...].astype(jnp.float32) + (own_ref[...] + other_ref[...])
+        )
+        normed = normal * gain_ref[0:1, :] + shift_ref[0:1, :]
+        first_ref[...] = normal
+        first_root_ref[...] = root
+        low_ref[...] = low(normed)
+        sum_ref[...] = normed
+
+    inner = dot(low_ref[...], w_in_ref[...])
+    inner_ref[...] = inner
+    act = low(0.5 * inner * (1.0 + lax.erf(inner * SQRT_HALF)))
+    act_ref[...] = act
+    sum_ref[...] += dot(act, w_out_ref[...])
+
+    @pl.when(step == pl.num_programs(0) - 1)
+    def finish():
+        normal, root = normalize(sum_ref[...])
+        second_ref[...] = normal
+        second_root_ref[...] = root
+        result = normal * gain_ref[1:2, :] + shift_ref[1:2, :]
+        result_ref[...] = result
+        rounded_ref[...] = low(result)
+
+
+def feed_forward(clock, x, own, other, gains, shifts, w_in, w_out, layer_at, at, carried):
+    length = x.shape[0]
+    rows = own.shape[0]
+    wide = w_in.shape[-1]
+    step = D
+    narrow = pl.BlockSpec((rows, D), lambda j: (at, 0))
+    thin = pl.BlockSpec((rows, 1), lambda j: (at, 0))
+    broad = pl.BlockSpec((rows, step), lambda j: (at, j))
+
+    def shape(columns, kind):
+        return jax.ShapeDtypeStruct((length, columns), kind)
+
+    return clock.call(
+        ffn_kernel,
+        [
+            shape(D, jnp.float32),
+            shape(D, jnp.bfloat16),
+            shape(D, jnp.float32),
+            shape(1, jnp.float32),
+            shape(D, jnp.bfloat16),
+            shape(wide, jnp.float32),
+            shape(wide, jnp.bfloat16),
+            shape(D, jnp.float32),
+            shape(1, jnp.float32),
+        ],
+        [x, own, other, gains, shifts, w_in, w_out],
+        [
+            narrow,
+            whole_spec((rows, D)),
+            whole_spec((rows, D)),
+            whole_spec((2, D)),
+            whole_spec((2, D)),
+            pl.BlockSpec((None, None, D, step), lambda j: (0, layer_at, 0, j)),
+            pl.BlockSpec((None, None, step, D), lambda j: (0, layer_at, j, 0)),
+        ],
+        [narrow, narrow, narrow, thin, narrow, broad, broad, narrow, thin],
+        (wide // step,),
+        "feed_forward",
+        [pltpu.VMEM((rows, D), jnp.float32)],
+        (),
+        carried,
+    )
 
 
 def attend_back_kernel(
@@ -247,10 +387,12 @@
 
 
 def attend_back(clock, projected, probs, context_grad, attn_low):
-    query, key, value_t, squery, skey = projected
-    length = query.shape[0]
+    tokens, tokens_t, places, places_t = projected
+    length = tokens.shape[1]
     pair = pl.BlockSpec((length, 2 * HD), lambda p: (0, p))
-    value_pair = pl.BlockSpec((2 * HD, length), lambda p: (p, 0))
+    first = pl.BlockSpec((None, length, 2 * HD), lambda p: (0, 0, p))
+    second = pl.BlockSpec((None, length, 2 * HD), lambda p: (1, 0, p))
+    value_pair = pl.BlockSpec((None, 2 * HD, length), lambda p: (1, p, 0))
     prob_specs = [pl.BlockSpec((2,) + prob.shape[1:], lambda p: (p, 0, 0)) for prob in probs]
     return clock.call(
         partial(attend_back_kernel, 128),
@@ -258,8 +400,8 @@
             jax.ShapeDtypeStruct((6, length, D), jnp.bfloat16),
             jax.ShapeDtypeStruct((HEADS, length, length), jnp.bfloat16),
         ],
-        [query, key, value_t, squery, skey, context_grad, attn_low, *probs],
-        [pair, pair, value_pair, pair, pair, pair, pair] + prob_specs,
+        [tokens, tokens, tokens_t, places, places, context_grad, attn_low, *probs],
+        [first, second, value_pair, first, second, pair, pair] + prob_specs,
         [
             pl.BlockSpec((6, length, 2 * HD), lambda p: (0, 0, p)),
             pl.BlockSpec((2, length, length), lambda p: (p, 0, 0)),
@@ -273,9 +415,10 @@
     )
 
 
-def bucket_kernel(one_ref, two_ref, grad_ref, out_ref, sum_ref):
+def bucket_kernel(group, one_ref, two_ref, *refs):
+    grad_refs, (out_ref, sum_ref) = refs[:-2], refs[-2:]
     step = pl.program_id(0)
-    group, length = one_ref.shape
+    rows, length = one_ref.shape
     buckets = NB1 + NB2
 
     @pl.when(step == 0)
@@ -284,40 +427,46 @@
 
     first_ids = lax.broadcasted_iota(jnp.int32, (NB1, 1), 0)
     second_ids = lax.broadcasted_iota(jnp.int32, (NB2, 1), 0)
-    hot = []
-    for row in range(group):
-        hot.append(low((one_ref[row : row + 1, :] == first_ids).astype(jnp.float32)))
-        hot.append(low((two_ref[row : row + 1, :] == second_ids).astype(jnp.float32)))
-    hot = jnp.concatenate(hot, axis=0)
-    grads = grad_ref[...].reshape(HEADS * group, length)
-    sum_ref[...] += dot(hot, grads, 1, 1)
+    hot, grads = [], []
+    for start in range(0, rows, group):
+        column = []
+        for row in range(start, start + group):
+            column.append(low((one_ref[row : row + 1, :] == first_ids).astype(jnp.float32)))
+            column.append(low((two_ref[row : row + 1, :] == second_ids).astype(jnp.float32)))
+        hot.append(jnp.concatenate(column, axis=0))
+        parts = [ref[:, start : start + group, :].reshape(HEADS * group, length) for ref in grad_refs]
+        grads.append(jnp.concatenate(parts, axis=0))
+    sum_ref[...] += dot(jnp.concatenate(hot, axis=1), jnp.concatenate(grads, axis=1), 1, 1)
 
     @pl.when(step == pl.num_programs(0) - 1)
     def finish():
-        member = lax.broadcasted_iota(jnp.int32, (1, HEADS * group), 1) % group
-        total = jnp.zeros((buckets, HEADS * group), jnp.float32)
+        member = lax.broadcasted_iota(jnp.int32, (1, sum_ref.shape[1]), 1) % group
+        total = jnp.zeros((buckets, sum_ref.shape[1]), jnp.float32)
         for row in range(group):
             block = sum_ref[row * buckets : (row + 1) * buckets, :]
             total = total + jnp.where(member == row, block, 0.0)
         out_ref[...] = total
 
 
-def bucket_sums(clock, rel_one, rel_two, score_grad):
+def bucket_sums(clock, rel_one, rel_two, score_grads):
     length = rel_one.shape[0]
-    group = 16
+    group, rows = 8, 32
     buckets = NB1 + NB2
-    rel = pl.BlockSpec((group, length), lambda i: (i, 0))
+    columns = len(score_grads) * HEADS * group
+    rel = pl.BlockSpec((rows, length), lambda i: (i, 0))
+    block = pl.BlockSpec((HEADS, rows, length), lambda i: (0, i, 0))
     sums = clock.call(
-        bucket_kernel,
-        jax.ShapeDtypeStruct((buckets, HEADS * group), jnp.float32),
-        [rel_one, rel_two, score_grad],
-        [rel, rel, pl.BlockSpec((HEADS, group, length), lambda i: (0, i, 0))],
-        whole_spec((buckets, HEADS * group)),
-        (length // group,),
+        partial(bucket_kernel, group),
+        jax.ShapeDtypeStruct((buckets, columns), jnp.float32),
+        [rel_one, rel_two, *score_grads],
+        [rel, rel] + [block] * len(score_grads),
+        whole_spec((buckets, columns)),
+        (length // rows,),
         "bucket_sums",
-        [pltpu.VMEM((group * buckets, HEADS * group), jnp.float32)],
-    )
-    return jnp.sum(sums.reshape(buckets, HEADS, group), axis=2).T
+        [pltpu.VMEM((group * buckets, columns), jnp.float32)],
+    )
+    sums = jnp.sum(sums.reshape(buckets, len(score_grads), HEADS, group), axis=3)
+    return jnp.transpose(sums, (1, 2, 0))
 
 
 def dp_strides(size):
@@ -537,42 +686,43 @@
     )
 
 
-def join_kernel(starts, *refs):
-    step = pl.program_id(0)
-    for part, ref in enumerate(refs[:-1]):
-
-        @pl.when((step >= starts[part]) & (step < starts[part + 1]))
-        def copy(ref=ref):
-            refs[-1][...] = ref[...]
-
-
-def join(clock, parts, at=None):
-    starts = [0]
+def join_kernel(swapped, at_ref, *refs):
+    parts, (out_ref, buffer, in_sem, out_sem) = refs[:-4], refs[-4:]
+    arrive, leave = [], []
+    spot = 0
     for part in parts:
-        starts.append(starts[-1] + part.shape[0])
-    shape = parts[0].shape[1:]
-    mask = starts[-1] - 1
-
-    def spec(index):
-        start, count = starts[index], parts[index].shape[0]
-        return pl.BlockSpec((1,) + shape, lambda i, *m: (jnp.clip(i - start, 0, count - 1), 0, 0))
-
-    def kernel(*refs):
-        join_kernel(starts, *(refs if at is None else refs[1:]))
-
-    def spot(i, *m):
-        return (i if at is None else jnp.bitwise_xor(i, m[0][0] & mask), 0, 0)
-
-    return clock.call(
-        kernel,
-        jax.ShapeDtypeStruct((starts[-1],) + shape, jnp.float32),
+        for block in range(part.shape[0]):
+            to = jnp.bitwise_xor(spot, at_ref[0] & swapped)
+            arrive.append(pltpu.make_async_copy(part.at[block], buffer.at[spot], in_sem.at[spot]))
+            leave.append(pltpu.make_async_copy(buffer.at[spot], out_ref.at[to], out_sem.at[spot]))
+            spot += 1
+    for copy in arrive:
+        copy.start()
+    for first, second in zip(arrive, leave):
+        first.wait()
+        second.start()
+    for copy in leave:
+        copy.wait()
+
+
+def join(clock, parts, at, swapped):
+    count = sum(part.shape[0] for part in parts)
+    shape = (count,) + parts[0].shape[1:]
+    anywhere = pl.BlockSpec(memory_space=pl.ANY)
+    return clock.call(
+        partial(join_kernel, swapped),
+        jax.ShapeDtypeStruct(shape, jnp.float32),
         parts,
-        [spec(index) for index in range(len(parts))],
-        pl.BlockSpec((1,) + shape, spot),
-        (starts[-1],),
+        [anywhere] * len(parts),
+        anywhere,
+        (),
         "join",
-        (),
-        () if at is None else [at],
+        [
+            pltpu.VMEM(shape, jnp.float32),
+            pltpu.SemaphoreType.DMA((count,)),
+            pltpu.SemaphoreType.DMA((count,)),
+        ],
+        [at],
     )
 
 
@@ -647,8 +797,8 @@
                 self.left = 0
                 sent = self.parts[0]
             else:
-                at = self.at if len(self.up) == 1 else None
-                sent = join(self.clock, self.parts, at)
+                swapped = self.size - 1 if len(self.up) == 1 else 0
+                sent = join(self.clock, self.parts, self.at, swapped)
                 self.parts = [sent]
             self.parts.append(self.swap(sent, self.up.pop(0)))
 
@@ -872,54 +1022,6 @@
 
 def swap_stream(values):
     return lax.ppermute(values, "stream", SWAP)
-
-
-def layer_forward(hidden, spatial, weights, out_w, layer_at, biases, count, pause):
-    projections, w_in, w_out, gains, shifts = weights
-    length = hidden.shape[0]
-    chunks = len(biases)
-    rows = length // chunks
-    rounded = low(hidden)
-    projected = (
-        low(dot(rounded, projections[0])),
-        low(dot(projections[1], rounded, 0, 1)),
-        low(dot(rounded, projections[2])),
-        low(dot(spatial, projections[3])),
-        low(dot(projections[4], spatial, 0, 1)),
-    )
-    contexts, mixed, probs = [], [], []
-    last = None
-    for at in range(chunks):
-        bias = biases[at]
-        bias = bias(last) if callable(bias) else bias
-        context, attn, prob = attend(count, projected, bias, out_w, layer_at, at, rows)
-        contexts.append(context)
-        mixed.append(attn + swap_stream(attn))
-        probs.append(prob)
-        last = attn
-    extra = pause(last)
-    mixed = jnp.concatenate(mixed, axis=0)
-    if extra is not None:
-        mixed = gate(mixed, *extra)
-    first_normal, first_root = normalize(hidden + mixed)
-    normed = first_normal * gains[0] + shifts[0]
-    normed_low = low(normed)
-    inner = dot(normed_low, w_in)
-    activated = low(0.5 * inner * (1.0 + lax.erf(inner * SQRT_HALF)))
-    second_normal, second_root = normalize(normed + dot(activated, w_out))
-    result = second_normal * gains[1] + shifts[1]
-    kept = (
-        rounded,
-        projected,
-        jnp.concatenate(contexts, axis=0),
-        probs,
-        (first_normal, first_root),
-        normed_low,
-        inner,
-        activated,
-        (second_normal, second_root),
-    )
-    return result, kept, extra
 
 
 def local(
@@ -958,43 +1060,63 @@
         axis=1,
     )
 
-    def layer_weights(layer_at):
-        return (
-            proj_weights[0, layer_at],
-            ffn_in[0, layer_at],
-            ffn_out[0, layer_at],
-            norm_gains[0, layer_at],
-            norm_shifts[0, layer_at],
-        )
-
+    clock = Order()
     chunks = 2
     rows = length // chunks
-
-    def bias_of(layer_at, at):
-        def make(last):
-            ones = rel[0] if last is None else gate(rel[0], last)
-            return score_bias(ones, rel[1], tables[layer_at], at, rows)
-
-        return make
-
-    hidden = tokens[0, 0].astype(jnp.float32)
+    hidden = rounded = tokens[0, 0]
     kept = []
-    biases = [bias_of(0, at) for at in range(chunks)]
+    places = project(clock, spatial, proj_weights, 0, 3, 2, 1)
+    biases = [None] * chunks
     for layer_at in range(LAYERS):
-
-        def pause(last, layer_at=layer_at):
-            if layer_at + 1 == LAYERS:
-                return None
-            return [bias_of(layer_at + 1, at)(last) for at in range(chunks)]
-
-        hidden, state, biases = layer_forward(
-            hidden, spatial, layer_weights(layer_at), out_weights, layer_at, biases, count, pause
+        last = layer_at + 1 == LAYERS
+        projected = (*project(clock, rounded, proj_weights, layer_at, 0, 3, 1), *places)
+        context, states, probs, moved, next_biases = (), (), [], [], []
+        for at in range(chunks):
+            bias = biases[at]
+            if bias is None:
+                bias = score_bias(clock, *rel, tables[layer_at], at, rows)
+            context, attn, prob = attend(
+                clock, count, projected, bias, out_weights, layer_at, at, rows, context
+            )
+            context = (context,)
+            probs.append(prob)
+            moved.append((attn, swap_stream(attn)))
+        for at in range(chunks):
+            states = feed_forward(
+                clock,
+                hidden,
+                *moved[at],
+                norm_gains[0, layer_at],
+                norm_shifts[0, layer_at],
+                ffn_in,
+                ffn_out,
+                layer_at,
+                at,
+                states,
+            )
+            if not last and at + 1 < chunks:
+                for part in range(chunks):
+                    next_biases.append(score_bias(clock, *rel, tables[layer_at + 1], part, rows))
+                places = project(clock, spatial, proj_weights, layer_at + 1, 3, 2, 1)
+        biases = next_biases
+        result, result_low, first, first_root, normed_low, inner, activated, second, second_root = states
+        kept.append(
+            (
+                rounded,
+                projected,
+                context[0],
+                probs,
+                (first, first_root),
+                normed_low,
+                inner,
+                activated,
+                (second, second_root),
+            )
         )
-        kept.append(state)
+        hidden, rounded = result, result_low
     output = low(hidden * rowmask)[None, None]
 
     grad = cotangent[0, 0].astype(jnp.float32) * rowmask
-    clock = Order()
     both_orders = orders(dp_size)
     step_order = {
         name + layer: both_orders[name + layer in NEAR]
@@ -1049,10 +1171,9 @@
         )
 
     def attention(layer):
-        query, key_t, value, squery, skey_t = kept[int(layer)][1]
         state["proj" + layer], state["scores" + layer] = attend_back(
             clock,
-            (query, key_t.T, value.T, squery, skey_t.T),
+            kept[int(layer)][1],
             kept[int(layer)][3],
             state["context" + layer],
             state["attn" + layer],
@@ -1087,17 +1208,16 @@
         moves["all0"] = EverySum(clock, boxes[0, 0], low(state["space0"]), bins, dp_size)
 
     def bucket(layer):
-        state["buckets" + layer] = bucket_sums(clock, rel[0], rel[1], state["scores" + layer])
+        scores = [state["scores" + at] for at in "01"]
+        state["buckets"] = bucket_sums(clock, rel[0], rel[1], scores)
 
     def tiny(layer):
         norms = []
         for at in "01":
             sums = (state["first_sums" + at], state["second_sums" + at])
             norms += [sums[0][0], sums[1][0], sums[0][1], sums[1][1]]
-        buckets = [state["buckets" + at] for at in "01"]
-        flat = jnp.concatenate(
-            [part.reshape(-1, LANES) for part in (jnp.stack(norms), jnp.stack(buckets))], axis=0
-        )
+        parts = (jnp.stack(norms), state["buckets"])
+        flat = jnp.concatenate([part.reshape(-1, LANES) for part in parts], axis=0)
         moves["norms0"] = SmallSum(clock, flat, dp_size)
 
     kernels = (
@@ -1152,13 +1272,12 @@
 (CONTEXT0, CONTEXT1, ATTEND0, ATTEND1, TOKEN0, TOKEN1, PLACE0, PLACE1, DX0, DX1) = range(10, 20)
 (SPACE0, SPACE1, TABLE0, TABLE1, BUCKET0, BUCKET1, TINY0, TINY1) = range(20, 28)
 (T0, T1, W0, W1, K0, K1, P0, P1, A0, A1, N0, N1) = range(28, 40)
-NEAR = ("wide1", "place1",)
+NEAR = ("wide1", "place1", "wide0",)
 PLAN = (
-    SECOND1, TALL1, INNER1, WIDE1, FIRST1, T1, W1, CONTEXT1, ATTEND1, T1, TOKEN1, W1, DX1, SECOND0,
-    K1, T1, TALL0, INNER0, W1, T1, WIDE0, T0, SPACE1, FIRST0, W1, K1, PLACE1, BUCKET1, CONTEXT0, P1,
-    W0, K1, ATTEND0, SPACE0, K1, TABLE0, DX0, P1, A0, W0, P1, A0, W0, P1, TOKEN0, A0, K0, T0, A0,
-    W0, PLACE0, A0, P0, A0, T0, BUCKET0, A0, K0, T0, TINY0, P0, A0, N0, N0, K0, P0, A0, N0, K0, N0,
-    A0, P0,
+    SECOND1, TALL1, INNER1, WIDE1, FIRST1, T1, W1, CONTEXT1, ATTEND1, T1, DX1, PLACE1, W1, TOKEN1,
+    T1, P1, SECOND0, K1, TALL0, W1, T1, INNER0, SPACE1, WIDE0, W1, FIRST0, K1, T0, W0, P1, CONTEXT0,
+    ATTEND0, SPACE0, TABLE0, P1, K1, A0, W0, T0, K1, W0, A0, PLACE0, P1, TOKEN0, P0, A0, K0, T0, A0,
+    BUCKET0, W0, A0, TINY0, A0, P0, A0, DX0, K0, A0, P0, N0, N0, T0, N0, K0, A0, K0, N0, P0, A0,
 )
 
 

time: 813 us -> 724 us (0.89)
  matrix products: 44.1 us -> 3.7 us
  local copies, waits for them, and re-layouts: 59.4 us -> 22.5 us
  starting transfers between devices: 70.5 us -> 46.5 us
  other arithmetic: 23.8 us -> 8.23 us
  waiting for transfers between devices: 162 us -> 176 us
  Pallas kernels: 440 us -> 451 us
    pallas_call x71 -> x86, Pallas kernels: 354 us -> 451 us  [call(): pl.pallas_call(body, grid_spec=pltpu.PrefetchScalarGridSpec(num_scalar_pr...]
    pallas_call x8 -> x0, Pallas kernels: 86.4 us -> none  [the longest x4 44.9 us: attend(): pl.pallas_call(partial(attend_kernel, at, 128), grid_spec=pltpu.PrefetchS...]
    dot_general x16 -> x2, matrix products: 44.1 us -> 3.7 us  [dot(): lax.dot_general(left, right, (((left_dim,), (right_dim,)), ((), ())), pre...]
    ppermute x44, waiting for transfers between devices: 91.9 us -> 123 us  [swap_dp(): lax.ppermute(values, 'dp', [(index, index ^ stride) for index in range(si...]
    unnamed x241 -> x199, local copies, waits for them, and re-layouts: 42.2 us -> 16.8 us
    ppermute x44, starting transfers between devices: 59.7 us -> 37.9 us  [swap_dp(): lax.ppermute(values, 'dp', [(index, index ^ stride) for index in range(si...]
    ppermute x2, waiting for transfers between devices: 21.2 us -> 4.39 us  [swap(): return lax.ppermute(values, 'stream', SWAP)]
  transfers between devices with their start and end apart: 52 -> 52, of which waited for: 19 -> 20; matrix products, arithmetic and copies ran while one was open for 3% -> 1% of each run, Pallas kernels for 48% -> 52%
where the time goes in v2:
time: 724 us; the launch traced here: 710 us
  Pallas kernels  451 us (62%)
  waiting for transfers between devices  176 us (24%)
  starting transfers between devices  46.5 us (6%)
  local copies, waits for them, and re-layouts  22.5 us (3%)
  other arithmetic  8.23 us (1%)
    pallas_call x86, Pallas kernels, call(): pl.pallas_call(body, grid_spec=pltpu.PrefetchScalarGridSpec(num_scalar_pr...  451 us
    ppermute x44, waiting for transfers between devices, swap_dp(): lax.ppermute(values, 'dp', [(index, index ^ stride) for index in range(si...  123 us
    ppermute x6, waiting for transfers between devices, swap_stream(): return lax.ppermute(values, 'stream', SWAP)  47.8 us
    ppermute x44, starting transfers between devices, swap_dp(): lax.ppermute(values, 'dp', [(index, index ^ stride) for index in range(si...  37.9 us
    unnamed x199, local copies, waits for them, and re-layouts  16.8 us
  transfers between devices with their start and end apart: 52, of which 20 were waited for; matrix products, arithmetic and copies ran while one was open for 1% of the time, Pallas kernels for 52%

profile of v2, /device:TPU:0, one launch (start us, length us, event | category | flops | bytes accessed | tf_op | source)
XLA Modules:
  0.0 710.2 jit_solution(8063867210992730204)
XLA Ops:
  19.7 9.3 %score_bias.4.refs_6_.refs_8_ = f32[12,256,512]{2,1,0:T(8,128)} custom-call(s32[512,512]{1,0:T(8,128)S(1)} %bitcast.88, s32[512,512]{1,0:T(8,128)S(1)} %bitcast.93, f32[2,12,128]{2,1,0:T(8,128)S(1)} %get-tuple-element.213.refs_2_, bf16[3,512,768]{2,1,0:T(8,128)(2,1)S(1)} %copy-done.42), custom_call_target="tpu_custom_call" | custom-call | flops 9999999827968 | bytes 1000000000 | tf_op jit(solution)/shard_map/score_bias/pallas_call | solution.py:69
  29.1 11.4 %attend.4 = (bf16[512,768]{1,0:T(8,128)(2,1)S(1)}, f32[256,768]{1,0:T(8,128)}, f32[12,256,512]{2,1,0:T(8,128)}) custom-call(s32[1]{0:T(128)} %select_n.47.refs_0_, bf16[3,512,768]{2,1,0:T(8,128)(2,1)} %get-tuple-element.102.refs_3_.refs_1_.refs_0_, bf16[2,768,512]{2,1,0:T(8,128)(2,1)S(1)} %get-tuple-element.103.refs_2_, ...), custom_call_target="tpu_custom_call" | custom-call | flops 9999999827968 | bytes 1000000000 | tf_op jit(solution)/shard_map/attend/pallas_call | solution.py:69
  43.4 9.3 %score_bias.5.refs_6_.refs_9_ = f32[12,256,512]{2,1,0:T(8,128)} custom-call(s32[512,512]{1,0:T(8,128)S(1)} %bitcast.89, s32[512,512]{1,0:T(8,128)S(1)} %bitcast.94, f32[2,12,128]{2,1,0:T(8,128)S(1)} %copy-done.10, f32[256,768]{1,0:T(8,128)} %get-tuple-element.105.refs_3_.refs_1_), custom_call_target="tpu_custom_call" | custom-call | flops 9999999827968 | bytes 1000000000 | tf_op jit(solution)/shard_map/score_bias/pallas_call | solution.py:69
  52.8 11.4 %attend.5 = (bf16[512,768]{1,0:T(8,128)(2,1)S(1)}, f32[256,768]{1,0:T(8,128)}, f32[12,256,512]{2,1,0:T(8,128)}) custom-call(s32[1]{0:T(128)} %select_n.47.refs_0_, bf16[3,512,768]{2,1,0:T(8,128)(2,1)} %get-tuple-element.102.refs_3_.refs_1_.refs_0_, bf16[2,768,512]{2,1,0:T(8,128)(2,1)S(1)} %get-tuple-element.103.refs_2_, ...), custom_call_target="tpu_custom_call", output_to_operand_aliasing={{0}: (8, {})} | custom-call | flops 9999999827968 | bytes 1000000000 | tf_op jit(solution)/shard_map/attend/pallas_call | solution.py:69
  65.8 10.0 %feed_forward.4 = (f32[512,768]{1,0:T(8,128)}, bf16[512,768]{1,0:T(8,128)(2,1)S(1)}, f32[512,768]{1,0:T(8,128)}, f32[512,1]{1,0:T(8,128)S(1)}, bf16[512,768]{1,0...) custom-call(bf16[512,768]{1,0:T(8,128)(2,1)S(1)} %bitcast.99, ...), custom_call_target="tpu_custom_call" | custom-call | flops 9999999827968 | bytes 1000000000 | tf_op jit(solution)/shard_map/feed_forward/pallas_call | solution.py:69
  77.3 9.3 %score_bias.6.refs_3_.refs_6_ = f32[12,256,512]{2,1,0:T(8,128)} custom-call(s32[512,512]{1,0:T(8,128)S(1)} %bitcast.90, s32[512,512]{1,0:T(8,128)S(1)} %bitcast.95, f32[2,12,128]{2,1,0:T(8,128)S(1)} %get-tuple-element.212.refs_2_, f32[512,768]{1,0:T(8,128)S(1)} %copy-done.46), custom_call_target="tpu_custom_call" | custom-call | flops 9999999827968 | bytes 1000000000 | tf_op jit(solution)/shard_map/score_bias/pallas_call | solution.py:69
  86.6 9.3 %score_bias.7.refs_2_.refs_6_ = f32[12,256,512]{2,1,0:T(8,128)} custom-call(s32[512,512]{1,0:T(8,128)S(1)} %bitcast.91, s32[512,512]{1,0:T(8,128)S(1)} %bitcast.96, f32[2,12,128]{2,1,0:T(8,128)S(1)} %get-tuple-element.212.refs_2_, f32[12,256,512]{2,1,0:T(8,128)} %score_bias.6.refs_3_.refs_6_), custom_call_target="tpu_custom_call" | custom-call | flops 9999999827968 | bytes 1000000000 | tf_op jit(solution)/shard_map/score_bias/pallas_call | solution.py:69
  100.4 9.6 %feed_forward.5 = (f32[512,768]{1,0:T(8,128)S(1)}, bf16[512,768]{1,0:T(8,128)(2,1)S(1)}, f32[512,768]{1,0:T(8,128)}, f32[512,1]{1,0:T(8,128)S(1)}, bf16[512,768]...) custom-call(bf16[512,768]{1,0:T(8,128)(2,1)S(1)} %bitcast.100, ...), custom_call_target="tpu_custom_call", output_to_operand_aliasing={{0}: (7, {}), {1}: (8, {}), {2}: (9, {}), {3}: (10, {}), {4... | custom-call | flops 9999999827968 | bytes 1000000000 | tf_op jit(solution)/shard_map/feed_forward/pallas_call | solution.py:69
  116.7 11.8 %attend.6 = (bf16[512,768]{1,0:T(8,128)(2,1)S(1)}, f32[256,768]{1,0:T(8,128)}, f32[12,256,512]{2,1,0:T(8,128)}) custom-call(s32[1]{0:T(128)} %select_n.47.refs_0_, bf16[3,512,768]{2,1,0:T(8,128)(2,1)} %get-tuple-element.120.refs_1_.refs_3_.refs_8_.refs_0_, bf16[2,768,512]{2,1,0:T(8,128)(2,1)S(1)} %get-tuple-element.121.refs_2_, ...), custom_call_target="tpu_custom_call" | custom-call | flops 9999999827968 | bytes 1000000000 | tf_op jit(solution)/shard_map/attend/pallas_call | solution.py:69
  130.5 11.4 %attend.7 = (bf16[512,768]{1,0:T(8,128)(2,1)S(1)}, f32[256,768]{1,0:T(8,128)}, f32[12,256,512]{2,1,0:T(8,128)}) custom-call(s32[1]{0:T(128)} %select_n.47.refs_0_, bf16[3,512,768]{2,1,0:T(8,128)(2,1)} %get-tuple-element.120.refs_1_.refs_3_.refs_8_.refs_0_, bf16[2,768,512]{2,1,0:T(8,128)(2,1)S(1)} %get-tuple-element.121.refs_2_, ...), custom_call_target="tpu_custom_call", output_to_operand_aliasing={{0}: (8, {})} | custom-call | flops 9999999827968 | bytes 1000000000 | tf_op jit(solution)/shard_map/attend/pallas_call | solution.py:69
  149.3 10.2 %feed_forward.6 = (f32[512,768]{1,0:T(8,128)S(1)}, bf16[512,768]{1,0:T(8,128)(2,1)S(1)}, f32[512,768]{1,0:T(8,128)}, f32[512,1]{1,0:T(8,128)S(1)}, bf16[512,768]...) custom-call(f32[512,768]{1,0:T(8,128)} %copy-done.48, ...), custom_call_target="tpu_custom_call" | custom-call | flops 9999999827968 | bytes 1000000000 | tf_op jit(solution)/shard_map/feed_forward/pallas_call | solution.py:69
  164.7 10.0 %feed_forward.7 = (f32[512,768]{1,0:T(8,128)S(1)}, bf16[512,768]{1,0:T(8,128)(2,1)S(1)}, f32[512,768]{1,0:T(8,128)}, f32[512,1]{1,0:T(8,128)S(1)}, bf16[512,768]...) custom-call(f32[512,768]{1,0:T(8,128)} %copy-done.48, ...), custom_call_target="tpu_custom_call", output_to_operand_aliasing={{0}: (7, {}), {1}: (8, {}), {2}: (9, {}), {3}: (10, {}), {4... | custom-call | flops 9999999827968 | bytes 1000000000 | tf_op jit(solution)/shard_map/feed_forward/pallas_call | solution.py:69
  225.4 21.9 %collective-permute-done.4.refs_2_ = f32[512,768]{1,0:T(8,128)} collective-permute-done((f32[512,768]{1,0:T(8,128)}, f32[512,768]{1,0:T(8,128)}, u32[]{:S(2)}, u32[]{:S(2)}) %collective-permute-start.4) | collective-permute-done | bytes 1572896 | tf_op jit(solution)/shard_map/ppermute | solution.py:1024
  250.6 19.6 %attend_back.2 = (bf16[6,512,768]{2,1,0:T(8,128)(2,1)}, bf16[12,512,512]{2,1,0:T(8,128)(2,1)}) custom-call(bf16[3,512,768]{2,1,0:T(8,128)(2,1)} %get-tuple-element.120.refs_1_.refs_3_.refs_8_.refs_0_, bf16[3,512,768]{2,1,0:T(8,128)(2,1)} %get-tuple-element.120.refs_1_.refs_3_.refs_8_.refs_0_, bf16[2,768,512]{2,1,0:T(8,128)(2,1)S(1)} %copy-done.59, ...), custom_call_target="tpu_custom_call" | custom-call | flops 9999999827968 | bytes 1000000000 | tf_op jit(solution)/shard_map/attend_back/pallas_call | solution.py:69
  359.3 14.4 %collective-permute-done.14.refs_4_ = f32[1,48,3072]{2,1,0:T(8,128)} collective-permute-done((f32[1,48,3072]{2,1,0:T(8,128)}, f32[1,48,3072]{2,1,0:T(8,128)}, u32[]{:S(2)}, u32[]{:S(2)}) %collective-permute-start.14) | collective-permute-done | bytes 589856 | tf_op jit(solution)/shard_map/ppermute | solution.py:612
  405.0 13.4 %collective-permute-done.15.refs_2_ = f32[512,768]{1,0:T(8,128)} collective-permute-done((f32[512,768]{1,0:T(8,128)}, f32[512,768]{1,0:T(8,128)}, u32[]{:S(2)}, u32[]{:S(2)}) %collective-permute-start.15) | collective-permute-done | bytes 1572896 | tf_op jit(solution)/shard_map/ppermute | solution.py:1024
  421.6 20.0 %attend_back.3 = (bf16[6,512,768]{2,1,0:T(8,128)(2,1)}, bf16[12,512,512]{2,1,0:T(8,128)(2,1)}) custom-call(bf16[3,512,768]{2,1,0:T(8,128)(2,1)} %get-tuple-element.102.refs_3_.refs_1_.refs_0_, bf16[3,512,768]{2,1,0:T(8,128)(2,1)} %get-tuple-element.102.refs_3_.refs_1_.refs_0_, bf16[2,768,512]{2,1,0:T(8,128)(2,1)S(1)} %copy-done.57, ...), custom_call_target="tpu_custom_call" | custom-call | flops 9999999827968 | bytes 1000000000 | tf_op jit(solution)/shard_map/attend_back/pallas_call | solution.py:69
  454.8 10.5 %collective-permute-done.22.refs_3_ = f32[2,3,48,768]{3,2,1,0:T(8,128)} collective-permute-done((f32[2,3,48,768]{3,2,1,0:T(8,128)}, f32[2,3,48,768]{3,2,1,0:T(8,128)}, u32[]{:S(2)}, u32[]{:S(2)}) %collective-permute-start.22) | collective-permute-done | bytes 884768 | tf_op jit(solution)/shard_map/ppermute | solution.py:612
  486.2 19.1 %collective-permute-done.26.refs_4_ = f32[1,3,48,768]{3,2,1,0:T(8,128)} collective-permute-done((f32[1,3,48,768]{3,2,1,0:T(8,128)}, f32[1,3,48,768]{3,2,1,0:T(8,128)}, u32[]{:S(2)}, u32[]{:S(2)}) %collective-permute-start.26) | collective-permute-done | bytes 442400 | tf_op jit(solution)/shard_map/ppermute | solution.py:612
  556.7 18.3 %bucket_sums.1.refs_5_ = f32[96,192]{1,0:T(8,128)S(1)} custom-call(s32[512,512]{1,0:T(8,128)S(1)} %bitcast.92, s32[512,512]{1,0:T(8,128)S(1)} %bitcast.97, bf16[12,512,512]{2,1,0:T(8,128)(2,1)} %get-tuple-element.186.refs_2_, bf16[12,512,512]{2,1,0:T(8,128)(2,1)} %get-tuple-element.187.refs_3_, f32[1,64,768]{2,1,0:T(8,128)} %add_blocks.68.refs_4_), custom_call_target="tpu_custom_call" | custom-call | flops 9999999827968 | bytes 1000000000 | tf_op jit(solution)/shard_map/bucket_sums/pallas_call | solution.py:69
  577.7 10.3 %collective-permute-done.34.refs_5_ = f32[1,64,768]{2,1,0:T(8,128)} collective-permute-done((f32[1,64,768]{2,1,0:T(8,128)}, f32[1,64,768]{2,1,0:T(8,128)}, u32[]{:S(2)}, u32[]{:S(2)}) %collective-permute-start.34) | collective-permute-done | bytes 196640 | tf_op jit(solution)/shard_map/ppermute | solution.py:612
  626.8 12.7 %collective-permute-done.39.refs_2_ = f32[4,64,768]{2,1,0:T(8,128)} collective-permute-done((f32[4,64,768]{2,1,0:T(8,128)}, f32[4,64,768]{2,1,0:T(8,128)}, u32[]{:S(2)}, u32[]{:S(2)}) %collective-permute-start.39) | collective-permute-done | bytes 786464 | tf_op jit(solution)/shard_map/ppermute | solution.py:612
  656.2 14.3 %collective-permute-done.42.refs_3_ = f32[2,3,48,768]{3,2,1,0:T(8,128)} collective-permute-done((f32[2,3,48,768]{3,2,1,0:T(8,128)}, f32[2,3,48,768]{3,2,1,0:T(8,128)}, u32[]{:S(2)}, u32[]{:S(2)}) %collective-permute-start.42) | collective-permute-done | bytes 884768 | tf_op jit(solution)/shard_map/ppermute | solution.py:612
  680.0 12.3 %collective-permute-done.50.refs_4_ = f32[1,3,48,768]{3,2,1,0:T(8,128)} collective-permute-done((f32[1,3,48,768]{3,2,1,0:T(8,128)}, f32[1,3,48,768]{3,2,1,0:T(8,128)}, u32[]{:S(2)}, u32[]{:S(2)}) %collective-permute-start.50) | collective-permute-done | bytes 442400 | tf_op jit(solution)/shard_map/ppermute | solution.py:612
  (403 shorter events, 397.3 us)
Async XLA Ops:
  65.1 35.2 %collective-permute-start = (f32[256,768]{1,0:T(8,128)}, f32[256,768]{1,0:T(8,128)}, u32[]{:S(2)}, u32[]{:S(2)}) collective-permute-start(f32[256,768]{1,0:T(8,128)} %get-tuple-element.107.refs_7_.refs_1_), channel_id=1, source_target_pairs={{0,16},{16,0},{1,17},{17,1},{2,18},{18,2},{3,19},{19,3},{4,20},{20... | collective-permute-start | bytes 2359304 | tf_op jit(solution)/shard_map/ppermute | solution.py:1024
  210.7 36.6 %collective-permute-start.4 = (f32[512,768]{1,0:T(8,128)}, f32[512,768]{1,0:T(8,128)}, u32[]{:S(2)}, u32[]{:S(2)}) collective-permute-start(f32[512,768]{1,0:T(8,128)} %get-tuple-element.147.refs_2_.refs_1_), channel_id=1, source_target_pairs={{0,16},{16,0},{1,17},{17,1},{2,18},{18,2},{3,19},{19,3},{4,20},{20... | collective-permute-start | bytes 4718600 | tf_op jit(solution)/shard_map/ppermute | solution.py:1024
  218.0 53.2 %collective-permute-start.7 = (f32[4,192,768]{2,1,0:T(8,128)}, f32[4,192,768]{2,1,0:T(8,128)}, u32[]{:S(2)}, u32[]{:S(2)}) collective-permute-start(f32[4,192,768]{2,1,0:T(8,128)} %add_blocks.41.refs_2_), channel_id=1, source_target_pairs={{0,2},{1,3},{2,0},{3,1},{4,6},{5,7},{6,4},{7,5},{8,10},{9,11},{10,... | collective-permute-start | bytes 7077896 | tf_op jit(solution)/shard_map/ppermute | solution.py:612
  223.8 64.3 %collective-permute-start.10 = (f32[4,48,3072]{2,1,0:T(8,128)}, f32[4,48,3072]{2,1,0:T(8,128)}, u32[]{:S(2)}, u32[]{:S(2)}) collective-permute-start(f32[4,48,3072]{2,1,0:T(8,128)} %add_blocks.42.refs_4_), channel_id=1, source_target_pairs={{0,4},{1,5},{2,6},{3,7},{4,0},{5,1},{6,2},{7,3},{8,12},{9,13},{10,... | collective-permute-start | bytes 7077896 | tf_op jit(solution)/shard_map/ppermute | solution.py:612
  297.7 35.0 %collective-permute-start.12 = (f32[2,48,3072]{2,1,0:T(8,128)}, f32[2,48,3072]{2,1,0:T(8,128)}, u32[]{:S(2)}, u32[]{:S(2)}) collective-permute-start(f32[2,48,3072]{2,1,0:T(8,128)} %add_blocks.44.refs_3_), channel_id=1, source_target_pairs={{0,2},{1,3},{2,0},{3,1},{4,6},{5,7},{6,4},{7,5},{8,10},{9,11},{10,... | collective-permute-start | bytes 3538952 | tf_op jit(solution)/shard_map/ppermute | solution.py:612
  315.9 86.0 %collective-permute-start.16 = (f32[4,3,48,768]{3,2,1,0:T(8,128)}, f32[4,3,48,768]{3,2,1,0:T(8,128)}, u32[]{:S(2)}, u32[]{:S(2)}) collective-permute-start(f32[4,3,48,768]{3,2,1,0:T(8,128)} %add_blocks.46.refs_4_), channel_id=1, source_target_pairs={{0,4},{1,5},{2,6},{3,7},{4,0},{5,1},{6,2},{7,3},{8,12},{9,13},{10,... | collective-permute-start | bytes 5308424 | tf_op jit(solution)/shard_map/ppermute | solution.py:612
  323.3 63.5 %collective-permute-start.19 = (f32[4,3,48,768]{3,2,1,0:T(8,128)}, f32[4,3,48,768]{3,2,1,0:T(8,128)}, u32[]{:S(2)}, u32[]{:S(2)}) collective-permute-start(f32[4,3,48,768]{3,2,1,0:T(8,128)} %add_blocks.47.refs_3_), channel_id=1, source_target_pairs={{0,2},{1,3},{2,0},{3,1},{4,6},{5,7},{6,4},{7,5},{8,10},{9,11},{10,... | collective-permute-start | bytes 5308424 | tf_op jit(solution)/shard_map/ppermute | solution.py:612
  332.6 59.0 %collective-permute-start.18 = (f32[8,192,768]{2,1,0:T(8,128)}, f32[8,192,768]{2,1,0:T(8,128)}, u32[]{:S(2)}, u32[]{:S(2)}) collective-permute-start(f32[8,192,768]{2,1,0:T(8,128)} %get-tuple-element.166.refs_4_), channel_id=1, source_target_pairs={{0,1},{1,0},{2,3},{3,2},{4,5},{5,4},{6,7},{7,6},{8,9},{9,8},{10,11... | collective-permute-start | bytes 14155784 | tf_op jit(solution)/shard_map/ppermute | solution.py:612
  335.2 38.5 %collective-permute-start.14 = (f32[1,48,3072]{2,1,0:T(8,128)}, f32[1,48,3072]{2,1,0:T(8,128)}, u32[]{:S(2)}, u32[]{:S(2)}) collective-permute-start(f32[1,48,3072]{2,1,0:T(8,128)} %add_blocks.48.refs_5_), channel_id=1, source_target_pairs={{0,8},{1,9},{2,10},{3,11},{4,12},{5,13},{6,14},{7,15},{8,0},{9,1},... | collective-permute-start | bytes 1769480 | tf_op jit(solution)/shard_map/ppermute | solution.py:612
  358.7 38.9 %collective-permute-start.17 = (f32[8,48,3072]{2,1,0:T(8,128)}, f32[8,48,3072]{2,1,0:T(8,128)}, u32[]{:S(2)}, u32[]{:S(2)}) collective-permute-start(f32[8,48,3072]{2,1,0:T(8,128)} %get-tuple-element.170.refs_5_), channel_id=1, source_target_pairs={{0,1},{1,0},{2,3},{3,2},{4,5},{5,4},{6,7},{7,6},{8,9},{9,8},{10,11... | collective-permute-start | bytes 14155784 | tf_op jit(solution)/shard_map/ppermute | solution.py:612
  389.3 79.6 %collective-permute-start.21 = (f32[2,3,48,768]{3,2,1,0:T(8,128)}, f32[2,3,48,768]{3,2,1,0:T(8,128)}, u32[]{:S(2)}, u32[]{:S(2)}) collective-permute-start(f32[2,3,48,768]{3,2,1,0:T(8,128)} %add_blocks.51.refs_2_), channel_id=1, source_target_pairs={{0,4},{1,5},{2,6},{3,7},{4,0},{5,1},{6,2},{7,3},{8,12},{9,13},{10,... | collective-permute-start | bytes 2654216 | tf_op jit(solution)/shard_map/ppermute | solution.py:612
  396.1 87.0 %collective-permute-start.27 = (f32[4,192,768]{2,1,0:T(8,128)}, f32[4,192,768]{2,1,0:T(8,128)}, u32[]{:S(2)}, u32[]{:S(2)}) collective-permute-start(f32[4,192,768]{2,1,0:T(8,128)} %add_blocks.52.refs_2_), channel_id=1, source_target_pairs={{0,2},{1,3},{2,0},{3,1},{4,6},{5,7},{6,4},{7,5},{8,10},{9,11},{10,... | collective-permute-start | bytes 7077896 | tf_op jit(solution)/shard_map/ppermute | solution.py:612
  401.9 76.8 %collective-permute-start.24 = (f32[4,48,3072]{2,1,0:T(8,128)}, f32[4,48,3072]{2,1,0:T(8,128)}, u32[]{:S(2)}, u32[]{:S(2)}) collective-permute-start(f32[4,48,3072]{2,1,0:T(8,128)} %add_blocks.53.refs_3_), channel_id=1, source_target_pairs={{0,4},{1,5},{2,6},{3,7},{4,0},{5,1},{6,2},{7,3},{8,12},{9,13},{10,... | collective-permute-start | bytes 7077896 | tf_op jit(solution)/shard_map/ppermute | solution.py:612
  404.5 60.8 %collective-permute-start.22 = (f32[2,3,48,768]{3,2,1,0:T(8,128)}, f32[2,3,48,768]{3,2,1,0:T(8,128)}, u32[]{:S(2)}, u32[]{:S(2)}) collective-permute-start(f32[2,3,48,768]{3,2,1,0:T(8,128)} %add_blocks.54.refs_4_), channel_id=1, source_target_pairs={{0,2},{1,3},{2,0},{3,1},{4,6},{5,7},{6,4},{7,5},{8,10},{9,11},{10,... | collective-permute-start | bytes 2654216 | tf_op jit(solution)/shard_map/ppermute | solution.py:612
  467.6 54.5 %collective-permute-start.30 = (f32[1,3,48,768]{3,2,1,0:T(8,128)}, f32[1,3,48,768]{3,2,1,0:T(8,128)}, u32[]{:S(2)}, u32[]{:S(2)}) collective-permute-start(f32[1,3,48,768]{3,2,1,0:T(8,128)} %add_blocks.55.refs_4_), channel_id=1, source_target_pairs={{0,8},{1,9},{2,10},{3,11},{4,12},{5,13},{6,14},{7,15},{8,0},{9,1},... | collective-permute-start | bytes 1327112 | tf_op jit(solution)/shard_map/ppermute | solution.py:612
  485.9 62.9 %collective-permute-start.32 = (f32[2,192,768]{2,1,0:T(8,128)}, f32[2,192,768]{2,1,0:T(8,128)}, u32[]{:S(2)}, u32[]{:S(2)}) collective-permute-start(f32[2,192,768]{2,1,0:T(8,128)} %add_blocks.59.refs_5_), channel_id=1, source_target_pairs={{0,4},{1,5},{2,6},{3,7},{4,0},{5,1},{6,2},{7,3},{8,12},{9,13},{10,... | collective-permute-start | bytes 3538952 | tf_op jit(solution)/shard_map/ppermute | solution.py:612
  509.8 66.0 %collective-permute-start.35 = (f32[1,48,3072]{2,1,0:T(8,128)}, f32[1,48,3072]{2,1,0:T(8,128)}, u32[]{:S(2)}, u32[]{:S(2)}) collective-permute-start(f32[1,48,3072]{2,1,0:T(8,128)} %add_blocks.61.refs_3_), channel_id=1, source_target_pairs={{0,8},{1,9},{2,10},{3,11},{4,12},{5,13},{6,14},{7,15},{8,0},{9,1},... | collective-permute-start | bytes 1769480 | tf_op jit(solution)/shard_map/ppermute | solution.py:612
  538.2 62.4 %collective-permute-start.38 = (f32[4,3,48,768]{3,2,1,0:T(8,128)}, f32[4,3,48,768]{3,2,1,0:T(8,128)}, u32[]{:S(2)}, u32[]{:S(2)}) collective-permute-start(f32[4,3,48,768]{3,2,1,0:T(8,128)} %add_blocks.64.refs_4_), channel_id=1, source_target_pairs={{0,2},{1,3},{2,0},{3,1},{4,6},{5,7},{6,4},{7,5},{8,10},{9,11},{10,... | collective-permute-start | bytes 5308424 | tf_op jit(solution)/shard_map/ppermute | solution.py:612
  547.3 73.9 %collective-permute-start.40 = (f32[4,3,48,768]{3,2,1,0:T(8,128)}, f32[4,3,48,768]{3,2,1,0:T(8,128)}, u32[]{:S(2)}, u32[]{:S(2)}) collective-permute-start(f32[4,3,48,768]{3,2,1,0:T(8,128)} %add_blocks.66.refs_4_), channel_id=1, source_target_pairs={{0,2},{1,3},{2,0},{3,1},{4,6},{5,7},{6,4},{7,5},{8,10},{9,11},{10,... | collective-permute-start | bytes 5308424 | tf_op jit(solution)/shard_map/ppermute | solution.py:612
  551.3 98.6 %collective-permute-start.46 = (f32[1,192,768]{2,1,0:T(8,128)}, f32[1,192,768]{2,1,0:T(8,128)}, u32[]{:S(2)}, u32[]{:S(2)}) collective-permute-start(f32[1,192,768]{2,1,0:T(8,128)} %add_blocks.67.refs_5_), channel_id=1, source_target_pairs={{0,8},{1,9},{2,10},{3,11},{4,12},{5,13},{6,14},{7,15},{8,0},{9,1},... | collective-permute-start | bytes 1769480 | tf_op jit(solution)/shard_map/ppermute | solution.py:612
  575.8 71.4 %collective-permute-start.43 = (f32[1,66,128]{2,1,0:T(8,128)}, f32[1,66,128]{2,1,0:T(8,128)}, u32[]{:S(2)}, u32[]{:S(2)}) collective-permute-start(f32[1,66,128]{2,1,0:T(8,128)} %maximum_bitcast_fusion.6.refs_0_), channel_id=1, source_target_pairs={{0,1},{1,0},{2,3},{3,2},{4,5},{5,4},{6,7},{7,6},{8,9},{9,8},{10,11... | collective-permute-start | bytes 101384 | tf_op jit(solution)/shard_map/ppermute | solution.py:612
  625.0 45.4 %collective-permute-start.42 = (f32[2,3,48,768]{3,2,1,0:T(8,128)}, f32[2,3,48,768]{3,2,1,0:T(8,128)}, u32[]{:S(2)}, u32[]{:S(2)}) collective-permute-start(f32[2,3,48,768]{3,2,1,0:T(8,128)} %add_blocks.72.refs_3_), channel_id=1, source_target_pairs={{0,4},{1,5},{2,6},{3,7},{4,0},{5,1},{6,2},{7,3},{8,12},{9,13},{10,... | collective-permute-start | bytes 2654216 | tf_op jit(solution)/shard_map/ppermute | solution.py:612
  646.0 49.5 %collective-permute-start.48 = (f32[1,3,48,768]{3,2,1,0:T(8,128)}, f32[1,3,48,768]{3,2,1,0:T(8,128)}, u32[]{:S(2)}, u32[]{:S(2)}) collective-permute-start(f32[1,3,48,768]{3,2,1,0:T(8,128)} %add_blocks.73.refs_2_), channel_id=1, source_target_pairs={{0,8},{1,9},{2,10},{3,11},{4,12},{5,13},{6,14},{7,15},{8,0},{9,1},... | collective-permute-start | bytes 1327112 | tf_op jit(solution)/shard_map/ppermute | solution.py:612
  654.4 39.5 %collective-permute-start.49 = (f32[1,66,128]{2,1,0:T(8,128)}, f32[1,66,128]{2,1,0:T(8,128)}, u32[]{:S(2)}, u32[]{:S(2)}) collective-permute-start(f32[1,66,128]{2,1,0:T(8,128)} %add_blocks.76.refs_4_.refs_0_), channel_id=1, source_target_pairs={{0,4},{1,5},{2,6},{3,7},{4,0},{5,1},{6,2},{7,3},{8,12},{9,13},{10,... | collective-permute-start | bytes 101384 | tf_op jit(solution)/shard_map/ppermute | solution.py:612
  (127 other events, 1244.5 us)

commit v3 on v2

--- a/solution.py
+++ b/solution.py
@@ -1274,10 +1274,10 @@
 (T0, T1, W0, W1, K0, K1, P0, P1, A0, A1, N0, N1) = range(28, 40)
 NEAR = ("wide1", "place1", "wide0",)
 PLAN = (
-    SECOND1, TALL1, INNER1, WIDE1, FIRST1, T1, W1, CONTEXT1, ATTEND1, T1, DX1, PLACE1, W1, TOKEN1,
-    T1, P1, SECOND0, K1, TALL0, W1, T1, INNER0, SPACE1, WIDE0, W1, FIRST0, K1, T0, W0, P1, CONTEXT0,
-    ATTEND0, SPACE0, TABLE0, P1, K1, A0, W0, T0, K1, W0, A0, PLACE0, P1, TOKEN0, P0, A0, K0, T0, A0,
-    BUCKET0, W0, A0, TINY0, A0, P0, A0, DX0, K0, A0, P0, N0, N0, T0, N0, K0, A0, K0, N0, P0, A0,
+    SECOND1, TALL1, INNER1, WIDE1, FIRST1, T1, W1, CONTEXT1, ATTEND1, T1, PLACE1, W1, DX1, TOKEN1,
+    T1, P1, K1, SECOND0, TALL0, W1, INNER0, T1, SPACE1, WIDE0, W1, FIRST0, K1, W0, T0, P1, CONTEXT0,
+    ATTEND0, SPACE0, TABLE0, K1, P1, A0, W0, T0, K1, W0, A0, PLACE0, TOKEN0, P0, A0, K0, T0, P1, A0,
+    BUCKET0, W0, DX0, A0, TINY0, A0, P0, A0, K0, A0, N0, P0, T0, N0, N0, K0, N0, A0, K0, P0, A0,
 )
 
 

time: 724 us -> 709 us (0.979)
  waiting for transfers between devices: 176 us -> 156 us
    ppermute x44, waiting for transfers between devices: 123 us -> 103 us  [swap_dp(): lax.ppermute(values, 'dp', [(index, index ^ stride) for index in range(si...]
    unnamed x199 -> x201, local copies, waits for them, and re-layouts: 16.8 us -> 16.5 us
  transfers between devices with their start and end apart: 52 -> 52, of which waited for: 20 -> 19; matrix products, arithmetic and copies ran while one was open for 1% -> 2% of each run, Pallas kernels for 52% -> 53%
where the time goes in v3:
time: 709 us; the launch traced here: 695 us
  Pallas kernels  449 us (63%)
  waiting for transfers between devices  156 us (22%)
  starting transfers between devices  52.9 us (7%)
  local copies, waits for them, and re-layouts  23.1 us (3%)
  other arithmetic  8.32 us (1%)
    pallas_call x86, Pallas kernels, call(): pl.pallas_call(body, grid_spec=pltpu.PrefetchScalarGridSpec(num_scalar_pr...  449 us
    ppermute x44, waiting for transfers between devices, swap_dp(): lax.ppermute(values, 'dp', [(index, index ^ stride) for index in range(si...  103 us
    ppermute x6, waiting for transfers between devices, swap_stream(): return lax.ppermute(values, 'stream', SWAP)  49.5 us
    ppermute x44, starting transfers between devices, swap_dp(): lax.ppermute(values, 'dp', [(index, index ^ stride) for index in range(si...  42.5 us
    unnamed x201, local copies, waits for them, and re-layouts  16.5 us
  transfers between devices with their start and end apart: 52, of which 19 were waited for; matrix products, arithmetic and copies ran while one was open for 2% of the time, Pallas kernels for 53%

profile of v3, /device:TPU:0, one launch (start us, length us, event | category | flops | bytes accessed | tf_op | source)
XLA Modules:
  0.0 695.1 jit_solution(3385764540382115702)
XLA Ops:
  19.7 9.3 %score_bias.4.refs_6_.refs_8_ = f32[12,256,512]{2,1,0:T(8,128)} custom-call(s32[512,512]{1,0:T(8,128)S(1)} %bitcast.88, s32[512,512]{1,0:T(8,128)S(1)} %bitcast.93, f32[2,12,128]{2,1,0:T(8,128)S(1)} %get-tuple-element.213.refs_2_, bf16[3,512,768]{2,1,0:T(8,128)(2,1)S(1)} %copy-done.43), custom_call_target="tpu_custom_call" | custom-call | flops 9999999827968 | bytes 1000000000 | tf_op jit(solution)/shard_map/score_bias/pallas_call | solution.py:69
  29.0 11.5 %attend.4 = (bf16[512,768]{1,0:T(8,128)(2,1)S(1)}, f32[256,768]{1,0:T(8,128)}, f32[12,256,512]{2,1,0:T(8,128)}) custom-call(s32[1]{0:T(128)} %select_n.47.refs_0_, bf16[3,512,768]{2,1,0:T(8,128)(2,1)} %get-tuple-element.102.refs_3_.refs_1_.refs_0_, bf16[2,768,512]{2,1,0:T(8,128)(2,1)S(1)} %get-tuple-element.103.refs_2_, ...), custom_call_target="tpu_custom_call" | custom-call | flops 9999999827968 | bytes 1000000000 | tf_op jit(solution)/shard_map/attend/pallas_call | solution.py:69
  43.5 9.3 %score_bias.5.refs_6_.refs_9_ = f32[12,256,512]{2,1,0:T(8,128)} custom-call(s32[512,512]{1,0:T(8,128)S(1)} %bitcast.89, s32[512,512]{1,0:T(8,128)S(1)} %bitcast.94, f32[2,12,128]{2,1,0:T(8,128)S(1)} %copy-done.11, f32[256,768]{1,0:T(8,128)} %get-tuple-element.105.refs_3_.refs_1_), custom_call_target="tpu_custom_call" | custom-call | flops 9999999827968 | bytes 1000000000 | tf_op jit(solution)/shard_map/score_bias/pallas_call | solution.py:69
  52.9 11.4 %attend.5 = (bf16[512,768]{1,0:T(8,128)(2,1)S(1)}, f32[256,768]{1,0:T(8,128)}, f32[12,256,512]{2,1,0:T(8,128)}) custom-call(s32[1]{0:T(128)} %select_n.47.refs_0_, bf16[3,512,768]{2,1,0:T(8,128)(2,1)} %get-tuple-element.102.refs_3_.refs_1_.refs_0_, bf16[2,768,512]{2,1,0:T(8,128)(2,1)S(1)} %get-tuple-element.103.refs_2_, ...), custom_call_target="tpu_custom_call", output_to_operand_aliasing={{0}: (8, {})} | custom-call | flops 9999999827968 | bytes 1000000000 | tf_op jit(solution)/shard_map/attend/pallas_call | solution.py:69
  65.8 10.0 %feed_forward.4 = (f32[512,768]{1,0:T(8,128)}, bf16[512,768]{1,0:T(8,128)(2,1)S(1)}, f32[512,768]{1,0:T(8,128)}, f32[512,1]{1,0:T(8,128)S(1)}, bf16[512,768]{1,0...) custom-call(bf16[512,768]{1,0:T(8,128)(2,1)S(1)} %bitcast.99, ...), custom_call_target="tpu_custom_call" | custom-call | flops 9999999827968 | bytes 1000000000 | tf_op jit(solution)/shard_map/feed_forward/pallas_call | solution.py:69
  77.3 9.3 %score_bias.6.refs_3_.refs_6_ = f32[12,256,512]{2,1,0:T(8,128)} custom-call(s32[512,512]{1,0:T(8,128)S(1)} %bitcast.90, s32[512,512]{1,0:T(8,128)S(1)} %bitcast.95, f32[2,12,128]{2,1,0:T(8,128)S(1)} %get-tuple-element.212.refs_2_, f32[512,768]{1,0:T(8,128)S(1)} %copy-done.47), custom_call_target="tpu_custom_call" | custom-call | flops 9999999827968 | bytes 1000000000 | tf_op jit(solution)/shard_map/score_bias/pallas_call | solution.py:69
  86.7 9.3 %score_bias.7.refs_2_.refs_6_ = f32[12,256,512]{2,1,0:T(8,128)} custom-call(s32[512,512]{1,0:T(8,128)S(1)} %bitcast.91, s32[512,512]{1,0:T(8,128)S(1)} %bitcast.96, f32[2,12,128]{2,1,0:T(8,128)S(1)} %get-tuple-element.212.refs_2_, f32[12,256,512]{2,1,0:T(8,128)} %score_bias.6.refs_3_.refs_6_), custom_call_target="tpu_custom_call" | custom-call | flops 9999999827968 | bytes 1000000000 | tf_op jit(solution)/shard_map/score_bias/pallas_call | solution.py:69
  100.4 9.7 %feed_forward.5 = (f32[512,768]{1,0:T(8,128)S(1)}, bf16[512,768]{1,0:T(8,128)(2,1)S(1)}, f32[512,768]{1,0:T(8,128)}, f32[512,1]{1,0:T(8,128)S(1)}, bf16[512,768]...) custom-call(bf16[512,768]{1,0:T(8,128)(2,1)S(1)} %bitcast.100, ...), custom_call_target="tpu_custom_call", output_to_operand_aliasing={{0}: (7, {}), {1}: (8, {}), {2}: (9, {}), {3}: (10, {}), {4... | custom-call | flops 9999999827968 | bytes 1000000000 | tf_op jit(solution)/shard_map/feed_forward/pallas_call | solution.py:69
  116.8 11.8 %attend.6 = (bf16[512,768]{1,0:T(8,128)(2,1)S(1)}, f32[256,768]{1,0:T(8,128)}, f32[12,256,512]{2,1,0:T(8,128)}) custom-call(s32[1]{0:T(128)} %select_n.47.refs_0_, bf16[3,512,768]{2,1,0:T(8,128)(2,1)} %get-tuple-element.120.refs_1_.refs_3_.refs_8_.refs_0_, bf16[2,768,512]{2,1,0:T(8,128)(2,1)S(1)} %get-tuple-element.121.refs_2_, ...), custom_call_target="tpu_custom_call" | custom-call | flops 9999999827968 | bytes 1000000000 | tf_op jit(solution)/shard_map/attend/pallas_call | solution.py:69
  130.6 11.4 %attend.7 = (bf16[512,768]{1,0:T(8,128)(2,1)S(1)}, f32[256,768]{1,0:T(8,128)}, f32[12,256,512]{2,1,0:T(8,128)}) custom-call(s32[1]{0:T(128)} %select_n.47.refs_0_, bf16[3,512,768]{2,1,0:T(8,128)(2,1)} %get-tuple-element.120.refs_1_.refs_3_.refs_8_.refs_0_, bf16[2,768,512]{2,1,0:T(8,128)(2,1)S(1)} %get-tuple-element.121.refs_2_, ...), custom_call_target="tpu_custom_call", output_to_operand_aliasing={{0}: (8, {})} | custom-call | flops 9999999827968 | bytes 1000000000 | tf_op jit(solution)/shard_map/attend/pallas_call | solution.py:69
  149.4 10.2 %feed_forward.6 = (f32[512,768]{1,0:T(8,128)S(1)}, bf16[512,768]{1,0:T(8,128)(2,1)S(1)}, f32[512,768]{1,0:T(8,128)}, f32[512,1]{1,0:T(8,128)S(1)}, bf16[512,768]...) custom-call(f32[512,768]{1,0:T(8,128)} %copy-done.49, ...), custom_call_target="tpu_custom_call" | custom-call | flops 9999999827968 | bytes 1000000000 | tf_op jit(solution)/shard_map/feed_forward/pallas_call | solution.py:69
  164.8 10.0 %feed_forward.7 = (f32[512,768]{1,0:T(8,128)S(1)}, bf16[512,768]{1,0:T(8,128)(2,1)S(1)}, f32[512,768]{1,0:T(8,128)}, f32[512,1]{1,0:T(8,128)S(1)}, bf16[512,768]...) custom-call(f32[512,768]{1,0:T(8,128)} %copy-done.49, ...), custom_call_target="tpu_custom_call", output_to_operand_aliasing={{0}: (7, {}), {1}: (8, {}), {2}: (9, {}), {3}: (10, {}), {4... | custom-call | flops 9999999827968 | bytes 1000000000 | tf_op jit(solution)/shard_map/feed_forward/pallas_call | solution.py:69
  225.2 22.0 %collective-permute-done.4.refs_2_ = f32[512,768]{1,0:T(8,128)} collective-permute-done((f32[512,768]{1,0:T(8,128)}, f32[512,768]{1,0:T(8,128)}, u32[]{:S(2)}, u32[]{:S(2)}) %collective-permute-start.4) | collective-permute-done | bytes 1572896 | tf_op jit(solution)/shard_map/ppermute | solution.py:1024
  250.4 19.7 %attend_back.2 = (bf16[6,512,768]{2,1,0:T(8,128)(2,1)}, bf16[12,512,512]{2,1,0:T(8,128)(2,1)}) custom-call(bf16[3,512,768]{2,1,0:T(8,128)(2,1)} %get-tuple-element.120.refs_1_.refs_3_.refs_8_.refs_0_, bf16[3,512,768]{2,1,0:T(8,128)(2,1)} %get-tuple-element.120.refs_1_.refs_3_.refs_8_.refs_0_, bf16[2,768,512]{2,1,0:T(8,128)(2,1)S(1)} %copy-done.60, ...), custom_call_target="tpu_custom_call" | custom-call | flops 9999999827968 | bytes 1000000000 | tf_op jit(solution)/shard_map/attend_back/pallas_call | solution.py:69
  352.8 16.7 %collective-permute-done.13.refs_4_ = f32[1,48,3072]{2,1,0:T(8,128)} collective-permute-done((f32[1,48,3072]{2,1,0:T(8,128)}, f32[1,48,3072]{2,1,0:T(8,128)}, u32[]{:S(2)}, u32[]{:S(2)}) %collective-permute-start.13) | collective-permute-done | bytes 589856 | tf_op jit(solution)/shard_map/ppermute | solution.py:612
  399.9 15.0 %collective-permute-done.15.refs_2_ = f32[512,768]{1,0:T(8,128)} collective-permute-done((f32[512,768]{1,0:T(8,128)}, f32[512,768]{1,0:T(8,128)}, u32[]{:S(2)}, u32[]{:S(2)}) %collective-permute-start.15) | collective-permute-done | bytes 1572896 | tf_op jit(solution)/shard_map/ppermute | solution.py:1024
  418.2 19.8 %attend_back.3 = (bf16[6,512,768]{2,1,0:T(8,128)(2,1)}, bf16[12,512,512]{2,1,0:T(8,128)(2,1)}) custom-call(bf16[3,512,768]{2,1,0:T(8,128)(2,1)} %get-tuple-element.102.refs_3_.refs_1_.refs_0_, bf16[3,512,768]{2,1,0:T(8,128)(2,1)} %get-tuple-element.102.refs_3_.refs_1_.refs_0_, bf16[2,768,512]{2,1,0:T(8,128)(2,1)S(1)} %copy-done.58, ...), custom_call_target="tpu_custom_call" | custom-call | flops 9999999827968 | bytes 1000000000 | tf_op jit(solution)/shard_map/attend_back/pallas_call | solution.py:69
  442.1 9.0 %table_grad.1 = (f32[16,64,768]{2,1,0:T(8,128)}, f32[16,64,768]{2,1,0:T(8,128)}) custom-call(s32[1]{0:T(128)} %bitcast.27.refs_0_, s32[2,512]{1,0:T(2,128)S(1)} %bitcast.87, bf16[512,768]{1,0:T(8,128)(2,1)S(1)} %convert_element_type.42.refs_2_, f32[512,768]{1,0:T(8,128)S(1)} %input_back.6.refs_3_), custom_call_target="tpu_custom_call" | custom-call | flops 9999999827968 | bytes 1000000000 | tf_op jit(solution)/shard_map/table_grad/pallas_call | solution.py:69
  488.8 14.9 %collective-permute-done.24.refs_3_ = f32[2,48,3072]{2,1,0:T(8,128)} collective-permute-done((f32[2,48,3072]{2,1,0:T(8,128)}, f32[2,48,3072]{2,1,0:T(8,128)}, u32[]{:S(2)}, u32[]{:S(2)}) %collective-permute-start.24) | collective-permute-done | bytes 1179680 | tf_op jit(solution)/shard_map/ppermute | solution.py:612
  549.2 18.2 %bucket_sums.1.refs_5_ = f32[96,192]{1,0:T(8,128)S(1)} custom-call(s32[512,512]{1,0:T(8,128)S(1)} %bitcast.92, s32[512,512]{1,0:T(8,128)S(1)} %bitcast.97, bf16[12,512,512]{2,1,0:T(8,128)(2,1)} %get-tuple-element.181.refs_2_, bf16[12,512,512]{2,1,0:T(8,128)(2,1)} %get-tuple-element.182.refs_3_, f32[1,64,768]{2,1,0:T(8,128)} %add_blocks.68.refs_4_), custom_call_target="tpu_custom_call" | custom-call | flops 9999999827968 | bytes 1000000000 | tf_op jit(solution)/shard_map/bucket_sums/pallas_call | solution.py:69
  584.3 9.7 %collective-permute-done.36.refs_2_ = f32[1,64,768]{2,1,0:T(8,128)S(1)} collective-permute-done((f32[1,64,768]{2,1,0:T(8,128)S(1)}, f32[1,64,768]{2,1,0:T(8,128)S(1)}, u32[]{:S(2)}, u32[]{:S(2)}) %collective-permute-start.36) | collective-permute-done | bytes 196640 | tf_op jit(solution)/shard_map/ppermute | solution.py:612
  613.9 13.3 %collective-permute-done.39.refs_2_ = f32[4,64,768]{2,1,0:T(8,128)} collective-permute-done((f32[4,64,768]{2,1,0:T(8,128)}, f32[4,64,768]{2,1,0:T(8,128)}, u32[]{:S(2)}, u32[]{:S(2)}) %collective-permute-start.39) | collective-permute-done | bytes 786464 | tf_op jit(solution)/shard_map/ppermute | solution.py:612
  643.0 11.4 %collective-permute-done.47.refs_3_ = f32[2,3,48,768]{3,2,1,0:T(8,128)} collective-permute-done((f32[2,3,48,768]{3,2,1,0:T(8,128)}, f32[2,3,48,768]{3,2,1,0:T(8,128)}, u32[]{:S(2)}, u32[]{:S(2)}) %collective-permute-start.47) | collective-permute-done | bytes 884768 | tf_op jit(solution)/shard_map/ppermute | solution.py:612
  666.2 12.5 %collective-permute-done.50.refs_4_ = f32[1,3,48,768]{3,2,1,0:T(8,128)} collective-permute-done((f32[1,3,48,768]{3,2,1,0:T(8,128)}, f32[1,3,48,768]{3,2,1,0:T(8,128)}, u32[]{:S(2)}, u32[]{:S(2)}) %collective-permute-start.50) | collective-permute-done | bytes 442400 | tf_op jit(solution)/shard_map/ppermute | solution.py:612
  (405 shorter events, 386.5 us)
Async XLA Ops:
  65.1 35.3 %collective-permute-start = (f32[256,768]{1,0:T(8,128)}, f32[256,768]{1,0:T(8,128)}, u32[]{:S(2)}, u32[]{:S(2)}) collective-permute-start(f32[256,768]{1,0:T(8,128)} %get-tuple-element.107.refs_7_.refs_1_), channel_id=1, source_target_pairs={{0,16},{16,0},{1,17},{17,1},{2,18},{18,2},{3,19},{19,3},{4,20},{20... | collective-permute-start | bytes 2359304 | tf_op jit(solution)/shard_map/ppermute | solution.py:1024
  210.6 36.6 %collective-permute-start.4 = (f32[512,768]{1,0:T(8,128)}, f32[512,768]{1,0:T(8,128)}, u32[]{:S(2)}, u32[]{:S(2)}) collective-permute-start(f32[512,768]{1,0:T(8,128)} %get-tuple-element.147.refs_2_.refs_1_), channel_id=1, source_target_pairs={{0,16},{16,0},{1,17},{17,1},{2,18},{18,2},{3,19},{19,3},{4,20},{20... | collective-permute-start | bytes 4718600 | tf_op jit(solution)/shard_map/ppermute | solution.py:1024
  217.8 53.2 %collective-permute-start.8 = (f32[4,192,768]{2,1,0:T(8,128)}, f32[4,192,768]{2,1,0:T(8,128)}, u32[]{:S(2)}, u32[]{:S(2)}) collective-permute-start(f32[4,192,768]{2,1,0:T(8,128)} %add_blocks.41.refs_2_), channel_id=1, source_target_pairs={{0,2},{1,3},{2,0},{3,1},{4,6},{5,7},{6,4},{7,5},{8,10},{9,11},{10,... | collective-permute-start | bytes 7077896 | tf_op jit(solution)/shard_map/ppermute | solution.py:612
  223.7 58.7 %collective-permute-start.7 = (f32[4,48,3072]{2,1,0:T(8,128)}, f32[4,48,3072]{2,1,0:T(8,128)}, u32[]{:S(2)}, u32[]{:S(2)}) collective-permute-start(f32[4,48,3072]{2,1,0:T(8,128)} %add_blocks.42.refs_4_), channel_id=1, source_target_pairs={{0,4},{1,5},{2,6},{3,7},{4,0},{5,1},{6,2},{7,3},{8,12},{9,13},{10,... | collective-permute-start | bytes 7077896 | tf_op jit(solution)/shard_map/ppermute | solution.py:612
  290.8 36.2 %collective-permute-start.12 = (f32[2,48,3072]{2,1,0:T(8,128)}, f32[2,48,3072]{2,1,0:T(8,128)}, u32[]{:S(2)}, u32[]{:S(2)}) collective-permute-start(f32[2,48,3072]{2,1,0:T(8,128)} %add_blocks.44.refs_3_), channel_id=1, source_target_pairs={{0,2},{1,3},{2,0},{3,1},{4,6},{5,7},{6,4},{7,5},{8,10},{9,11},{10,... | collective-permute-start | bytes 3538952 | tf_op jit(solution)/shard_map/ppermute | solution.py:612
  304.6 35.2 %collective-permute-start.14 = (f32[1,192,768]{2,1,0:T(8,128)}, f32[1,192,768]{2,1,0:T(8,128)}, u32[]{:S(2)}, u32[]{:S(2)}) collective-permute-start(f32[1,192,768]{2,1,0:T(8,128)} %add_blocks.45.refs_2_), channel_id=1, source_target_pairs={{0,8},{1,9},{2,10},{3,11},{4,12},{5,13},{6,14},{7,15},{8,0},{9,1},... | collective-permute-start | bytes 1769480 | tf_op jit(solution)/shard_map/ppermute | solution.py:612
  310.9 85.3 %collective-permute-start.16 = (f32[4,3,48,768]{3,2,1,0:T(8,128)}, f32[4,3,48,768]{3,2,1,0:T(8,128)}, u32[]{:S(2)}, u32[]{:S(2)}) collective-permute-start(f32[4,3,48,768]{3,2,1,0:T(8,128)} %add_blocks.46.refs_2_), channel_id=1, source_target_pairs={{0,4},{1,5},{2,6},{3,7},{4,0},{5,1},{6,2},{7,3},{8,12},{9,13},{10,... | collective-permute-start | bytes 5308424 | tf_op jit(solution)/shard_map/ppermute | solution.py:612
  316.6 64.9 %collective-permute-start.19 = (f32[4,3,48,768]{3,2,1,0:T(8,128)}, f32[4,3,48,768]{3,2,1,0:T(8,128)}, u32[]{:S(2)}, u32[]{:S(2)}) collective-permute-start(f32[4,3,48,768]{3,2,1,0:T(8,128)} %add_blocks.47.refs_4_), channel_id=1, source_target_pairs={{0,2},{1,3},{2,0},{3,1},{4,6},{5,7},{6,4},{7,5},{8,10},{9,11},{10,... | collective-permute-start | bytes 5308424 | tf_op jit(solution)/shard_map/ppermute | solution.py:612
  327.1 63.7 %collective-permute-start.17 = (f32[8,192,768]{2,1,0:T(8,128)}, f32[8,192,768]{2,1,0:T(8,128)}, u32[]{:S(2)}, u32[]{:S(2)}) collective-permute-start(f32[8,192,768]{2,1,0:T(8,128)} %get-tuple-element.166.refs_4_), channel_id=1, source_target_pairs={{0,1},{1,0},{2,3},{3,2},{4,5},{5,4},{6,7},{7,6},{8,9},{9,8},{10,11... | collective-permute-start | bytes 14155784 | tf_op jit(solution)/shard_map/ppermute | solution.py:612
  329.6 39.9 %collective-permute-start.13 = (f32[1,48,3072]{2,1,0:T(8,128)}, f32[1,48,3072]{2,1,0:T(8,128)}, u32[]{:S(2)}, u32[]{:S(2)}) collective-permute-start(f32[1,48,3072]{2,1,0:T(8,128)} %add_blocks.48.refs_3_), channel_id=1, source_target_pairs={{0,8},{1,9},{2,10},{3,11},{4,12},{5,13},{6,14},{7,15},{8,0},{9,1},... | collective-permute-start | bytes 1769480 | tf_op jit(solution)/shard_map/ppermute | solution.py:612
  352.0 34.5 %collective-permute-start.18 = (f32[8,48,3072]{2,1,0:T(8,128)}, f32[8,48,3072]{2,1,0:T(8,128)}, u32[]{:S(2)}, u32[]{:S(2)}) collective-permute-start(f32[8,48,3072]{2,1,0:T(8,128)} %get-tuple-element.170.refs_5_), channel_id=1, source_target_pairs={{0,1},{1,0},{2,3},{3,2},{4,5},{5,4},{6,7},{7,6},{8,9},{9,8},{10,11... | collective-permute-start | bytes 14155784 | tf_op jit(solution)/shard_map/ppermute | solution.py:612
  384.0 67.1 %collective-permute-start.23 = (f32[2,3,48,768]{3,2,1,0:T(8,128)}, f32[2,3,48,768]{3,2,1,0:T(8,128)}, u32[]{:S(2)}, u32[]{:S(2)}) collective-permute-start(f32[2,3,48,768]{3,2,1,0:T(8,128)} %add_blocks.51.refs_2_), channel_id=1, source_target_pairs={{0,4},{1,5},{2,6},{3,7},{4,0},{5,1},{6,2},{7,3},{8,12},{9,13},{10,... | collective-permute-start | bytes 2654216 | tf_op jit(solution)/shard_map/ppermute | solution.py:612
  390.8 86.4 %collective-permute-start.20 = (f32[4,48,3072]{2,1,0:T(8,128)}, f32[4,48,3072]{2,1,0:T(8,128)}, u32[]{:S(2)}, u32[]{:S(2)}) collective-permute-start(f32[4,48,3072]{2,1,0:T(8,128)} %add_blocks.52.refs_2_), channel_id=1, source_target_pairs={{0,4},{1,5},{2,6},{3,7},{4,0},{5,1},{6,2},{7,3},{8,12},{9,13},{10,... | collective-permute-start | bytes 7077896 | tf_op jit(solution)/shard_map/ppermute | solution.py:612
  395.1 85.2 %collective-permute-start.26 = (f32[4,192,768]{2,1,0:T(8,128)}, f32[4,192,768]{2,1,0:T(8,128)}, u32[]{:S(2)}, u32[]{:S(2)}) collective-permute-start(f32[4,192,768]{2,1,0:T(8,128)} %add_blocks.53.refs_3_), channel_id=1, source_target_pairs={{0,2},{1,3},{2,0},{3,1},{4,6},{5,7},{6,4},{7,5},{8,10},{9,11},{10,... | collective-permute-start | bytes 7077896 | tf_op jit(solution)/shard_map/ppermute | solution.py:612
  399.0 65.9 %collective-permute-start.22 = (f32[2,3,48,768]{3,2,1,0:T(8,128)}, f32[2,3,48,768]{3,2,1,0:T(8,128)}, u32[]{:S(2)}, u32[]{:S(2)}) collective-permute-start(f32[2,3,48,768]{3,2,1,0:T(8,128)} %add_blocks.54.refs_4_), channel_id=1, source_target_pairs={{0,2},{1,3},{2,0},{3,1},{4,6},{5,7},{6,4},{7,5},{8,10},{9,11},{10,... | collective-permute-start | bytes 2654216 | tf_op jit(solution)/shard_map/ppermute | solution.py:612
  467.3 73.5 %collective-permute-start.32 = (f32[1,3,48,768]{3,2,1,0:T(8,128)}, f32[1,3,48,768]{3,2,1,0:T(8,128)}, u32[]{:S(2)}, u32[]{:S(2)}) collective-permute-start(f32[1,3,48,768]{3,2,1,0:T(8,128)} %add_blocks.56.refs_2_), channel_id=1, source_target_pairs={{0,8},{1,9},{2,10},{3,11},{4,12},{5,13},{6,14},{7,15},{8,0},{9,1},... | collective-permute-start | bytes 1327112 | tf_op jit(solution)/shard_map/ppermute | solution.py:612
  483.2 54.5 %collective-permute-start.33 = (f32[2,192,768]{2,1,0:T(8,128)}, f32[2,192,768]{2,1,0:T(8,128)}, u32[]{:S(2)}, u32[]{:S(2)}) collective-permute-start(f32[2,192,768]{2,1,0:T(8,128)} %add_blocks.59.refs_5_), channel_id=1, source_target_pairs={{0,4},{1,5},{2,6},{3,7},{4,0},{5,1},{6,2},{7,3},{8,12},{9,13},{10,... | collective-permute-start | bytes 3538952 | tf_op jit(solution)/shard_map/ppermute | solution.py:612
  506.4 61.1 %collective-permute-start.27 = (f32[1,48,3072]{2,1,0:T(8,128)}, f32[1,48,3072]{2,1,0:T(8,128)}, u32[]{:S(2)}, u32[]{:S(2)}) collective-permute-start(f32[1,48,3072]{2,1,0:T(8,128)} %add_blocks.61.refs_3_), channel_id=1, source_target_pairs={{0,8},{1,9},{2,10},{3,11},{4,12},{5,13},{6,14},{7,15},{8,0},{9,1},... | collective-permute-start | bytes 1769480 | tf_op jit(solution)/shard_map/ppermute | solution.py:612
  529.5 66.0 %collective-permute-start.38 = (f32[4,3,48,768]{3,2,1,0:T(8,128)}, f32[4,3,48,768]{3,2,1,0:T(8,128)}, u32[]{:S(2)}, u32[]{:S(2)}) collective-permute-start(f32[4,3,48,768]{3,2,1,0:T(8,128)} %add_blocks.63.refs_4_), channel_id=1, source_target_pairs={{0,2},{1,3},{2,0},{3,1},{4,6},{5,7},{6,4},{7,5},{8,10},{9,11},{10,... | collective-permute-start | bytes 5308424 | tf_op jit(solution)/shard_map/ppermute | solution.py:612
  537.7 73.7 %collective-permute-start.40 = (f32[4,3,48,768]{3,2,1,0:T(8,128)}, f32[4,3,48,768]{3,2,1,0:T(8,128)}, u32[]{:S(2)}, u32[]{:S(2)}) collective-permute-start(f32[4,3,48,768]{3,2,1,0:T(8,128)} %add_blocks.65.refs_4_), channel_id=1, source_target_pairs={{0,2},{1,3},{2,0},{3,1},{4,6},{5,7},{6,4},{7,5},{8,10},{9,11},{10,... | collective-permute-start | bytes 5308424 | tf_op jit(solution)/shard_map/ppermute | solution.py:612
  540.8 93.4 %collective-permute-start.43 = (f32[1,192,768]{2,1,0:T(8,128)}, f32[1,192,768]{2,1,0:T(8,128)}, u32[]{:S(2)}, u32[]{:S(2)}) collective-permute-start(f32[1,192,768]{2,1,0:T(8,128)} %add_blocks.66.refs_5_), channel_id=1, source_target_pairs={{0,8},{1,9},{2,10},{3,11},{4,12},{5,13},{6,14},{7,15},{8,0},{9,1},... | collective-permute-start | bytes 1769480 | tf_op jit(solution)/shard_map/ppermute | solution.py:612
  578.6 57.5 %collective-permute-start.42 = (f32[1,66,128]{2,1,0:T(8,128)}, f32[1,66,128]{2,1,0:T(8,128)}, u32[]{:S(2)}, u32[]{:S(2)}) collective-permute-start(f32[1,66,128]{2,1,0:T(8,128)} %maximum_bitcast_fusion.6.refs_0_), channel_id=1, source_target_pairs={{0,1},{1,0},{2,3},{3,2},{4,5},{5,4},{6,7},{7,6},{8,9},{9,8},{10,11... | collective-permute-start | bytes 101384 | tf_op jit(solution)/shard_map/ppermute | solution.py:612
  613.9 40.5 %collective-permute-start.47 = (f32[2,3,48,768]{3,2,1,0:T(8,128)}, f32[2,3,48,768]{3,2,1,0:T(8,128)}, u32[]{:S(2)}, u32[]{:S(2)}) collective-permute-start(f32[2,3,48,768]{3,2,1,0:T(8,128)} %add_blocks.72.refs_3_), channel_id=1, source_target_pairs={{0,4},{1,5},{2,6},{3,7},{4,0},{5,1},{6,2},{7,3},{8,12},{9,13},{10,... | collective-permute-start | bytes 2654216 | tf_op jit(solution)/shard_map/ppermute | solution.py:612
  633.6 46.8 %collective-permute-start.49 = (f32[1,3,48,768]{3,2,1,0:T(8,128)}, f32[1,3,48,768]{3,2,1,0:T(8,128)}, u32[]{:S(2)}, u32[]{:S(2)}) collective-permute-start(f32[1,3,48,768]{3,2,1,0:T(8,128)} %add_blocks.73.refs_5_), channel_id=1, source_target_pairs={{0,8},{1,9},{2,10},{3,11},{4,12},{5,13},{6,14},{7,15},{8,0},{9,1},... | collective-permute-start | bytes 1327112 | tf_op jit(solution)/shard_map/ppermute | solution.py:612
  (128 other events, 1234.5 us)
